TPU v7x, 128 devices: a whole 4x4x4 slice. The times are simulated.
128 devices in a mesh: branch: 2 (over y_lo), rows: 64 (over x, y_hi, z, core).
Axes of the slice: x: 4, y: 4 (y_hi: 2, y_lo: 2; y = y_hi * 2 + y_lo), z: 4, core: 2. Of those that a mesh axis runs over, the one named last changes fastest.
Arguments:
- homolog_features: bfloat16 [128, 1024, 256], P(('branch', 'rows')), may hold values from -6 to 6
- pairwise_input: bfloat16 [1024, 1024, 128], P('rows', 'branch'), may hold values from -6 to 6
- transition_expand_matrix: bfloat16 [256, 1024], replicated, may hold values from -0.375 to 0.375
- transition_contract_matrix: bfloat16 [1024, 256], replicated, may hold values from -0.1875 to 0.1875
- factor_pair_matrices: bfloat16 [256, 64], replicated, may hold values from -0.375 to 0.375
- outer_output_weight: bfloat16 [1024, 128], replicated, may hold values from -0.75 to 0.75
- triangle_projection_weight: bfloat16 [128, 640], replicated, may hold values from -0.5 to 0.5
- triangle_output_weight: bfloat16 [128, 128], replicated, may hold values from -1 to 1
- pairwise_up_weight: bfloat16 [128, 512], replicated, may hold values from -0.5 to 0.5
- pairwise_down_weight: bfloat16 [512, 128], replicated, may hold values from -0.25 to 0.25
Outputs:
- refreshed_homolog_features: bfloat16 [128, 1024, 256], P(('branch', 'rows'))
- pairwise_output: bfloat16 [1024, 1024, 128], P('rows', 'branch')
All inputs are finite; a program needn't handle non-finite values.
Results may differ from a plain program's by a relative error of at most 0.0085.
Values may be sent and summed in bfloat16 or wider, within the bound.
A program may use at most 128 MiB of HBM per device.

v0:
```python
import jax
import jax.numpy as jnp
from jax import lax
from jax.experimental import pallas as pl
from jax.experimental.pallas import tpu as pltpu
from jax.sharding import PartitionSpec as P


def standardize_features(values, dimension):
    average = jnp.mean(values, axis=dimension, keepdims=True)
    centered = values - average
    variance = jnp.mean(centered * centered, axis=dimension, keepdims=True)
    return centered * lax.rsqrt(variance + 1e-05)


def alignment_branch(
    homolog_features, transition_expand_matrix, transition_contract_matrix, factor_pair_matrices
):
    local_rows, sequence_length, channel_width = homolog_features.shape
    homolog_real_matrix = homolog_features.astype(jnp.float32)
    standardized_homologs = (
        standardize_features(homolog_real_matrix, -1)
        .astype(jnp.bfloat16)
        .reshape(local_rows * sequence_length, channel_width)
    )
    expanded_activations = jax.nn.relu(
        jnp.dot(standardized_homologs, transition_expand_matrix, preferred_element_type=jnp.float32)
    ).astype(jnp.bfloat16)
    refreshed_homolog_features = (
        homolog_real_matrix
        + jnp.dot(
            expanded_activations, transition_contract_matrix, preferred_element_type=jnp.float32
        ).reshape(homolog_features.shape)
    ).astype(jnp.bfloat16)
    standardized_for_factors = (
        standardize_features(refreshed_homolog_features.astype(jnp.float32), -1)
        .astype(jnp.bfloat16)
        .reshape(local_rows * sequence_length, channel_width)
    )
    projected = jnp.dot(
        standardized_for_factors, factor_pair_matrices, preferred_element_type=jnp.float32
    ).reshape(local_rows, sequence_length, -1)
    channels = projected.shape[-1] // 2
    left_side = projected[..., :channels].astype(jnp.bfloat16)
    right_side = jnp.swapaxes(projected[..., channels:].astype(jnp.bfloat16), 1, 2)
    return (refreshed_homolog_features, left_side, right_side)


def gather_sides(left_side, right_side):
    left_pair = lax.all_gather(left_side, "branch", axis=0, tiled=True)
    left_gathered = lax.all_to_all(left_pair, "rows", split_axis=1, concat_axis=0, tiled=True)
    right_pair = lax.all_to_all(right_side, "branch", split_axis=2, concat_axis=0, tiled=True)
    right_gathered = lax.all_gather(jnp.swapaxes(right_pair, 0, 1), "rows", axis=1, tiled=True)
    return left_gathered, right_gathered


def send_whole(tri_left, tri_right):
    both = ("branch", "rows")
    return (
        lax.all_to_all(tri_left, both, split_axis=0, concat_axis=0, tiled=True),
        lax.all_to_all(tri_right, both, split_axis=0, concat_axis=0, tiled=True),
    )


def send_back(product):
    return lax.all_to_all(product, ("branch", "rows"), split_axis=0, concat_axis=0, tiled=True)


def pair_front(pairwise_input, triangle_projection_weight):
    tile_rows, columns, chans = pairwise_input.shape
    pair_float = pairwise_input.astype(jnp.float32)
    pair_norm = standardize_features(pair_float, -1).astype(jnp.bfloat16)
    norm_flat = pair_norm.reshape(tile_rows * columns, chans)
    proj_flat = lax.dot_general(
        triangle_projection_weight,
        norm_flat,
        (((0,), (1,)), ((), ())),
        preferred_element_type=jnp.float32,
    )
    proj_tile = proj_flat[: 4 * chans].reshape(4 * chans, tile_rows, columns)
    gate_vals = jax.nn.sigmoid(proj_flat[4 * chans :])
    tri_left = (jax.nn.sigmoid(proj_tile[chans : 2 * chans]) * proj_tile[:chans]).astype(
        jnp.bfloat16
    )
    tri_right = (jax.nn.sigmoid(proj_tile[3 * chans :]) * proj_tile[2 * chans : 3 * chans]).astype(
        jnp.bfloat16
    )
    return pair_float, gate_vals, tri_left, tri_right


def triangle_product(left_chan, right_chan):
    halves = lax.axis_size("branch")
    columns = left_chan.shape[-1]
    tile_rows = left_chan.shape[1]
    left_src = left_chan.reshape(halves, -1, columns)
    right_src = right_chan.reshape(halves, halves, -1, columns)
    product = jnp.einsum(
        "bik,bhjk->hij", left_src, right_src, preferred_element_type=jnp.float32
    ).astype(jnp.bfloat16)
    return product.reshape(-1, tile_rows, columns)


def pair_back(
    pair_float,
    gate_vals,
    product_tile,
    triangle_output_weight,
    pairwise_up_weight,
    pairwise_down_weight,
):
    tile_rows, columns, chans = pair_float.shape
    prod_norm = (
        standardize_features(product_tile.astype(jnp.float32), 0)
        .astype(jnp.bfloat16)
        .reshape(chans, tile_rows * columns)
    )
    tri_update = lax.dot_general(
        triangle_output_weight,
        prod_norm,
        (((0,), (0,)), ((), ())),
        preferred_element_type=jnp.float32,
    )
    gated_update = jnp.transpose(gate_vals * tri_update).reshape(tile_rows, columns, chans)
    pair_mid = pair_float + gated_update
    mid_norm = standardize_features(pair_mid, -1).astype(jnp.bfloat16)
    pair_hidden = jax.nn.relu(
        jnp.einsum("ijd,dh->ijh", mid_norm, pairwise_up_weight, preferred_element_type=jnp.float32)
    ).astype(jnp.bfloat16)
    return pair_mid + jnp.einsum(
        "ijh,hd->ijd", pair_hidden, pairwise_down_weight, preferred_element_type=jnp.float32
    )


def outer_kernel(lt_ref, r_ref, wt_ref, out_ref, x_ref):
    n_factor = r_ref.shape[0]
    tile_rows = out_ref.shape[0]
    scale = 1.0 / r_ref.shape[1]

    def fill(d, carry):
        vals = jnp.dot(lt_ref[...], r_ref[d], preferred_element_type=jnp.float32)
        vals = (vals * scale).astype(jnp.bfloat16)
        start = pl.multiple_of(d * n_factor, n_factor)
        for i in range(tile_rows):
            x_ref[i, pl.ds(start, n_factor), :] = vals[i * n_factor : (i + 1) * n_factor, :]
        return carry

    lax.fori_loop(0, n_factor, fill, 0)

    def emit(i, carry):
        upd = jnp.dot(wt_ref[...], x_ref[i], preferred_element_type=jnp.float32)
        out_ref[i] = upd.T
        return carry

    lax.fori_loop(0, tile_rows, emit, 0)


def outer_product(left_gathered, right_gathered, outer_output_weight):
    total_rows, tile_rows, channels = left_gathered.shape
    columns = right_gathered.shape[2]
    pair = outer_output_weight.shape[1]
    left_t = jnp.transpose(left_gathered, (1, 2, 0)).reshape(tile_rows * channels, total_rows)
    weight_t = jnp.transpose(
        outer_output_weight.reshape(channels, channels, pair), (1, 0, 2)
    ).reshape(channels * channels, pair).T
    flops = 4 * tile_rows * channels * channels * columns * (total_rows + pair) // 2
    return pl.pallas_call(
        outer_kernel,
        out_shape=jax.ShapeDtypeStruct((tile_rows, columns, pair), jnp.float32),
        in_specs=[pl.BlockSpec(memory_space=pltpu.VMEM)] * 3,
        out_specs=pl.BlockSpec(memory_space=pltpu.VMEM),
        scratch_shapes=[pltpu.VMEM((tile_rows, channels * channels, columns), jnp.bfloat16)],
        compiler_params=pltpu.CompilerParams(vmem_limit_bytes=56 * 1024 * 1024),
        cost_estimate=pl.CostEstimate(
            flops=flops, transcendentals=0, bytes_accessed=right_gathered.size * 2 + tile_rows * columns * pair * 4
        ),
    )(left_t, right_gathered, weight_t)


def on_device(
    homolog_features,
    pairwise_input,
    transition_expand_matrix,
    transition_contract_matrix,
    factor_pair_matrices,
    outer_output_weight,
    triangle_projection_weight,
    triangle_output_weight,
    pairwise_up_weight,
    pairwise_down_weight,
):
    refreshed_homolog_features, left_side, right_side = alignment_branch(
        homolog_features, transition_expand_matrix, transition_contract_matrix, factor_pair_matrices
    )
    left_gathered, right_gathered = gather_sides(left_side, right_side)
    pairwise_input, right_side = lax.optimization_barrier((pairwise_input, right_side))
    pair_float, gate_vals, tri_left, tri_right = pair_front(
        pairwise_input, triangle_projection_weight
    )
    left_chan, right_chan = send_whole(tri_left, tri_right)
    left_gathered, right_gathered, tri_right = lax.optimization_barrier(
        (left_gathered, right_gathered, tri_right)
    )
    outer_update = outer_product(left_gathered, right_gathered, outer_output_weight)
    left_chan, right_chan, outer_update = lax.optimization_barrier(
        (left_chan, right_chan, outer_update)
    )
    product_tile = send_back(triangle_product(left_chan, right_chan))
    pair_mid = pair_back(
        pair_float,
        gate_vals,
        product_tile,
        triangle_output_weight,
        pairwise_up_weight,
        pairwise_down_weight,
    )
    pairwise_output = (pair_mid + outer_update).astype(jnp.bfloat16)
    return (refreshed_homolog_features, pairwise_output)


def solution(mesh):
    return jax.shard_map(
        on_device,
        mesh=mesh,
        in_specs=(
            P(("branch", "rows"), None, None),
            P("rows", "branch", None),
            P(),
            P(),
            P(),
            P(),
            P(),
            P(),
            P(),
            P(),
        ),
        out_specs=(P(("branch", "rows"), None, None), P("rows", "branch", None)),
        check_vma=False,
    )
```

profile of v0, /device:TPU:1, one launch (start us, length us, event | category | flops | bytes accessed | tf_op | source)
XLA Modules:
  0.0 259.0 jit_solution(11947248166641858322)
XLA Ops:
  7.2 0.0 copy-start
  7.2 1.3 copy.51
  8.5 0.0 copy-start.10
  8.5 0.1 convert_reduce_fusion.2
  8.6 0.2 fusion.35
  8.8 0.0 copy-start.3
  8.8 3.3 %convert_reduce_fusion.3 = (f32[1024]{0:T(1024)S(1)}, bf16[1,1024,256]{1,2,0:T(8,128)(2,1)}) fusion(bf16[1024,256]{1,0:T(8,128)(2,1)S(1)} %copy-done, bf16[256,1024]{1,0:T(8,128)(2,1)} %param.12, bf16[1,1024,256]{1,2,0:T(8,128)(2,1)S(1)} %copy.51, f32[1024]{0:T(1024)S(1)} %add_rsqrt_fusion.4, f32[1024]{0:T(1024)S(1)} %broadcast_multiply_fusion.4), kind=kOutput, calls=%fused_computation.49 | convolution fusion | flops 1078197248 | bytes 2109440 | tf_op jit(solution)/shard_map/dot_general | solution.py:31
  12.1 1.2 fusion.37
  13.3 1.3 fusion.34
  14.6 0.4 copy.57
  15.0 0.5 broadcast.135
  15.5 2.3 reduce.4
  17.8 0.9 reshape.164
  18.7 3.4 %all-to-all-start.3 = ((bf16[2,2,8192]{2,1,0:T(2,128)(2,1)}), bf16[2,2,8192]{2,1,0:T(2,128)(2,1)S(1)}, u32[]{:S(2)}, u32[]{:S(2)}) async-start(bf16[2,2,8192]{2,1,0:T(2,128)(2,1)} %reshape.164), calls=%async_computation.3 | async-start | bytes 131072 | tf_op jit(solution)/shard_map/all_to_all | solution.py:52
  22.1 0.6 convert_reduce_fusion
  22.8 4.8 %all_gather.6 = bf16[2,1024,32]{1,2,0:T(8,128)(2,1)S(1)} all-gather(bf16[1,1024,32]{1,2,0:T(8,128)(2,1)S(1)} %get-tuple-element.26), channel_id=1, replica_groups=mesh['branch'=2,'rows'=64] {'branch'}, dimensions={0}, use_global_device_ids=true | all-gather | bytes 196608 | tf_op jit(solution)/shard_map/all_gather | solution.py:50
  27.5 0.4 copy.54
  27.9 1.1 reshape.162
  29.0 0.0 all-to-all-done.3
  29.0 12.7 %all-to-all-start.2 = ((bf16[64,2,512]{2,1,0:T(2,128)(2,1)}), bf16[64,2,512]{2,1,0:T(2,128)(2,1)S(1)}, u32[]{:S(2)}, u32[]{:S(2)}) async-start(bf16[64,2,512]{2,1,0:T(2,128)(2,1)} %reshape.162), calls=%async_computation.2 | async-start | bytes 262144 | tf_op jit(solution)/shard_map/all_to_all | solution.py:51
  41.7 0.2 all-gather.2.cloned.1.call-start
  41.9 0.4 reshape.165
  42.3 0.3 copy.58
  42.6 0.6 copy.59
  43.2 0.0 all-gather.2.cloned.1.call-update
  43.3 2.4 fusion.5
  45.7 2.5 fusion.6
  48.2 2.9 %convolution_bitcast_fusion = f32[640,8192]{0,1:T(8,128)S(1)} fusion(bf16[8192,128]{1,0:T(8,128)(2,1)S(1)} %bitcast.89, bf16[128,640]{1,0:T(8,128)(2,1)S(1)} %copy-done.7), kind=kOutput, calls=%fused_computation.1 | convolution fusion | flops 1342177280 | bytes 23232512 | tf_op jit(solution)/shard_map/dot_general | solution.py:74
  51.0 0.0 copy-start.2
  51.0 4.5 %fusion.9 = (bf16[128,8192]{0,1:T(8,128)(2,1)}, bf16[128,8192]{0,1:T(8,128)(2,1)}) fusion(f32[640,8192]{0,1:T(8,128)S(1)} %convolution_bitcast_fusion), kind=kLoop, calls=%fused_computation.18 | loop fusion | flops 10485760 | bytes 20971520 | tf_op jit(solution)/shard_map/convert_element_type | solution.py:85
  55.6 3.7 %copy-done.2 = f32[640,8192]{0,1:T(8,128)} copy-done((f32[640,8192]{0,1:T(8,128)}, f32[640,8192]{0,1:T(8,128)S(1)}, u32[]{:S(2)}) %copy-start.2) | copy-done | bytes 20971544
  59.3 4.6 %copy.52 = bf16[128,16,512]{2,1,0:T(8,128)(2,1)} copy(bf16[128,16,512]{0,2,1:T(8,128)(2,1)} %bitcast.86) | data formatting | bytes 4194304 | tf_op jit(solution)/shard_map/convert_element_type | solution.py:82
  63.9 0.0 all-to-all-done.2
  63.9 10.4 %all-to-all-start = ((bf16[128,16,512]{2,1,0:T(8,128)(2,1)}), bf16[128,16,512]{2,1,0:T(8,128)(2,1)}, u32[]{:S(2)}, u32[]{:S(2)}) async-start(bf16[128,16,512]{2,1,0:T(8,128)(2,1)} %copy.52), calls=%async_computation | async-start | bytes 4194304 | tf_op jit(solution)/shard_map/all_to_all | solution.py:60
  74.3 0.0 copy-start.6
  74.3 4.6 %copy.53 = bf16[128,16,512]{2,1,0:T(8,128)(2,1)} copy(bf16[128,16,512]{0,2,1:T(8,128)(2,1)} %bitcast.85) | data formatting | bytes 4194304 | tf_op jit(solution)/shard_map/convert_element_type | solution.py:85
  78.9 27.7 %all-to-all-done = bf16[128,16,512]{2,1,0:T(8,128)(2,1)} async-done(((bf16[128,16,512]{2,1,0:T(8,128)(2,1)}), bf16[128,16,512]{2,1,0:T(8,128)(2,1)}, u32[]{:S(2)}, u32[]{:S(2)}) %all-to-all-start) | async-done | bytes 2097184 | tf_op jit(solution)/shard_map/all_to_all | solution.py:60
  106.6 5.5 %all-to-all-start.1 = ((bf16[128,16,512]{2,1,0:T(8,128)(2,1)}), bf16[128,16,512]{2,1,0:T(8,128)(2,1)}, u32[]{:S(2)}, u32[]{:S(2)}) async-start(bf16[128,16,512]{2,1,0:T(8,128)(2,1)} %copy.53), calls=%async_computation.1 | async-start | bytes 4194304 | tf_op jit(solution)/shard_map/all_to_all | solution.py:61
  112.2 0.1 copy.61
  112.3 0.8 copy.62
  113.1 0.3 reshape.163
  113.4 0.1 copy.55
  113.5 42.1 %all-gather.2.cloned.1.call-done = bf16[32,128,512]{2,0,1:T(8,128)(2,1)} async-done(((bf16[32,2,512]{2,0,1:T(8,128)(2,1)}), bf16[32,128,512]{2,0,1:T(8,128)(2,1)}) %all-gather.2.cloned.1.call-update) | async-done | bytes 4194320 | tf_op jit(solution)/shard_map/all_gather | solution.py:53
  155.7 1.1 copy.60
  156.7 6.5 %copy.63.r_ref = bf16[32,128,512]{2,1,0:T(8,128)(2,1)} copy(bf16[32,128,512]{2,0,1:T(8,128)(2,1)} %all-gather.2.cloned.1.call-done) | data formatting | bytes 8388608 | tf_op jit(solution)/shard_map/optimization_barrier | solution.py:200
  163.2 19.9 %shard_map.113 = f32[16,512,128]{2,1,0:T(8,128)} custom-call(bf16[512,128]{1,0:T(8,128)(2,1)} %bitcast.101, bf16[32,128,512]{2,1,0:T(8,128)(2,1)} %copy.63.r_ref, bf16[128,1024]{1,0:T(8,128)(2,1)} %bitcast.99), custom_call_target="tpu_custom_call" | custom-call | flops 4294967296 | bytes 8388608 | tf_op jit(solution)/shard_map/pallas_call | solution.py:166
  183.2 0.0 all-to-all-done.1
  183.2 5.9 %fusion.25 = bf16[2,1024,512]{1,2,0:T(8,128)(2,1)} fusion(bf16[2,2,512,512]{3,2,1,0:T(8,128)(2,1)} %bitcast.21, bf16[2,1024,512,1]{2,1,3,0:T(8,128)(2,1)} %bitcast.24), kind=kOutput, calls=%fused_computation.41 | convolution fusion | flops 2148532224 | bytes 6291456 | tf_op jit(solution)/shard_map/bik,bhjk->hij/dot_general | solution.py:97
  189.1 4.0 %copy.64 = bf16[2,1024,512]{2,1,0:T(8,128)(2,1)} copy(bf16[2,1024,512]{1,2,0:T(8,128)(2,1)} %fusion.25) | data formatting | bytes 4194304 | tf_op jit(solution)/shard_map/convert_element_type | solution.py:99
  193.1 5.3 %all-to-all-start.4 = ((bf16[128,16,512]{2,1,0:T(8,128)(2,1)}), bf16[128,16,512]{2,1,0:T(8,128)(2,1)}, u32[]{:S(2)}, u32[]{:S(2)}) async-start(bf16[128,16,512]{2,1,0:T(8,128)(2,1)} %bitcast.87), calls=%async_computation.4 | async-start | bytes 4194304 | tf_op jit(solution)/shard_map/all_to_all | solution.py:66
  198.4 1.0 copy.65
  199.4 28.8 %all-to-all-done.4 = bf16[128,16,512]{2,1,0:T(8,128)(2,1)} async-done(((bf16[128,16,512]{2,1,0:T(8,128)(2,1)}), bf16[128,16,512]{2,1,0:T(8,128)(2,1)}, u32[]{:S(2)}, u32[]{:S(2)}) %all-to-all-start.4) | async-done | bytes 2097184 | tf_op jit(solution)/shard_map/all_to_all | solution.py:66
  228.2 2.0 convert_reduce_fusion.1
  230.1 2.2 fusion.7
  232.3 0.0 copy-start.11
  232.4 2.2 fusion.8
  234.5 1.4 copy.67
  235.9 3.5 %fusion = f32[128,8192]{0,1:T(8,128)S(1)} fusion(bf16[128,8192]{1,0:T(8,128)(2,1)S(1)} %bitcast.94, bf16[128,128]{1,0:T(8,128)(2,1)S(1)} %copy-done.11, f32[640,8192]{0,1:T(8,128)} %copy-done.2), kind=kOutput, calls=%fused_computation.3 | convolution fusion | flops 272629760 | bytes 10518528 | tf_op jit(solution)/shard_map/dot_general | solution.py:117
  239.4 1.2 fusion.27
  240.7 0.0 copy-start.8
  240.7 0.0 copy-start.9
  240.7 2.4 multiply_reduce_fusion
  243.2 0.0 copy-start.1
  243.2 8.9 %add_convert_fusion = bf16[16,512,128]{2,1,0:T(8,128)(2,1)} fusion(f32[16,512,128]{2,1,0:T(8,128)} %shard_map.113, f32[16,512]{1,0:T(8,128)S(1)} %add_rsqrt_fusion, f32[16,512]{1,0:T(8,128)S(1)} %broadcast_multiply_fusion, f32[16,512,128]{2,1,0:T(8,128)} %bitcast.84, bf16[16,512,128]{2,1,0:T(8,128)(2,1)S(1)} %copy-done.3, ...), kind=kOutput, calls=%fused_computation.34 | convolution fusion | flops 2166358016 | bytes 12910592 | tf_op jit(solution)/shard_map/ijh,hd->ijd/dot_general | solution.py:129
  (27 shorter events, 0.2 us)
Async XLA Ops:
  7.2 1.6 copy-start
  8.5 4.8 %copy-start.10 = (bf16[256,64]{0,1:T(8,128)(2,1)S(1)}, bf16[256,64]{0,1:T(8,128)(2,1)}, u32[]{:S(2)}) copy-start(bf16[256,64]{0,1:T(8,128)(2,1)} %param.14) | copy-start | bytes 98308
  8.8 13.3 %copy-start.3 = (bf16[16,512,128]{2,1,0:T(8,128)(2,1)S(1)}, bf16[16,512,128]{2,1,0:T(8,128)(2,1)}, u32[]{:S(2)}) copy-start(bf16[16,512,128]{2,1,0:T(8,128)(2,1)} %param.11) | copy-start | bytes 6291460
  18.7 10.2 %all-to-all-start.3 = ((bf16[2,2,8192]{2,1,0:T(2,128)(2,1)}), bf16[2,2,8192]{2,1,0:T(2,128)(2,1)S(1)}, u32[]{:S(2)}, u32[]{:S(2)}) async-start(bf16[2,2,8192]{2,1,0:T(2,128)(2,1)} %reshape.164), calls=%async_computation.3 | async-start | bytes 131072 | tf_op jit(solution)/shard_map/all_to_all | solution.py:52
  29.0 19.2 %copy-start.7 = (bf16[128,640]{1,0:T(8,128)(2,1)S(1)}, bf16[128,640]{1,0:T(8,128)(2,1)}, u32[]{:S(2)}) copy-start(bf16[128,640]{1,0:T(8,128)(2,1)} %param.16) | copy-start | bytes 491524
  29.0 34.9 %all-to-all-start.2 = ((bf16[64,2,512]{2,1,0:T(2,128)(2,1)}), bf16[64,2,512]{2,1,0:T(2,128)(2,1)S(1)}, u32[]{:S(2)}, u32[]{:S(2)}) async-start(bf16[64,2,512]{2,1,0:T(2,128)(2,1)} %reshape.162), calls=%async_computation.2 | async-start | bytes 262144 | tf_op jit(solution)/shard_map/all_to_all | solution.py:51
  41.7 114.0 %all-gather.2.cloned.1.call-start = ((), (), s32[]{:S(2)}) async-start(), calls=%async_computation.5 | async-start | bytes 4259840 | tf_op jit(solution)/shard_map/all_gather | solution.py:53
  51.0 8.3 %copy-start.2 = (f32[640,8192]{0,1:T(8,128)}, f32[640,8192]{0,1:T(8,128)S(1)}, u32[]{:S(2)}) copy-start(f32[640,8192]{0,1:T(8,128)S(1)} %convolution_bitcast_fusion) | copy-start | bytes 62914564
  63.9 42.8 %all-to-all-start = ((bf16[128,16,512]{2,1,0:T(8,128)(2,1)}), bf16[128,16,512]{2,1,0:T(8,128)(2,1)}, u32[]{:S(2)}, u32[]{:S(2)}) async-start(bf16[128,16,512]{2,1,0:T(8,128)(2,1)} %copy.52), calls=%async_computation | async-start | bytes 4194304 | tf_op jit(solution)/shard_map/all_to_all | solution.py:60
  74.3 37.9 %copy-start.6 = (bf16[1024,128]{1,0:T(8,128)(2,1)S(1)}, bf16[1024,128]{1,0:T(8,128)(2,1)}, u32[]{:S(2)}) copy-start(bf16[1024,128]{1,0:T(8,128)(2,1)} %param.15) | copy-start | bytes 786436
  106.6 76.5 %all-to-all-start.1 = ((bf16[128,16,512]{2,1,0:T(8,128)(2,1)}), bf16[128,16,512]{2,1,0:T(8,128)(2,1)}, u32[]{:S(2)}, u32[]{:S(2)}) async-start(bf16[128,16,512]{2,1,0:T(8,128)(2,1)} %copy.53), calls=%async_computation.1 | async-start | bytes 4194304 | tf_op jit(solution)/shard_map/all_to_all | solution.py:61
  189.1 9.3 %copy-start.5 = (bf16[1,1024,256]{1,2,0:T(8,128)(2,1)S(1)}, bf16[1,1024,256]{1,2,0:T(8,128)(2,1)}, u32[]{:S(2)}) copy-start(bf16[1,1024,256]{1,2,0:T(8,128)(2,1)} %get-tuple-element.29) | copy-start | bytes 1572868
  193.1 35.1 %all-to-all-start.4 = ((bf16[128,16,512]{2,1,0:T(8,128)(2,1)}), bf16[128,16,512]{2,1,0:T(8,128)(2,1)}, u32[]{:S(2)}, u32[]{:S(2)}) async-start(bf16[128,16,512]{2,1,0:T(8,128)(2,1)} %bitcast.87), calls=%async_computation.4 | async-start | bytes 4194304 | tf_op jit(solution)/shard_map/all_to_all | solution.py:66
  232.3 3.6 %copy-start.11 = (bf16[128,128]{1,0:T(8,128)(2,1)S(1)}, bf16[128,128]{1,0:T(8,128)(2,1)}, u32[]{:S(2)}) copy-start(bf16[128,128]{1,0:T(8,128)(2,1)} %param.17) | copy-start | bytes 98308
  239.4 3.7 %copy-start.4 = (f32[128,8192]{0,1:T(8,128)}, f32[128,8192]{0,1:T(8,128)S(1)}, u32[]{:S(2)}) copy-start(f32[128,8192]{0,1:T(8,128)S(1)} %fusion) | copy-start | bytes 12582916
  240.7 2.5 copy-start.8
  240.7 2.5 copy-start.9
  243.2 8.9 %copy-start.1 = (bf16[1024,256]{1,0:T(8,128)(2,1)S(1)}, bf16[1024,256]{1,0:T(8,128)(2,1)}, u32[]{:S(2)}) copy-start(bf16[1024,256]{1,0:T(8,128)(2,1)} %param.13) | copy-start | bytes 1572868
Sparse Core Ops, SparseCore 0:
  45.7 109.9 all-gather.1
where the time goes:
time: 260 us; the launch traced here: 259 us
  waiting for transfers between devices  98.7 us (38%)
  starting transfers between devices  37.5 us (14%)
  local copies, waits for them, and re-layouts  34.1 us (13%)
  matrix products  25.8 us (10%)
  other arithmetic  23.8 us (9%)
  Pallas kernels  19.9 us (8%)
  between operations  14.4 us (6%)
  blocking collectives  4.78 us (2%)
    all_gather x1, waiting for transfers between devices, gather_sides(): lax.all_gather(jnp.swapaxes(right_pair, 0, 1), 'rows', axis=1, tiled=True)  42.1 us
    all_to_all x1, waiting for transfers between devices, send_back(): lax.all_to_all(product, ('branch', 'rows'), split_axis=0, concat_axis=0,...  28.8 us
    all_to_all x1, waiting for transfers between devices, send_whole(): lax.all_to_all(tri_left, both, split_axis=0, concat_axis=0, tiled=True)  27.7 us
    pallas_call x1, Pallas kernels, outer_product(): pl.pallas_call(outer_kernel, out_shape=jax.ShapeDtypeStruct((tile_rows, c...  19.9 us
    all_to_all x1, starting transfers between devices, gather_sides(): lax.all_to_all(left_pair, 'rows', split_axis=1, concat_axis=0, tiled=True)  12.7 us
    unnamed x32, local copies, waits for them, and re-layouts  10.6 us
    all_to_all x1, starting transfers between devices, send_whole(): lax.all_to_all(tri_left, both, split_axis=0, concat_axis=0, tiled=True)  10.4 us
    dot_general x1, matrix products, pair_back(): jnp.einsum('ijh,hd->ijd', pair_hidden, pairwise_down_weight, preferred_el...  8.9 us
  transfers between devices with their start and end apart: 6, of which 3 were waited for; matrix products, arithmetic and copies ran while one was open for 13% of the time, Pallas kernels for 8%

commit v1 on v0

--- a/solution.py
+++ b/solution.py
@@ -46,20 +46,30 @@
     return (refreshed_homolog_features, left_side, right_side)
 
 
+def branch_pair(mine, theirs):
+    first = lax.axis_index("branch") == 0
+    return jnp.where(first, jnp.concatenate([mine, theirs]), jnp.concatenate([theirs, mine]))
+
+
 def gather_sides(left_side, right_side):
-    left_pair = lax.all_gather(left_side, "branch", axis=0, tiled=True)
+    swap = [(0, 1), (1, 0)]
+    left_pair = branch_pair(left_side, lax.ppermute(left_side, "branch", swap))
     left_gathered = lax.all_to_all(left_pair, "rows", split_axis=1, concat_axis=0, tiled=True)
-    right_pair = lax.all_to_all(right_side, "branch", split_axis=2, concat_axis=0, tiled=True)
+    half = right_side.shape[2] // 2
+    me = lax.axis_index("branch")
+    keep = lax.dynamic_slice_in_dim(right_side, me * half, half, axis=2)
+    send = lax.dynamic_slice_in_dim(right_side, (1 - me) * half, half, axis=2)
+    right_pair = branch_pair(keep, lax.ppermute(send, "branch", swap))
     right_gathered = lax.all_gather(jnp.swapaxes(right_pair, 0, 1), "rows", axis=1, tiled=True)
     return left_gathered, right_gathered
 
 
 def send_whole(tri_left, tri_right):
     both = ("branch", "rows")
-    return (
-        lax.all_to_all(tri_left, both, split_axis=0, concat_axis=0, tiled=True),
-        lax.all_to_all(tri_right, both, split_axis=0, concat_axis=0, tiled=True),
-    )
+    moved = lax.all_to_all(
+        jnp.stack([tri_left, tri_right], axis=1), both, split_axis=0, concat_axis=0, tiled=True
+    )
+    return moved[:, 0], moved[:, 1]
 
 
 def send_back(product):
@@ -197,14 +207,13 @@
         pairwise_input, triangle_projection_weight
     )
     left_chan, right_chan = send_whole(tri_left, tri_right)
-    left_gathered, right_gathered, tri_right = lax.optimization_barrier(
-        (left_gathered, right_gathered, tri_right)
-    )
+    product = triangle_product(left_chan, right_chan)
+    product, left_gathered, right_gathered = lax.optimization_barrier(
+        (product, left_gathered, right_gathered)
+    )
+    product_tile = send_back(product)
     outer_update = outer_product(left_gathered, right_gathered, outer_output_weight)
-    left_chan, right_chan, outer_update = lax.optimization_barrier(
-        (left_chan, right_chan, outer_update)
-    )
-    product_tile = send_back(triangle_product(left_chan, right_chan))
+    product_tile, outer_update = lax.optimization_barrier((product_tile, outer_update))
     pair_mid = pair_back(
         pair_float,
         gate_vals,

time: 260 us -> 214 us (0.82)
  waiting for transfers between devices: 98.7 us -> 65.5 us
  starting transfers between devices: 37.5 us -> 27.3 us
  blocking collectives: 4.78 us -> 0 us
  other arithmetic: 23.8 us -> 27.6 us
    all_gather x1, waiting for transfers between devices: 42.1 us -> 0.01 us  [gather_sides(): lax.all_gather(jnp.swapaxes(right_pair, 0, 1), 'rows', axis=1, tiled=True)]
    all_to_all x3 -> x1, waiting for transfers between devices: 27.8 us -> 59 us  [send_whole(): lax.all_to_all(jnp.stack([tri_left, tri_right], axis=1), both, split_axis...]
    all_to_all x1, waiting for transfers between devices: 28.8 us -> 0.33 us  [send_back(): lax.all_to_all(product, ('branch', 'rows'), split_axis=0, concat_axis=0,...]
    all_to_all x3 -> x1, starting transfers between devices: 19.3 us -> 5.12 us  [send_whole(): lax.all_to_all(jnp.stack([tri_left, tri_right], axis=1), both, split_axis...]
    all_to_all x1, waiting for transfers between devices: 0.01 us -> 6.12 us  [gather_sides(): lax.all_to_all(left_pair, 'rows', split_axis=1, concat_axis=0, tiled=True)]
    all_gather x1 -> x0, blocking collectives: 4.78 us -> none  [gather_sides(): left_pair = lax.all_gather(left_side, 'branch', axis=0, tiled=True)]
    another operation x0 -> x1, other arithmetic: none -> 4.59 us  [send_whole(): jnp.stack([tri_left, tri_right], axis=1)]
    slice x1 -> x2, local copies, waits for them, and re-layouts: 0.01 us -> 2.7 us  [the longest x1 2.69 us: send_whole(): return (moved[:, 0], moved[:, 1])]
  transfers between devices with their start and end apart: 6 -> 6, of which waited for: 3 -> 3; matrix products, arithmetic and copies ran while one was open for 13% -> 24% of each run, Pallas kernels for 8% -> 9%
where the time goes in v1:
time: 214 us
  waiting for transfers between devices  65.5 us (31%)
  local copies, waits for them, and re-layouts  33.8 us (16%)
  other arithmetic  27.6 us (13%)
  starting transfers between devices  27.3 us (13%)
  matrix products  25.1 us (12%)
  Pallas kernels  19.9 us (9%)
  between operations  14.3 us (7%)
    all_to_all x1, waiting for transfers between devices, send_whole(): lax.all_to_all(jnp.stack([tri_left, tri_right], axis=1), both, split_axis...  59 us
    pallas_call x1, Pallas kernels, outer_product(): pl.pallas_call(outer_kernel, out_shape=jax.ShapeDtypeStruct((tile_rows, c...  19.9 us
    all_to_all x1, starting transfers between devices, gather_sides(): lax.all_to_all(left_pair, 'rows', split_axis=1, concat_axis=0, tiled=True)  12.3 us
    unnamed x29, local copies, waits for them, and re-layouts  8.91 us
    dot_general x1, matrix products, pair_back(): jnp.einsum('ijh,hd->ijd', pair_hidden, pairwise_down_weight, preferred_el...  8.91 us
    reduce_sum x5, other arithmetic, standardize_features(): variance = jnp.mean(centered * centered, axis=dimension, keepdims=True)  8.36 us
    all_to_all x1, starting transfers between devices, send_back(): lax.all_to_all(product, ('branch', 'rows'), split_axis=0, concat_axis=0,...  7.46 us
    optimization_barrier x1, local copies, waits for them, and re-layouts, on_device(): lax.optimization_barrier((product, left_gathered, right_gathered))  6.5 us
  transfers between devices with their start and end apart: 6, of which 3 were waited for; matrix products, arithmetic and copies ran while one was open for 24% of the time, Pallas kernels for 9%

profile of v1, /device:TPU:1, one launch (start us, length us, event | category | flops | bytes accessed | tf_op | source)
XLA Modules:
  0.0 213.6 jit_solution(17995558620573634007)
XLA Ops:
  7.2 0.0 copy-start
  7.2 0.0 all-gather.2.cloned.1.call-start
  7.2 1.3 copy.38
  8.5 0.0 copy-start.10
  8.5 0.1 convert_reduce_fusion.2
  8.6 0.2 fusion.35
  8.8 0.0 copy-start.3
  8.8 0.0 copy-done
  8.8 3.3 %convert_reduce_fusion.3 = (f32[1024]{0:T(1024)S(1)}, bf16[1,1024,256]{1,2,0:T(8,128)(2,1)}) fusion(bf16[1024,256]{1,0:T(8,128)(2,1)S(1)} %copy-done, bf16[256,1024]{1,0:T(8,128)(2,1)} %param.12, bf16[1,1024,256]{1,2,0:T(8,128)(2,1)S(1)} %copy.38, f32[1024]{0:T(1024)S(1)} %add_rsqrt_fusion.4, f32[1024]{0:T(1024)S(1)} %broadcast_multiply_fusion.4), kind=kOutput, calls=%fused_computation.50 | convolution fusion | flops 1078197248 | bytes 2109440 | tf_op jit(solution)/shard_map/dot_general | solution.py:31
  12.1 1.2 fusion.37
  13.3 0.0 copy-done.10
  13.3 1.3 fusion.34
  14.7 2.2 %collective-permute-start = (bf16[1,1024,32]{1,2,0:T(8,128)(2,1)S(1)}, bf16[1,1024,32]{1,2,0:T(8,128)(2,1)S(1)}, u32[]{:S(2)}, u32[]{:S(2)}) collective-permute-start(bf16[1,1024,32]{1,2,0:T(8,128)(2,1)S(1)} %get-tuple-element.25), channel_id=1, source_target_pairs={{0,64},{64,0},{1,65},{65,1},{2,66},{66,2},{3,67},{67,3},{4,68},{68... | collective-permute-start | bytes 196616 | tf_op jit(solution)/shard_map/ppermute | solution.py:56
  16.9 0.1 collective-permute-start.1
  17.0 0.0 copy-done.3
  17.0 0.6 convert_reduce_fusion
  17.6 2.4 %fusion.5 = f32[16,512]{1,0:T(8,128)S(1)} fusion(bf16[16,512,128]{2,1,0:T(8,128)(2,1)S(1)} %copy-done.3, f32[16,512]{1,0:T(8,128)S(1)} %broadcast_multiply_fusion.2), kind=kLoop, calls=%fused_computation.13 | loop fusion | flops 4186112 | bytes 2162688 | tf_op jit(solution)/shard_map/reduce_sum | solution.py:12
  20.0 3.4 %fusion.6 = bf16[16,512,128]{2,1,0:T(8,128)(2,1)} fusion(bf16[16,512,128]{2,1,0:T(8,128)(2,1)S(1)} %copy-done.3, f32[16,512]{1,0:T(8,128)S(1)} %add_rsqrt_fusion.2, f32[16,512]{1,0:T(8,128)S(1)} %broadcast_multiply_fusion.2), kind=kLoop, calls=%fused_computation.14 | loop fusion | flops 4194304 | bytes 4259840 | tf_op jit(solution)/shard_map/convert_element_type | solution.py:82
  23.5 0.0 collective-permute-done.1
  23.5 0.6 fusion.53
  24.1 0.0 all-gather.2.cloned.1.call-update
  24.1 0.0 copy-done.7
  24.1 4.5 %convolution_bitcast_fusion = f32[640,8192]{0,1:T(8,128)S(1)} fusion(bf16[8192,128]{1,0:T(8,128)(2,1)} %bitcast.88, bf16[128,640]{1,0:T(8,128)(2,1)S(1)} %copy-done.7), kind=kOutput, calls=%fused_computation.1 | convolution fusion | flops 1342177280 | bytes 23232512 | tf_op jit(solution)/shard_map/dot_general | solution.py:84
  28.6 0.0 copy-start.2
  28.6 4.4 %fusion.13 = (bf16[128,8192]{0,1:T(8,128)(2,1)}, bf16[128,8192]{0,1:T(8,128)(2,1)}) fusion(f32[640,8192]{0,1:T(8,128)S(1)} %convolution_bitcast_fusion), kind=kLoop, calls=%fused_computation.24 | loop fusion | flops 10485760 | bytes 20971520 | tf_op jit(solution)/shard_map/convert_element_type | solution.py:92
  33.0 3.8 %copy-done.2 = f32[640,8192]{0,1:T(8,128)} copy-done((f32[640,8192]{0,1:T(8,128)}, f32[640,8192]{0,1:T(8,128)S(1)}, u32[]{:S(2)}) %copy-start.2) | copy-done | bytes 20971544
  36.8 4.6 %copy.40 = bf16[128,1,16,512]{3,2,1,0:T(8,128)(2,1)} copy(bf16[128,1,16,512]{0,3,2,1:T(8,128)(2,1)} %bitcast.85) | data formatting | bytes 4194304 | tf_op jit(solution)/shard_map/convert_element_type | solution.py:95
  41.5 4.6 %copy.39 = bf16[128,1,16,512]{3,2,1,0:T(8,128)(2,1)} copy(bf16[128,1,16,512]{0,3,2,1:T(8,128)(2,1)} %bitcast.84) | data formatting | bytes 4194304 | tf_op jit(solution)/shard_map/convert_element_type | solution.py:92
  46.0 0.0 collective-permute-done
  46.1 0.4 copy.43
  46.5 1.1 reshape.218
  47.5 12.3 %all-to-all-start.1 = ((bf16[64,2,512]{2,1,0:T(2,128)(2,1)}), bf16[64,2,512]{2,1,0:T(2,128)(2,1)S(1)}, u32[]{:S(2)}, u32[]{:S(2)}) async-start(bf16[64,2,512]{2,1,0:T(2,128)(2,1)} %reshape.218), calls=%async_computation.1 | async-start | bytes 262144 | tf_op jit(solution)/shard_map/all_to_all | solution.py:57
  59.9 4.6 %pad_maximum_fusion = bf16[128,2,16,512]{3,2,1,0:T(8,128)(2,1)} fusion(bf16[128,1,16,512]{3,2,1,0:T(8,128)(2,1)} %copy.40, bf16[128,1,16,512]{3,2,1,0:T(8,128)(2,1)} %copy.39), kind=kLoop, calls=%fused_computation.33 | loop fusion | flops 2097152 | bytes 8388608 | tf_op jit(solution)/shard_map/stack | solution.py:70
  64.5 6.1 %all-to-all-done.1 = bf16[64,2,512]{2,1,0:T(2,128)(2,1)S(1)} async-done(((bf16[64,2,512]{2,1,0:T(2,128)(2,1)}), bf16[64,2,512]{2,1,0:T(2,128)(2,1)S(1)}, u32[]{:S(2)}, u32[]{:S(2)}) %all-to-all-start.1) | async-done | bytes 131104 | tf_op jit(solution)/shard_map/all_to_all | solution.py:57
  70.6 5.1 %all-to-all-start = ((bf16[128,2,16,512]{3,2,1,0:T(8,128)(2,1)}), bf16[128,2,16,512]{3,2,1,0:T(8,128)(2,1)}, u32[]{:S(2)}, u32[]{:S(2)}) async-start(bf16[128,2,16,512]{3,2,1,0:T(8,128)(2,1)} %pad_maximum_fusion), calls=%async_computation | async-start | bytes 8388608 | tf_op jit(solution)/shard_map/all_to_all | solution.py:69
  75.7 0.3 reshape.219
  76.0 0.1 copy.44
  76.1 59.0 %all-to-all-done = bf16[128,2,16,512]{3,2,1,0:T(8,128)(2,1)} async-done(((bf16[128,2,16,512]{3,2,1,0:T(8,128)(2,1)}), bf16[128,2,16,512]{3,2,1,0:T(8,128)(2,1)}, u32[]{:S(2)}, u32[]{:S(2)}) %all-to-all-start) | async-done | bytes 4194336 | tf_op jit(solution)/shard_map/all_to_all | solution.py:69
  135.1 2.7 %fusion.56 = (bf16[128,1,16,512]{3,2,1,0:T(8,128)(2,1)S(1)}, bf16[128,1,16,512]{3,2,1,0:T(8,128)(2,1)S(1)}) fusion(bf16[128,2,16,512]{3,2,1,0:T(8,128)(2,1)} %all-to-all-done), kind=kLoop, calls=%fused_computation.87 | loop fusion | bytes 8388608 | tf_op jit(solution)/shard_map/slice | solution.py:72
  137.8 3.7 %fusion.25 = bf16[2,1024,512]{1,2,0:T(8,128)(2,1)} fusion(bf16[2,2,512,512]{3,2,1,0:T(8,128)(2,1)S(1)} %bitcast.95, bf16[2,1024,512,1]{2,1,3,0:T(8,128)(2,1)S(1)} %bitcast.94), kind=kOutput, calls=%fused_computation.42 | convolution fusion | flops 2148532224 | bytes 6291456 | tf_op jit(solution)/shard_map/bik,bhjk->hij/dot_general | solution.py:107
  141.5 4.0 %copy.42 = bf16[2,1024,512]{2,1,0:T(8,128)(2,1)} copy(bf16[2,1024,512]{1,2,0:T(8,128)(2,1)} %fusion.25) | data formatting | bytes 4194304 | tf_op jit(solution)/shard_map/convert_element_type | solution.py:109
  145.5 7.5 %all-to-all-start.2 = ((bf16[128,16,512]{2,1,0:T(8,128)(2,1)}), bf16[128,16,512]{2,1,0:T(8,128)(2,1)}, u32[]{:S(2)}, u32[]{:S(2)}) async-start(bf16[128,16,512]{2,1,0:T(8,128)(2,1)} %bitcast.86), calls=%async_computation.2 | async-start | bytes 4194304 | tf_op jit(solution)/shard_map/all_to_all | solution.py:76
  153.0 0.0 copy-done.5
  153.0 1.0 copy.50
  154.0 0.0 copy-done.6
  154.0 0.1 copy.47
  154.1 0.9 copy.48
  155.0 1.1 copy.46
  156.0 6.5 %copy.49.r_ref = bf16[32,128,512]{2,1,0:T(8,128)(2,1)} copy(bf16[32,128,512]{2,0,1:T(8,128)(2,1)} %all-gather.2.cloned.1.call-done) | data formatting | bytes 8388608 | tf_op jit(solution)/shard_map/optimization_barrier | solution.py:211
  162.5 19.9 %shard_map.113 = f32[16,512,128]{2,1,0:T(8,128)} custom-call(bf16[512,128]{1,0:T(8,128)(2,1)} %bitcast.99, bf16[32,128,512]{2,1,0:T(8,128)(2,1)} %copy.49.r_ref, bf16[128,1024]{1,0:T(8,128)(2,1)} %bitcast.98), custom_call_target="tpu_custom_call" | custom-call | flops 4294967296 | bytes 8388608 | tf_op jit(solution)/shard_map/pallas_call | solution.py:176
  182.5 0.3 all-to-all-done.2
  182.8 2.0 convert_reduce_fusion.1
  184.7 2.2 %fusion.7 = f32[16,512]{1,0:T(8,128)S(1)} fusion(bf16[128,16,512]{2,1,0:T(8,128)(2,1)} %all-to-all-done.2, f32[16,512]{1,0:T(8,128)S(1)} %broadcast_multiply_fusion.1), kind=kLoop, calls=%fused_computation.15 | loop fusion | flops 4186112 | bytes 2162688 | tf_op jit(solution)/shard_map/reduce_sum | solution.py:12
  187.0 0.0 copy-start.11
  187.0 2.2 %fusion.8 = bf16[128,16,512]{2,1,0:T(8,128)(2,1)S(1)} fusion(bf16[128,16,512]{2,1,0:T(8,128)(2,1)} %all-to-all-done.2, f32[16,512]{1,0:T(8,128)S(1)} %add_rsqrt_fusion.1, f32[16,512]{1,0:T(8,128)S(1)} %broadcast_multiply_fusion.1), kind=kLoop, calls=%fused_computation.16 | loop fusion | flops 4194304 | bytes 4259840 | tf_op jit(solution)/shard_map/convert_element_type | solution.py:124
  189.1 1.4 copy.53
  190.5 3.5 %fusion = f32[128,8192]{0,1:T(8,128)S(1)} fusion(bf16[128,8192]{1,0:T(8,128)(2,1)S(1)} %bitcast.92, bf16[128,128]{1,0:T(8,128)(2,1)S(1)} %copy-done.11, f32[640,8192]{0,1:T(8,128)} %copy-done.2), kind=kOutput, calls=%fused_computation.3 | convolution fusion | flops 272629760 | bytes 10518528 | tf_op jit(solution)/shard_map/dot_general | solution.py:127
  194.0 1.2 fusion.27
  195.3 0.0 copy-start.8
  195.3 0.0 copy-start.9
  195.3 2.4 %multiply_reduce_fusion = f32[16,512]{1,0:T(8,128)S(1)} fusion(f32[16,512]{1,0:T(8,128)S(1)} %broadcast_multiply_fusion, f32[16,512,128]{2,1,0:T(8,128)S(1)} %bitcast.82, bf16[16,512,128]{2,1,0:T(8,128)(2,1)S(1)} %copy-done.3), kind=kLoop, calls=%fused_computation.37 | loop fusion | flops 5234688 | bytes 6356992 | tf_op jit(solution)/shard_map/reduce_sum | solution.py:12
  197.8 0.0 copy-done.4
  197.8 0.0 copy-start.1
  197.8 8.9 %add_convert_fusion = bf16[16,512,128]{2,1,0:T(8,128)(2,1)} fusion(f32[16,512,128]{2,1,0:T(8,128)} %shard_map.113, f32[16,512]{1,0:T(8,128)S(1)} %add_rsqrt_fusion, f32[16,512]{1,0:T(8,128)S(1)} %broadcast_multiply_fusion, f32[16,512,128]{2,1,0:T(8,128)} %bitcast.83, bf16[16,512,128]{2,1,0:T(8,128)(2,1)S(1)} %copy-done.3, ...), kind=kOutput, calls=%fused_computation.35 | convolution fusion | flops 2166358016 | bytes 12910592 | tf_op jit(solution)/shard_map/ijh,hd->ijd/dot_general | solution.py:139
  (23 shorter events, 0.2 us)
Async XLA Ops:
  7.2 1.7 copy-start
  7.2 138.4 %all-gather.2.cloned.1.call-start = ((), (), s32[]{:S(2)}) async-start(), calls=%async_computation.3 | async-start | bytes 4259840 | tf_op jit(solution)/shard_map/all_gather | solution.py:63
  8.5 4.8 %copy-start.10 = (bf16[256,64]{0,1:T(8,128)(2,1)S(1)}, bf16[256,64]{0,1:T(8,128)(2,1)}, u32[]{:S(2)}) copy-start(bf16[256,64]{0,1:T(8,128)(2,1)} %param.14) | copy-start | bytes 98308
  8.8 8.2 %copy-start.3 = (bf16[16,512,128]{2,1,0:T(8,128)(2,1)S(1)}, bf16[16,512,128]{2,1,0:T(8,128)(2,1)}, u32[]{:S(2)}) copy-start(bf16[16,512,128]{2,1,0:T(8,128)(2,1)} %param.11) | copy-start | bytes 6291460
  14.7 31.4 %collective-permute-start = (bf16[1,1024,32]{1,2,0:T(8,128)(2,1)S(1)}, bf16[1,1024,32]{1,2,0:T(8,128)(2,1)S(1)}, u32[]{:S(2)}, u32[]{:S(2)}) collective-permute-start(bf16[1,1024,32]{1,2,0:T(8,128)(2,1)S(1)} %get-tuple-element.25), channel_id=1, source_target_pairs={{0,64},{64,0},{1,65},{65,1},{2,66},{66,2},{3,67},{67,3},{4,68},{68... | collective-permute-start | bytes 196616 | tf_op jit(solution)/shard_map/ppermute | solution.py:56
  16.9 7.2 %copy-start.7 = (bf16[128,640]{1,0:T(8,128)(2,1)S(1)}, bf16[128,640]{1,0:T(8,128)(2,1)}, u32[]{:S(2)}) copy-start(bf16[128,640]{1,0:T(8,128)(2,1)} %param.16) | copy-start | bytes 491524
  16.9 6.6 %collective-permute-start.1 = (bf16[1,32,512]{2,1,0:T(8,128)(2,1)S(1)}, bf16[1,32,512]{2,1,0:T(8,128)(2,1)S(1)}, u32[]{:S(2)}, u32[]{:S(2)}) collective-permute-start(bf16[1,32,512]{2,1,0:T(8,128)(2,1)S(1)} %get-tuple-element.27), channel_id=1, source_target_pairs={{0,64},{64,0},{1,65},{65,1},{2,66},{66,2},{3,67},{67,3},{4,68},{68... | collective-permute-start | bytes 98312 | tf_op jit(solution)/shard_map/ppermute | solution.py:62
  28.6 8.2 %copy-start.2 = (f32[640,8192]{0,1:T(8,128)}, f32[640,8192]{0,1:T(8,128)S(1)}, u32[]{:S(2)}) copy-start(f32[640,8192]{0,1:T(8,128)S(1)} %convolution_bitcast_fusion) | copy-start | bytes 62914564
  47.5 23.0 %all-to-all-start.1 = ((bf16[64,2,512]{2,1,0:T(2,128)(2,1)}), bf16[64,2,512]{2,1,0:T(2,128)(2,1)S(1)}, u32[]{:S(2)}, u32[]{:S(2)}) async-start(bf16[64,2,512]{2,1,0:T(2,128)(2,1)} %reshape.218), calls=%async_computation.1 | async-start | bytes 262144 | tf_op jit(solution)/shard_map/all_to_all | solution.py:57
  70.6 64.6 %all-to-all-start = ((bf16[128,2,16,512]{3,2,1,0:T(8,128)(2,1)}), bf16[128,2,16,512]{3,2,1,0:T(8,128)(2,1)}, u32[]{:S(2)}, u32[]{:S(2)}) async-start(bf16[128,2,16,512]{3,2,1,0:T(8,128)(2,1)} %pad_maximum_fusion), calls=%async_computation | async-start | bytes 8388608 | tf_op jit(solution)/shard_map/all_to_all | solution.py:69
  141.5 11.5 %copy-start.5 = (bf16[1,1024,256]{1,2,0:T(8,128)(2,1)S(1)}, bf16[1,1024,256]{1,2,0:T(8,128)(2,1)}, u32[]{:S(2)}) copy-start(bf16[1,1024,256]{1,2,0:T(8,128)(2,1)} %get-tuple-element.29) | copy-start | bytes 1572868
  141.5 12.5 %copy-start.6 = (bf16[1024,128]{1,0:T(8,128)(2,1)S(1)}, bf16[1024,128]{1,0:T(8,128)(2,1)}, u32[]{:S(2)}) copy-start(bf16[1024,128]{1,0:T(8,128)(2,1)} %param.15) | copy-start | bytes 786436
  145.5 37.3 %all-to-all-start.2 = ((bf16[128,16,512]{2,1,0:T(8,128)(2,1)}), bf16[128,16,512]{2,1,0:T(8,128)(2,1)}, u32[]{:S(2)}, u32[]{:S(2)}) async-start(bf16[128,16,512]{2,1,0:T(8,128)(2,1)} %bitcast.86), calls=%async_computation.2 | async-start | bytes 4194304 | tf_op jit(solution)/shard_map/all_to_all | solution.py:76
  187.0 3.6 %copy-start.11 = (bf16[128,128]{1,0:T(8,128)(2,1)S(1)}, bf16[128,128]{1,0:T(8,128)(2,1)}, u32[]{:S(2)}) copy-start(bf16[128,128]{1,0:T(8,128)(2,1)} %param.17) | copy-start | bytes 98308
  194.0 3.7 %copy-start.4 = (f32[128,8192]{0,1:T(8,128)}, f32[128,8192]{0,1:T(8,128)S(1)}, u32[]{:S(2)}) copy-start(f32[128,8192]{0,1:T(8,128)S(1)} %fusion) | copy-start | bytes 12582916
  195.3 2.5 %copy-start.8 = (bf16[512,128]{1,0:T(8,128)(2,1)S(1)}, bf16[512,128]{1,0:T(8,128)(2,1)}, u32[]{:S(2)}) copy-start(bf16[512,128]{1,0:T(8,128)(2,1)} %param.19) | copy-start | bytes 393220
  195.3 2.5 %copy-start.9 = (bf16[128,512]{1,0:T(8,128)(2,1)S(1)}, bf16[128,512]{1,0:T(8,128)(2,1)}, u32[]{:S(2)}) copy-start(bf16[128,512]{1,0:T(8,128)(2,1)} %param.18) | copy-start | bytes 393220
  197.8 8.9 %copy-start.1 = (bf16[1024,256]{1,0:T(8,128)(2,1)S(1)}, bf16[1024,256]{1,0:T(8,128)(2,1)}, u32[]{:S(2)}) copy-start(bf16[1024,256]{1,0:T(8,128)(2,1)} %param.13) | copy-start | bytes 1572868
Sparse Core Ops, SparseCore 0:
  24.2 116.5 all-gather.1

commit v2 on v1

--- a/solution.py
+++ b/solution.py
@@ -53,23 +53,27 @@
 
 def gather_sides(left_side, right_side):
     swap = [(0, 1), (1, 0)]
-    left_pair = branch_pair(left_side, lax.ppermute(left_side, "branch", swap))
-    left_gathered = lax.all_to_all(left_pair, "rows", split_axis=1, concat_axis=0, tiled=True)
     half = right_side.shape[2] // 2
     me = lax.axis_index("branch")
     keep = lax.dynamic_slice_in_dim(right_side, me * half, half, axis=2)
     send = lax.dynamic_slice_in_dim(right_side, (1 - me) * half, half, axis=2)
     right_pair = branch_pair(keep, lax.ppermute(send, "branch", swap))
     right_gathered = lax.all_gather(jnp.swapaxes(right_pair, 0, 1), "rows", axis=1, tiled=True)
-    return left_gathered, right_gathered
-
-
-def send_whole(tri_left, tri_right):
+    return right_gathered
+
+
+def send_whole(tri_left, tri_right, left_side):
     both = ("branch", "rows")
-    moved = lax.all_to_all(
-        jnp.stack([tri_left, tri_right], axis=1), both, split_axis=0, concat_axis=0, tiled=True
-    )
-    return moved[:, 0], moved[:, 1]
+    chans, tile_rows, columns = tri_left.shape
+    halves = lax.axis_size("branch")
+    tri_flat = jnp.stack([tri_left, tri_right], axis=1).reshape(chans, -1)
+    left_dest = left_side.reshape(lax.axis_size("rows"), -1)
+    payload = jnp.concatenate([tri_flat, jnp.tile(left_dest, (halves, 1))], axis=1)
+    moved = lax.all_to_all(payload, both, split_axis=0, concat_axis=0, tiled=True)
+    tri_moved = moved[:, : tri_flat.shape[1]].reshape(chans, 2, tile_rows, columns)
+    left_gathered = moved[:, tri_flat.shape[1] :].reshape(halves, chans // halves, -1)
+    left_gathered = jnp.swapaxes(left_gathered, 0, 1).reshape(chans, -1, left_side.shape[-1])
+    return tri_moved[:, 0], tri_moved[:, 1], left_gathered
 
 
 def send_back(product):
@@ -201,12 +205,12 @@
     refreshed_homolog_features, left_side, right_side = alignment_branch(
         homolog_features, transition_expand_matrix, transition_contract_matrix, factor_pair_matrices
     )
-    left_gathered, right_gathered = gather_sides(left_side, right_side)
+    right_gathered = gather_sides(left_side, right_side)
     pairwise_input, right_side = lax.optimization_barrier((pairwise_input, right_side))
     pair_float, gate_vals, tri_left, tri_right = pair_front(
         pairwise_input, triangle_projection_weight
     )
-    left_chan, right_chan = send_whole(tri_left, tri_right)
+    left_chan, right_chan, left_gathered = send_whole(tri_left, tri_right, left_side)
     product = triangle_product(left_chan, right_chan)
     product, left_gathered, right_gathered = lax.optimization_barrier(
         (product, left_gathered, right_gathered)

time: 214 us -> 276 us (1.29)
  blocking collectives: 0 us -> 72.5 us
  waiting for transfers between devices: 65.5 us -> 0.34 us
  local copies, waits for them, and re-layouts: 33.8 us -> 83.5 us
  starting transfers between devices: 27.3 us -> 9.52 us
  other arithmetic: 27.6 us -> 42.7 us
  matrix products: 25.1 us -> 31.4 us
    all_to_all x0 -> x1, blocking collectives: none -> 72.5 us  [send_whole(): lax.all_to_all(payload, both, split_axis=0, concat_axis=0, tiled=True)]
    all_to_all x2 -> x0, waiting for transfers between devices: 65.1 us -> none  [the longest x1 59 us: send_whole(): lax.all_to_all(jnp.stack([tri_left, tri_right], axis=1), both, split_axis...]
    unnamed x29 -> x27, local copies, waits for them, and re-layouts: 8.91 us -> 30.4 us
    all_to_all x2, local copies, waits for them, and re-layouts: 0.11 us -> 18.2 us  [send_whole(): lax.all_to_all(payload, both, split_axis=0, concat_axis=0, tiled=True)]
    all_to_all x2 -> x0, starting transfers between devices: 17.5 us -> none  [the longest x1 12.3 us: gather_sides(): lax.all_to_all(left_pair, 'rows', split_axis=1, concat_axis=0, tiled=True)]
    slice x1 -> x7, local copies, waits for them, and re-layouts: 2.69 us -> 15.2 us  [the longest x3 11.7 us: send_whole(): return (tri_moved[:, 0], tri_moved[:, 1], left_gathered)]
    all_to_all x0 -> x2, other arithmetic: none -> 11.3 us  [send_whole(): lax.all_to_all(payload, both, split_axis=0, concat_axis=0, tiled=True)]
    convert_element_type x2 -> x0, local copies, waits for them, and re-layouts: 9.18 us -> none  [the longest x1 4.62 us: pair_front(): (jax.nn.sigmoid(proj_tile[3 * chans:]) * proj_tile[2 * chans:3 * chans])....]
  transfers between devices with their start and end apart: 6 -> 3, of which waited for: 3 -> 1; matrix products, arithmetic and copies ran while one was open for 24% -> 46% of each run, Pallas kernels for 9% -> 7%
where the time goes in v2:
time: 276 us; the launch traced here: 274 us
  local copies, waits for them, and re-layouts  83.5 us (30%)
  blocking collectives  72.5 us (26%)
  other arithmetic  42.7 us (15%)
  matrix products  31.4 us (11%)
  Pallas kernels  19.9 us (7%)
  between operations  14.4 us (5%)
  starting transfers between devices  9.52 us (3%)
    all_to_all x1, blocking collectives, send_whole(): lax.all_to_all(payload, both, split_axis=0, concat_axis=0, tiled=True)  72.5 us
    unnamed x27, local copies, waits for them, and re-layouts  30.4 us
    pallas_call x1, Pallas kernels, outer_product(): pl.pallas_call(outer_kernel, out_shape=jax.ShapeDtypeStruct((tile_rows, c...  19.9 us
    all_to_all x2, local copies, waits for them, and re-layouts, send_whole(): lax.all_to_all(payload, both, split_axis=0, concat_axis=0, tiled=True)  18.2 us
    slice x3, local copies, waits for them, and re-layouts, send_whole(): return (tri_moved[:, 0], tri_moved[:, 1], left_gathered)  11.7 us
    all_to_all x2, other arithmetic, send_whole(): lax.all_to_all(payload, both, split_axis=0, concat_axis=0, tiled=True)  11.3 us
    convert_element_type x1, other arithmetic, pair_front(): (jax.nn.sigmoid(proj_tile[chans:2 * chans]) * proj_tile[:chans]).astype(j...  9.14 us
    dot_general x1, matrix products, pair_back(): jnp.einsum('ijh,hd->ijd', pair_hidden, pairwise_down_weight, preferred_el...  8.91 us
  transfers between devices with their start and end apart: 3, of which 1 were waited for; matrix products, arithmetic and copies ran while one was open for 46% of the time, Pallas kernels for 7%

profile of v2, /device:TPU:1, one launch (start us, length us, event | category | flops | bytes accessed | tf_op | source)
XLA Modules:
  0.0 274.3 jit_solution(13212087470917072829)
XLA Ops:
  7.2 0.0 copy-start
  7.2 0.0 all-gather.2.cloned.1.call-start
  7.2 1.3 copy.55
  8.5 0.0 copy-start.9
  8.5 0.1 convert_reduce_fusion.2
  8.7 0.2 fusion.35
  8.8 0.0 copy-start.2
  8.8 0.0 copy-done
  8.8 3.3 %convert_reduce_fusion.3 = (f32[1024]{0:T(1024)S(1)}, bf16[1,1024,256]{1,2,0:T(8,128)(2,1)}) fusion(bf16[1024,256]{1,0:T(8,128)(2,1)S(1)} %copy-done, bf16[256,1024]{1,0:T(8,128)(2,1)} %param.12, bf16[1,1024,256]{1,2,0:T(8,128)(2,1)S(1)} %copy.55, f32[1024]{0:T(1024)S(1)} %add_rsqrt_fusion.4, f32[1024]{0:T(1024)S(1)} %broadcast_multiply_fusion.4), kind=kOutput, calls=%fused_computation.51 | convolution fusion | flops 1078197248 | bytes 2109440 | tf_op jit(solution)/shard_map/dot_general | solution.py:31
  12.1 1.2 fusion.37
  13.3 1.3 fusion.34
  14.7 0.0 copy-start.6
  14.7 2.2 collective-permute-start
  16.9 0.6 convert_reduce_fusion
  17.6 2.4 fusion.5
  19.9 2.5 fusion.6
  22.4 8.5 %convolution_bitcast_fusion = f32[640,8192]{0,1:T(8,128)} fusion(bf16[8192,128]{1,0:T(8,128)(2,1)S(1)} %bitcast.93, bf16[128,640]{1,0:T(8,128)(2,1)S(1)} %copy-done.6), kind=kOutput, calls=%fused_computation.1 | convolution fusion | flops 1342177280 | bytes 23232512 | tf_op jit(solution)/shard_map/dot_general | solution.py:88
  30.9 0.0 collective-permute-done
  30.9 0.6 fusion.53
  31.6 0.0 all-gather.2.cloned.1.call-update
  31.6 9.1 %fusion.13 = (bf16[128,8192]{0,1:T(8,128)(2,1)}, bf16[128,8192]{0,1:T(8,128)(2,1)}) fusion(f32[640,8192]{0,1:T(8,128)} %convolution_bitcast_fusion), kind=kLoop, calls=%fused_computation.25 | loop fusion | flops 10485760 | bytes 20971520 | tf_op jit(solution)/shard_map/convert_element_type | solution.py:96
  40.7 0.2 copy.57
  40.9 0.2 tile.10
  41.1 4.6 %pad_maximum_fusion = bf16[128,2,16,512]{0,3,2,1:T(8,128)(2,1)} fusion(bf16[128,1,16,512]{0,3,2,1:T(8,128)(2,1)} %bitcast.91, bf16[128,1,16,512]{0,3,2,1:T(8,128)(2,1)} %bitcast.90), kind=kLoop, calls=%fused_computation.34 | loop fusion | flops 2097152 | bytes 8388608 | tf_op jit(solution)/shard_map/stack | solution.py:69
  45.7 6.4 %copy.71 = bf16[128,16384]{1,0:T(8,128)(2,1)} copy(bf16[128,16384]{0,1:T(8,128)(2,1)} %bitcast.88) | data formatting | bytes 8388608 | tf_op jit(solution)/shard_map/reshape | solution.py:69
  52.2 4.5 %maximum_bitcast_fusion = bf16[128,1,16896]{2,0,1:T(8,128)(2,1)} fusion(bf16[128,512]{1,0:T(8,128)(2,1)S(1)} %bitcast.99, bf16[128,16384]{1,0:T(8,128)(2,1)} %copy.71), kind=kLoop, calls=%fused_computation.13 | loop fusion | flops 8650752 | bytes 8650752 | tf_op jit(solution)/shard_map/all_to_all | solution.py:72
  56.7 0.5 broadcast.165
  57.2 6.8 %reduce.4 = bf16[128,16896]{1,0:T(8,128)(2,1)} reduce(bf16[128,1,16896]{2,0,1:T(8,128)(2,1)} %maximum_bitcast_fusion, bf16[]{:T(256)} %broadcast.165), dimensions={1}, to_apply=%copy.58.reduce_sub_computation | reduce | bytes 8650754 | tf_op jit(solution)/shard_map/all_to_all | solution.py:72
  64.0 7.0 %reshape.240 = bf16[128,2,8448]{2,1,0:T(2,128)(2,1)} reshape(bf16[128,16896]{1,0:T(8,128)(2,1)} %reduce.4) | data formatting | bytes 8650752
  71.1 72.5 %all_to_all.17 = bf16[128,2,8448]{2,1,0:T(2,128)(2,1)} all-to-all(bf16[128,2,8448]{2,1,0:T(2,128)(2,1)} %reshape.240), channel_id=1, replica_groups=mesh['branch'=2,'rows'=64] {'branch','rows'}, dimensions={0} | all-to-all | bytes 8650752 | tf_op jit(solution)/shard_map/all_to_all | solution.py:72
  143.6 19.6 %reshape.241 = bf16[128,1,16896]{2,1,0:T(2,128)(2,1)} reshape(bf16[128,2,8448]{2,1,0:T(2,128)(2,1)} %all_to_all.17) | data formatting | bytes 8650752
  163.2 17.7 %copy.59 = bf16[128,1,16896]{0,2,1:T(8,128)(2,1)} copy(bf16[128,1,16896]{2,1,0:T(2,128)(2,1)} %reshape.241) | data formatting | bytes 8650752 | tf_op jit(solution)/shard_map/all_to_all | solution.py:72
  180.9 2.4 slice.67
  183.3 0.9 slice.70
  184.2 2.5 fusion.56
  186.7 4.6 %copy.60 = bf16[128,1,16,512]{3,2,0,1:T(8,128)(2,1)} copy(bf16[128,1,16,512]{0,3,2,1:T(8,128)(2,1)} %get-tuple-element.25) | data formatting | bytes 4194304 | tf_op jit(solution)/shard_map/slice | solution.py:76
  191.3 4.6 %copy.61 = bf16[128,1,16,512]{3,2,0,1:T(8,128)(2,1)} copy(bf16[128,1,16,512]{0,3,2,1:T(8,128)(2,1)} %get-tuple-element.24) | data formatting | bytes 4194304 | tf_op jit(solution)/shard_map/slice | solution.py:76
  195.9 5.9 %fusion.25 = bf16[2,1024,512]{1,2,0:T(8,128)(2,1)} fusion(bf16[2,2,512,512]{3,2,1,0:T(8,128)(2,1)} %bitcast.95, bf16[2,1024,512,1]{2,1,3,0:T(8,128)(2,1)} %bitcast.96), kind=kOutput, calls=%fused_computation.43 | convolution fusion | flops 2148532224 | bytes 6291456 | tf_op jit(solution)/shard_map/bik,bhjk->hij/dot_general | solution.py:111
  201.8 4.0 %copy.62 = bf16[2,1024,512]{2,1,0:T(8,128)(2,1)} copy(bf16[2,1024,512]{1,2,0:T(8,128)(2,1)} %fusion.25) | data formatting | bytes 4194304 | tf_op jit(solution)/shard_map/convert_element_type | solution.py:113
  205.8 0.1 copy.63
  205.9 0.1 copy.64
  206.1 0.3 reshape.225
  206.4 0.0 all-gather.2.cloned.1.call-done
  206.4 7.3 %all-to-all-start.1 = ((bf16[128,16,512]{2,1,0:T(8,128)(2,1)}), bf16[128,16,512]{2,1,0:T(8,128)(2,1)}, u32[]{:S(2)}, u32[]{:S(2)}) async-start(bf16[128,16,512]{2,1,0:T(8,128)(2,1)} %bitcast.89), calls=%async_computation.1 | async-start | bytes 4194304 | tf_op jit(solution)/shard_map/all_to_all | solution.py:80
  213.7 1.0 copy.69
  214.7 0.1 copy.66
  214.8 0.9 copy.67
  215.6 6.5 %copy.68.r_ref = bf16[32,128,512]{2,1,0:T(8,128)(2,1)} copy(bf16[32,128,512]{2,0,1:T(8,128)(2,1)} %all-gather.2.cloned.1.call-done) | data formatting | bytes 8388608 | tf_op jit(solution)/shard_map/optimization_barrier | solution.py:215
  222.1 1.1 copy.65
  223.2 19.9 %shard_map.113 = f32[16,512,128]{2,1,0:T(8,128)} custom-call(bf16[512,128]{1,0:T(8,128)(2,1)} %bitcast.103, bf16[32,128,512]{2,1,0:T(8,128)(2,1)} %copy.68.r_ref, bf16[128,1024]{1,0:T(8,128)(2,1)} %bitcast.102), custom_call_target="tpu_custom_call" | custom-call | flops 4294967296 | bytes 8388608 | tf_op jit(solution)/shard_map/pallas_call | solution.py:180
  243.2 0.3 all-to-all-done.1
  243.5 2.0 convert_reduce_fusion.1
  245.4 2.2 fusion.7
  247.6 0.0 copy-start.10
  247.6 2.2 fusion.8
  249.8 1.4 copy.72
  251.2 3.5 %fusion = f32[128,8192]{0,1:T(8,128)S(1)} fusion(bf16[128,8192]{1,0:T(8,128)(2,1)S(1)} %bitcast.97, bf16[128,128]{1,0:T(8,128)(2,1)S(1)} %copy-done.10, f32[640,8192]{0,1:T(8,128)} %convolution_bitcast_fusion), kind=kOutput, calls=%fused_computation.3 | convolution fusion | flops 272629760 | bytes 10518528 | tf_op jit(solution)/shard_map/dot_general | solution.py:131
  254.7 1.2 fusion.27
  256.0 0.0 copy-start.7
  256.0 0.0 copy-start.8
  256.0 2.4 multiply_reduce_fusion
  258.5 0.0 copy-start.1
  258.5 8.9 %add_convert_fusion = bf16[16,512,128]{2,1,0:T(8,128)(2,1)} fusion(f32[16,512,128]{2,1,0:T(8,128)} %shard_map.113, f32[16,512]{1,0:T(8,128)S(1)} %add_rsqrt_fusion, f32[16,512]{1,0:T(8,128)S(1)} %broadcast_multiply_fusion, f32[16,512,128]{2,1,0:T(8,128)} %bitcast.86, bf16[16,512,128]{2,1,0:T(8,128)(2,1)S(1)} %copy-done.2, ...), kind=kOutput, calls=%fused_computation.36 | convolution fusion | flops 2166358016 | bytes 12910592 | tf_op jit(solution)/shard_map/ijh,hd->ijd/dot_general | solution.py:143
  267.4 0.0 copy-done.1
  (25 shorter events, 0.1 us)
Async XLA Ops:
  7.2 1.7 copy-start
  7.2 199.2 %all-gather.2.cloned.1.call-start = ((), (), s32[]{:S(2)}) async-start(), calls=%async_computation.2 | async-start | bytes 4259840 | tf_op jit(solution)/shard_map/all_gather | solution.py:61
  8.5 4.8 %copy-start.9 = (bf16[256,64]{0,1:T(8,128)(2,1)S(1)}, bf16[256,64]{0,1:T(8,128)(2,1)}, u32[]{:S(2)}) copy-start(bf16[256,64]{0,1:T(8,128)(2,1)} %param.14) | copy-start | bytes 98308
  8.8 8.1 %copy-start.2 = (bf16[16,512,128]{2,1,0:T(8,128)(2,1)S(1)}, bf16[16,512,128]{2,1,0:T(8,128)(2,1)}, u32[]{:S(2)}) copy-start(bf16[16,512,128]{2,1,0:T(8,128)(2,1)} %param.11) | copy-start | bytes 6291460
  14.7 7.7 %copy-start.6 = (bf16[128,640]{1,0:T(8,128)(2,1)S(1)}, bf16[128,640]{1,0:T(8,128)(2,1)}, u32[]{:S(2)}) copy-start(bf16[128,640]{1,0:T(8,128)(2,1)} %param.16) | copy-start | bytes 491524
  14.7 16.2 %collective-permute-start = (bf16[1,32,512]{2,1,0:T(8,128)(2,1)S(1)}, bf16[1,32,512]{2,1,0:T(8,128)(2,1)S(1)}, u32[]{:S(2)}, u32[]{:S(2)}) collective-permute-start(bf16[1,32,512]{2,1,0:T(8,128)(2,1)S(1)} %get-tuple-element.29), channel_id=1, source_target_pairs={{0,64},{64,0},{1,65},{65,1},{2,66},{66,2},{3,67},{67,3},{4,68},{68... | collective-permute-start | bytes 98312 | tf_op jit(solution)/shard_map/ppermute | solution.py:60
  201.8 11.9 %copy-start.4 = (bf16[1,1024,256]{1,2,0:T(8,128)(2,1)S(1)}, bf16[1,1024,256]{1,2,0:T(8,128)(2,1)}, u32[]{:S(2)}) copy-start(bf16[1,1024,256]{1,2,0:T(8,128)(2,1)} %get-tuple-element.31) | copy-start | bytes 1572868
  205.8 8.9 %copy-start.5 = (bf16[1024,128]{1,0:T(8,128)(2,1)S(1)}, bf16[1024,128]{1,0:T(8,128)(2,1)}, u32[]{:S(2)}) copy-start(bf16[1024,128]{1,0:T(8,128)(2,1)} %param.15) | copy-start | bytes 786436
  206.4 37.1 %all-to-all-start.1 = ((bf16[128,16,512]{2,1,0:T(8,128)(2,1)}), bf16[128,16,512]{2,1,0:T(8,128)(2,1)}, u32[]{:S(2)}, u32[]{:S(2)}) async-start(bf16[128,16,512]{2,1,0:T(8,128)(2,1)} %bitcast.89), calls=%async_computation.1 | async-start | bytes 4194304 | tf_op jit(solution)/shard_map/all_to_all | solution.py:80
  247.6 3.6 %copy-start.10 = (bf16[128,128]{1,0:T(8,128)(2,1)S(1)}, bf16[128,128]{1,0:T(8,128)(2,1)}, u32[]{:S(2)}) copy-start(bf16[128,128]{1,0:T(8,128)(2,1)} %param.17) | copy-start | bytes 98308
  254.7 3.7 %copy-start.3 = (f32[128,8192]{0,1:T(8,128)}, f32[128,8192]{0,1:T(8,128)S(1)}, u32[]{:S(2)}) copy-start(f32[128,8192]{0,1:T(8,128)S(1)} %fusion) | copy-start | bytes 12582916
  256.0 2.5 copy-start.7
  256.0 2.5 copy-start.8
  258.5 8.9 %copy-start.1 = (bf16[1024,256]{1,0:T(8,128)(2,1)S(1)}, bf16[1024,256]{1,0:T(8,128)(2,1)}, u32[]{:S(2)}) copy-start(bf16[1024,256]{1,0:T(8,128)(2,1)} %param.13) | copy-start | bytes 1572868
Sparse Core Ops, SparseCore 0:
  31.7 116.1 all-gather.1

commit v3 on v1

--- a/solution.py
+++ b/solution.py
@@ -82,20 +82,19 @@
     pair_norm = standardize_features(pair_float, -1).astype(jnp.bfloat16)
     norm_flat = pair_norm.reshape(tile_rows * columns, chans)
     proj_flat = lax.dot_general(
-        triangle_projection_weight,
+        triangle_projection_weight[:, : 4 * chans],
         norm_flat,
         (((0,), (1,)), ((), ())),
         preferred_element_type=jnp.float32,
     )
-    proj_tile = proj_flat[: 4 * chans].reshape(4 * chans, tile_rows, columns)
-    gate_vals = jax.nn.sigmoid(proj_flat[4 * chans :])
+    proj_tile = proj_flat.reshape(4 * chans, tile_rows, columns)
     tri_left = (jax.nn.sigmoid(proj_tile[chans : 2 * chans]) * proj_tile[:chans]).astype(
         jnp.bfloat16
     )
     tri_right = (jax.nn.sigmoid(proj_tile[3 * chans :]) * proj_tile[2 * chans : 3 * chans]).astype(
         jnp.bfloat16
     )
-    return pair_float, gate_vals, tri_left, tri_right
+    return tri_left, tri_right
 
 
 def triangle_product(left_chan, right_chan):
@@ -110,34 +109,69 @@
     return product.reshape(-1, tile_rows, columns)
 
 
+def back_kernel(prod_ref, pair_ref, outer_ref, wo_ref, wg_ref, wu_ref, wd_ref, out_ref):
+    rows, columns, chans = pair_ref.shape
+    for r in range(rows):
+        prod = prod_ref[:, r * columns : (r + 1) * columns].astype(jnp.float32)
+        prod_norm = standardize_features(prod, 0).T.astype(jnp.bfloat16)
+        tri_update = jnp.dot(prod_norm, wo_ref[...], preferred_element_type=jnp.float32)
+        pair_float = pair_ref[r].astype(jnp.float32)
+        pair_norm = standardize_features(pair_float, -1).astype(jnp.bfloat16)
+        gate = jax.nn.sigmoid(
+            jnp.dot(pair_norm, wg_ref[...], preferred_element_type=jnp.float32)
+        )
+        pair_mid = pair_float + gate * tri_update
+        mid_norm = standardize_features(pair_mid, -1).astype(jnp.bfloat16)
+        hidden = jnp.maximum(
+            jnp.dot(mid_norm, wu_ref[...], preferred_element_type=jnp.float32), 0.0
+        ).astype(jnp.bfloat16)
+        down = jnp.dot(hidden, wd_ref[...], preferred_element_type=jnp.float32)
+        out_ref[r] = (pair_mid + down + outer_ref[r]).astype(out_ref.dtype)
+
+
 def pair_back(
-    pair_float,
-    gate_vals,
+    pairwise_input,
     product_tile,
+    outer_update,
+    triangle_projection_weight,
     triangle_output_weight,
     pairwise_up_weight,
     pairwise_down_weight,
 ):
-    tile_rows, columns, chans = pair_float.shape
-    prod_norm = (
-        standardize_features(product_tile.astype(jnp.float32), 0)
-        .astype(jnp.bfloat16)
-        .reshape(chans, tile_rows * columns)
-    )
-    tri_update = lax.dot_general(
+    tile_rows, columns, chans = pairwise_input.shape
+    step_rows = 4
+    prod_flat = product_tile.reshape(chans, tile_rows * columns)
+    gate_weight = triangle_projection_weight[:, 4 * chans :]
+    hidden = pairwise_up_weight.shape[1]
+    row_block = lambda g: (g, 0, 0)
+    fixed = lambda g: (0, 0)
+    return pl.pallas_call(
+        back_kernel,
+        out_shape=jax.ShapeDtypeStruct((tile_rows, columns, chans), jnp.bfloat16),
+        grid=(tile_rows // step_rows,),
+        in_specs=[
+            pl.BlockSpec((chans, step_rows * columns), lambda g: (0, g)),
+            pl.BlockSpec((step_rows, columns, chans), row_block),
+            pl.BlockSpec((step_rows, columns, chans), row_block),
+            pl.BlockSpec((chans, chans), fixed),
+            pl.BlockSpec((chans, chans), fixed),
+            pl.BlockSpec((chans, hidden), fixed),
+            pl.BlockSpec((hidden, chans), fixed),
+        ],
+        out_specs=pl.BlockSpec((step_rows, columns, chans), row_block),
+        cost_estimate=pl.CostEstimate(
+            flops=2 * tile_rows * columns * chans * (3 * chans + 2 * hidden) // 1,
+            transcendentals=tile_rows * columns * chans,
+            bytes_accessed=tile_rows * columns * chans * 10,
+        ),
+    )(
+        prod_flat,
+        pairwise_input,
+        outer_update,
         triangle_output_weight,
-        prod_norm,
-        (((0,), (0,)), ((), ())),
-        preferred_element_type=jnp.float32,
-    )
-    gated_update = jnp.transpose(gate_vals * tri_update).reshape(tile_rows, columns, chans)
-    pair_mid = pair_float + gated_update
-    mid_norm = standardize_features(pair_mid, -1).astype(jnp.bfloat16)
-    pair_hidden = jax.nn.relu(
-        jnp.einsum("ijd,dh->ijh", mid_norm, pairwise_up_weight, preferred_element_type=jnp.float32)
-    ).astype(jnp.bfloat16)
-    return pair_mid + jnp.einsum(
-        "ijh,hd->ijd", pair_hidden, pairwise_down_weight, preferred_element_type=jnp.float32
+        gate_weight,
+        pairwise_up_weight,
+        pairwise_down_weight,
     )
 
 
@@ -203,7 +237,7 @@
     )
     left_gathered, right_gathered = gather_sides(left_side, right_side)
     pairwise_input, right_side = lax.optimization_barrier((pairwise_input, right_side))
-    pair_float, gate_vals, tri_left, tri_right = pair_front(
+    tri_left, tri_right = pair_front(
         pairwise_input, triangle_projection_weight
     )
     left_chan, right_chan = send_whole(tri_left, tri_right)
@@ -214,15 +248,15 @@
     product_tile = send_back(product)
     outer_update = outer_product(left_gathered, right_gathered, outer_output_weight)
     product_tile, outer_update = lax.optimization_barrier((product_tile, outer_update))
-    pair_mid = pair_back(
-        pair_float,
-        gate_vals,
+    pairwise_output = pair_back(
+        pairwise_input,
         product_tile,
+        outer_update,
+        triangle_projection_weight,
         triangle_output_weight,
         pairwise_up_weight,
         pairwise_down_weight,
     )
-    pairwise_output = (pair_mid + outer_update).astype(jnp.bfloat16)
     return (refreshed_homolog_features, pairwise_output)
 
 

time: 214 us -> 196 us (0.916)
  Pallas kernels: 19.9 us -> 36.5 us
  matrix products: 25.1 us -> 9.27 us
  other arithmetic: 27.6 us -> 15.4 us
  local copies, waits for them, and re-layouts: 33.8 us -> 29.7 us
  starting transfers between devices: 27.3 us -> 24.7 us
    pallas_call x0 -> x1, Pallas kernels: none -> 16.6 us  [pair_back(): pl.pallas_call(back_kernel, out_shape=jax.ShapeDtypeStruct((tile_rows, co...]
    dot_general x3 -> x1, matrix products: 16.9 us -> 2.32 us  [pair_front(): lax.dot_general(triangle_projection_weight[:, :4 * chans], norm_flat, (((...]
    reduce_sum x5 -> x3, other arithmetic: 8.36 us -> 3.73 us  [standardize_features(): variance = jnp.mean(centered * centered, axis=dimension, keepdims=True)]
    reduce_sum x4 -> x2, other arithmetic: 3.91 us -> 0.71 us  [standardize_features(): average = jnp.mean(values, axis=dimension, keepdims=True)]
    all_gather x1, waiting for transfers between devices: 0.01 us -> 3.02 us  [gather_sides(): lax.all_gather(jnp.swapaxes(right_pair, 0, 1), 'rows', axis=1, tiled=True)]
    all_to_all x1, waiting for transfers between devices: 59 us -> 56.4 us  [send_whole(): lax.all_to_all(jnp.stack([tri_left, tri_right], axis=1), both, split_axis...]
    unnamed x29 -> x19, local copies, waits for them, and re-layouts: 8.91 us -> 6.39 us
    all_to_all x1, starting transfers between devices: 7.46 us -> 5.21 us  [send_back(): lax.all_to_all(product, ('branch', 'rows'), split_axis=0, concat_axis=0,...]
  transfers between devices with their start and end apart: 6 -> 6, of which waited for: 3 -> 4; matrix products, arithmetic and copies ran while one was open for 24% -> 23% of each run, Pallas kernels for 9% -> 10%
where the time goes in v3:
time: 196 us; the launch traced here: 195 us
  waiting for transfers between devices  65.1 us (33%)
  Pallas kernels  36.5 us (19%)
  local copies, waits for them, and re-layouts  29.7 us (15%)
  starting transfers between devices  24.7 us (13%)
  other arithmetic  15.4 us (8%)
  between operations  14.2 us (7%)
  matrix products  9.27 us (5%)
    all_to_all x1, waiting for transfers between devices, send_whole(): lax.all_to_all(jnp.stack([tri_left, tri_right], axis=1), both, split_axis...  56.4 us
    pallas_call x1, Pallas kernels, outer_product(): pl.pallas_call(outer_kernel, out_shape=jax.ShapeDtypeStruct((tile_rows, c...  19.9 us
    pallas_call x1, Pallas kernels, pair_back(): pl.pallas_call(back_kernel, out_shape=jax.ShapeDtypeStruct((tile_rows, co...  16.6 us
    all_to_all x1, starting transfers between devices, gather_sides(): lax.all_to_all(left_pair, 'rows', split_axis=1, concat_axis=0, tiled=True)  12.2 us
    optimization_barrier x1, local copies, waits for them, and re-layouts, on_device(): lax.optimization_barrier((product, left_gathered, right_gathered))  6.51 us
    unnamed x19, local copies, waits for them, and re-layouts  6.39 us
    all_to_all x1, waiting for transfers between devices, gather_sides(): lax.all_to_all(left_pair, 'rows', split_axis=1, concat_axis=0, tiled=True)  5.41 us
    all_to_all x1, starting transfers between devices, send_back(): lax.all_to_all(product, ('branch', 'rows'), split_axis=0, concat_axis=0,...  5.21 us
  transfers between devices with their start and end apart: 6, of which 4 were waited for; matrix products, arithmetic and copies ran while one was open for 23% of the time, Pallas kernels for 10%

profile of v3, /device:TPU:1, one launch (start us, length us, event | category | flops | bytes accessed | tf_op | source)
XLA Modules:
  0.0 194.9 jit_solution(14543472658497923977)
XLA Ops:
  7.2 0.0 copy-start
  7.2 0.0 all-gather.2.cloned.1.call-start
  7.2 1.3 copy.38
  8.5 0.0 copy-start.6
  8.5 0.1 convert_reduce_fusion.1
  8.6 0.2 fusion.21
  8.8 0.0 copy-start.2
  8.8 0.0 copy-done
  8.8 3.3 %convert_reduce_fusion.2 = (f32[1024]{0:T(1024)S(1)}, bf16[1,1024,256]{1,2,0:T(8,128)(2,1)}) fusion(bf16[1024,256]{1,0:T(8,128)(2,1)S(1)} %copy-done, bf16[256,1024]{1,0:T(8,128)(2,1)} %param.12, bf16[1,1024,256]{1,2,0:T(8,128)(2,1)S(1)} %copy.38, f32[1024]{0:T(1024)S(1)} %add_rsqrt_fusion.2, f32[1024]{0:T(1024)S(1)} %broadcast_multiply_fusion.2), kind=kOutput, calls=%fused_computation.29 | convolution fusion | flops 1078197248 | bytes 2109440 | tf_op jit(solution)/shard_map/dot_general | solution.py:31
  12.1 1.2 fusion.23
  13.3 0.0 copy-done.6
  13.3 1.3 fusion.20
  14.7 2.2 %collective-permute-start = (bf16[1,1024,32]{1,2,0:T(8,128)(2,1)S(1)}, bf16[1,1024,32]{1,2,0:T(8,128)(2,1)S(1)}, u32[]{:S(2)}, u32[]{:S(2)}) collective-permute-start(bf16[1,1024,32]{1,2,0:T(8,128)(2,1)S(1)} %get-tuple-element.25), channel_id=1, source_target_pairs={{0,64},{64,0},{1,65},{65,1},{2,66},{66,2},{3,67},{67,3},{4,68},{68... | collective-permute-start | bytes 196616 | tf_op jit(solution)/shard_map/ppermute | solution.py:56
  16.9 0.0 copy-start.5
  16.9 0.1 collective-permute-start.1
  17.0 0.0 copy-done.2
  17.0 0.6 convert_reduce_fusion
  17.6 2.4 %fusion.2 = f32[16,512]{1,0:T(8,128)S(1)} fusion(bf16[16,512,128]{2,1,0:T(8,128)(2,1)S(1)} %copy-done.2, f32[16,512]{1,0:T(8,128)S(1)} %broadcast_multiply_fusion), kind=kLoop, calls=%fused_computation.5 | loop fusion | flops 4186112 | bytes 2162688 | tf_op jit(solution)/shard_map/reduce_sum | solution.py:12
  20.0 0.3 collective-permute-done.1
  20.4 0.6 fusion.37
  21.0 0.0 all-gather.2.cloned.1.call-update
  21.0 2.5 %fusion.3 = bf16[16,512,128]{2,1,0:T(8,128)(2,1)S(1)} fusion(bf16[16,512,128]{2,1,0:T(8,128)(2,1)S(1)} %copy-done.2, f32[16,512]{1,0:T(8,128)S(1)} %add_rsqrt_fusion, f32[16,512]{1,0:T(8,128)S(1)} %broadcast_multiply_fusion), kind=kLoop, calls=%fused_computation.6 | loop fusion | flops 4194304 | bytes 4259840 | tf_op jit(solution)/shard_map/convert_element_type | solution.py:82
  23.5 0.0 copy-done.5
  23.5 2.3 %convolution_bitcast_fusion = f32[512,8192]{0,1:T(8,128)S(1)} fusion(bf16[8192,128]{1,0:T(8,128)(2,1)S(1)} %bitcast.64, bf16[128,640]{1,0:T(8,128)(2,1)S(1)} %copy-done.5), kind=kOutput, calls=%fused_computation | convolution fusion | flops 1073741824 | bytes 19005440 | tf_op jit(solution)/shard_map/dot_general | solution.py:84
  25.8 3.2 %fusion.8 = (bf16[128,8192]{0,1:T(8,128)(2,1)S(1)}, bf16[128,8192]{0,1:T(8,128)(2,1)}) fusion(f32[512,8192]{0,1:T(8,128)S(1)} %convolution_bitcast_fusion), kind=kLoop, calls=%fused_computation.14 | loop fusion | flops 10485760 | bytes 20971520 | tf_op jit(solution)/shard_map/convert_element_type | solution.py:91
  29.0 4.6 %copy.40 = bf16[128,1,16,512]{3,2,1,0:T(8,128)(2,1)} copy(bf16[128,1,16,512]{0,3,2,1:T(8,128)(2,1)} %bitcast.66) | data formatting | bytes 4194304 | tf_op jit(solution)/shard_map/convert_element_type | solution.py:94
  33.6 2.9 %copy.39 = bf16[128,1,16,512]{3,2,1,0:T(8,128)(2,1)} copy(bf16[128,1,16,512]{0,3,2,1:T(8,128)(2,1)S(1)} %bitcast.65) | data formatting | bytes 4194304 | tf_op jit(solution)/shard_map/convert_element_type | solution.py:91
  36.5 0.0 collective-permute-done
  36.6 0.4 copy.43
  36.9 1.1 reshape.188
  38.0 12.2 %all-to-all-start.1 = ((bf16[64,2,512]{2,1,0:T(2,128)(2,1)}), bf16[64,2,512]{2,1,0:T(2,128)(2,1)S(1)}, u32[]{:S(2)}, u32[]{:S(2)}) async-start(bf16[64,2,512]{2,1,0:T(2,128)(2,1)} %reshape.188), calls=%async_computation.1 | async-start | bytes 262144 | tf_op jit(solution)/shard_map/all_to_all | solution.py:57
  50.2 4.6 %pad_maximum_fusion = bf16[128,2,16,512]{3,2,1,0:T(8,128)(2,1)} fusion(bf16[128,1,16,512]{3,2,1,0:T(8,128)(2,1)} %copy.40, bf16[128,1,16,512]{3,2,1,0:T(8,128)(2,1)} %copy.39), kind=kLoop, calls=%fused_computation.19 | loop fusion | flops 2097152 | bytes 8388608 | tf_op jit(solution)/shard_map/stack | solution.py:70
  54.8 5.4 %all-to-all-done.1 = bf16[64,2,512]{2,1,0:T(2,128)(2,1)S(1)} async-done(((bf16[64,2,512]{2,1,0:T(2,128)(2,1)}), bf16[64,2,512]{2,1,0:T(2,128)(2,1)S(1)}, u32[]{:S(2)}, u32[]{:S(2)}) %all-to-all-start.1) | async-done | bytes 131104 | tf_op jit(solution)/shard_map/all_to_all | solution.py:57
  60.2 5.0 %all-to-all-start = ((bf16[128,2,16,512]{3,2,1,0:T(8,128)(2,1)}), bf16[128,2,16,512]{3,2,1,0:T(8,128)(2,1)}, u32[]{:S(2)}, u32[]{:S(2)}) async-start(bf16[128,2,16,512]{3,2,1,0:T(8,128)(2,1)} %pad_maximum_fusion), calls=%async_computation | async-start | bytes 8388608 | tf_op jit(solution)/shard_map/all_to_all | solution.py:69
  65.1 0.3 reshape.189
  65.4 0.1 copy.44
  65.6 56.4 %all-to-all-done = bf16[128,2,16,512]{3,2,1,0:T(8,128)(2,1)} async-done(((bf16[128,2,16,512]{3,2,1,0:T(8,128)(2,1)}), bf16[128,2,16,512]{3,2,1,0:T(8,128)(2,1)}, u32[]{:S(2)}, u32[]{:S(2)}) %all-to-all-start) | async-done | bytes 4194336 | tf_op jit(solution)/shard_map/all_to_all | solution.py:69
  121.9 2.8 %fusion.39 = (bf16[128,1,16,512]{3,2,1,0:T(8,128)(2,1)S(1)}, bf16[128,1,16,512]{3,2,1,0:T(8,128)(2,1)S(1)}) fusion(bf16[128,2,16,512]{3,2,1,0:T(8,128)(2,1)} %all-to-all-done), kind=kLoop, calls=%fused_computation.60 | loop fusion | bytes 8388608 | tf_op jit(solution)/shard_map/slice | solution.py:72
  124.7 2.4 %fusion.12 = bf16[2,1024,512]{1,2,0:T(8,128)(2,1)S(1)} fusion(bf16[2,2,512,512]{3,2,1,0:T(8,128)(2,1)S(1)} %bitcast.74, bf16[2,1024,512,1]{2,1,3,0:T(8,128)(2,1)S(1)} %bitcast.73), kind=kOutput, calls=%fused_computation.22 | convolution fusion | flops 2148532224 | bytes 6291456 | tf_op jit(solution)/shard_map/bik,bhjk->hij/dot_general | solution.py:106
  127.1 0.0 copy-start.3
  127.1 0.0 copy-start.4
  127.1 2.6 %copy.42 = bf16[2,1024,512]{2,1,0:T(8,128)(2,1)} copy(bf16[2,1024,512]{1,2,0:T(8,128)(2,1)S(1)} %fusion.12) | data formatting | bytes 4194304 | tf_op jit(solution)/shard_map/convert_element_type | solution.py:108
  129.7 3.0 %all-gather.2.cloned.1.call-done = bf16[32,128,512]{2,0,1:T(8,128)(2,1)} async-done(((bf16[32,2,512]{2,0,1:T(8,128)(2,1)}), bf16[32,128,512]{2,0,1:T(8,128)(2,1)}) %all-gather.2.cloned.1.call-update) | async-done | bytes 4194320 | tf_op jit(solution)/shard_map/all_gather | solution.py:63
  132.7 5.2 %all-to-all-start.2 = ((bf16[128,16,512]{2,1,0:T(8,128)(2,1)}), bf16[128,16,512]{2,1,0:T(8,128)(2,1)S(1)}, u32[]{:S(2)}, u32[]{:S(2)}) async-start(bf16[128,16,512]{2,1,0:T(8,128)(2,1)} %bitcast.12), calls=%async_computation.2 | async-start | bytes 4194304 | tf_op jit(solution)/shard_map/all_to_all | solution.py:76
  137.9 0.0 copy-done.3
  137.9 1.0 copy.50
  138.9 1.4 slice.51.wg_ref
  140.3 0.0 copy-done.4
  140.3 0.1 copy.47
  140.4 0.9 copy.48
  141.3 1.1 copy.46
  142.4 6.5 %copy.49.r_ref = bf16[32,128,512]{2,1,0:T(8,128)(2,1)} copy(bf16[32,128,512]{2,0,1:T(8,128)(2,1)} %all-gather.2.cloned.1.call-done) | data formatting | bytes 8388608 | tf_op jit(solution)/shard_map/optimization_barrier | solution.py:245
  148.9 19.9 %shard_map.113.outer_ref = f32[16,512,128]{2,1,0:T(8,128)} custom-call(bf16[512,128]{1,0:T(8,128)(2,1)} %bitcast.78, bf16[32,128,512]{2,1,0:T(8,128)(2,1)} %copy.49.r_ref, bf16[128,1024]{1,0:T(8,128)(2,1)} %bitcast.77), custom_call_target="tpu_custom_call" | custom-call | flops 4294967296 | bytes 8388608 | tf_op jit(solution)/shard_map/pallas_call | solution.py:210
  168.8 0.0 all-to-all-done.2
  168.8 2.7 %copy.53 = bf16[16,8,16,512]{3,1,2,0:T(8,128)(2,1)} copy(bf16[16,8,16,512]{3,2,1,0:T(8,128)(2,1)S(1)} %bitcast.67) | data formatting | bytes 4194304
  171.5 0.0 copy-start.1
  171.5 16.6 %shard_map.114 = bf16[16,512,128]{2,1,0:T(8,128)(2,1)} custom-call(bf16[128,8192]{1,0:T(8,128)(2,1)} %bitcast.71, bf16[16,512,128]{2,1,0:T(8,128)(2,1)} %pair_ref, f32[16,512,128]{2,1,0:T(8,128)} %shard_map.113.outer_ref, bf16[128,128]{1,0:T(8,128)(2,1)} %wo_ref.1, bf16[128,128]{1,0:T(8,128)(2,1)} %slice.51.wg_ref, bf16[128,512]{1,0:T(8,128)(2,1)} %wu_ref.1, ...), custom_call_target="tpu_custom_call" | custom-call | flops 2952790016 | bytes 10485760 | tf_op jit(solution)/shard_map/pallas_call | solution.py:148
  188.1 0.0 copy-done.1
  (10 shorter events, 0.1 us)
Async XLA Ops:
  7.2 1.7 copy-start
  7.2 125.5 %all-gather.2.cloned.1.call-start = ((), (), s32[]{:S(2)}) async-start(), calls=%async_computation.3 | async-start | bytes 4259840 | tf_op jit(solution)/shard_map/all_gather | solution.py:63
  8.5 4.8 %copy-start.6 = (bf16[256,64]{0,1:T(8,128)(2,1)S(1)}, bf16[256,64]{0,1:T(8,128)(2,1)}, u32[]{:S(2)}) copy-start(bf16[256,64]{0,1:T(8,128)(2,1)} %param.14) | copy-start | bytes 98308
  8.8 8.2 %copy-start.2 = (bf16[16,512,128]{2,1,0:T(8,128)(2,1)S(1)}, bf16[16,512,128]{2,1,0:T(8,128)(2,1)}, u32[]{:S(2)}) copy-start(bf16[16,512,128]{2,1,0:T(8,128)(2,1)} %pair_ref) | copy-start | bytes 6291460
  14.7 21.9 %collective-permute-start = (bf16[1,1024,32]{1,2,0:T(8,128)(2,1)S(1)}, bf16[1,1024,32]{1,2,0:T(8,128)(2,1)S(1)}, u32[]{:S(2)}, u32[]{:S(2)}) collective-permute-start(bf16[1,1024,32]{1,2,0:T(8,128)(2,1)S(1)} %get-tuple-element.25), channel_id=1, source_target_pairs={{0,64},{64,0},{1,65},{65,1},{2,66},{66,2},{3,67},{67,3},{4,68},{68... | collective-permute-start | bytes 196616 | tf_op jit(solution)/shard_map/ppermute | solution.py:56
  16.9 6.6 %copy-start.5 = (bf16[128,640]{1,0:T(8,128)(2,1)S(1)}, bf16[128,640]{1,0:T(8,128)(2,1)}, u32[]{:S(2)}) copy-start(bf16[128,640]{1,0:T(8,128)(2,1)} %param.16) | copy-start | bytes 491524
  16.9 3.5 %collective-permute-start.1 = (bf16[1,32,512]{2,1,0:T(8,128)(2,1)S(1)}, bf16[1,32,512]{2,1,0:T(8,128)(2,1)S(1)}, u32[]{:S(2)}, u32[]{:S(2)}) collective-permute-start(bf16[1,32,512]{2,1,0:T(8,128)(2,1)S(1)} %get-tuple-element.27), channel_id=1, source_target_pairs={{0,64},{64,0},{1,65},{65,1},{2,66},{66,2},{3,67},{67,3},{4,68},{68... | collective-permute-start | bytes 98312 | tf_op jit(solution)/shard_map/ppermute | solution.py:62
  38.0 22.2 %all-to-all-start.1 = ((bf16[64,2,512]{2,1,0:T(2,128)(2,1)}), bf16[64,2,512]{2,1,0:T(2,128)(2,1)S(1)}, u32[]{:S(2)}, u32[]{:S(2)}) async-start(bf16[64,2,512]{2,1,0:T(2,128)(2,1)} %reshape.188), calls=%async_computation.1 | async-start | bytes 262144 | tf_op jit(solution)/shard_map/all_to_all | solution.py:57
  60.2 61.7 %all-to-all-start = ((bf16[128,2,16,512]{3,2,1,0:T(8,128)(2,1)}), bf16[128,2,16,512]{3,2,1,0:T(8,128)(2,1)}, u32[]{:S(2)}, u32[]{:S(2)}) async-start(bf16[128,2,16,512]{3,2,1,0:T(8,128)(2,1)} %pad_maximum_fusion), calls=%async_computation | async-start | bytes 8388608 | tf_op jit(solution)/shard_map/all_to_all | solution.py:69
  127.1 10.8 %copy-start.3 = (bf16[1,1024,256]{1,2,0:T(8,128)(2,1)S(1)}, bf16[1,1024,256]{1,2,0:T(8,128)(2,1)}, u32[]{:S(2)}) copy-start(bf16[1,1024,256]{1,2,0:T(8,128)(2,1)} %get-tuple-element.29) | copy-start | bytes 1572868
  127.1 13.2 %copy-start.4 = (bf16[1024,128]{1,0:T(8,128)(2,1)S(1)}, bf16[1024,128]{1,0:T(8,128)(2,1)}, u32[]{:S(2)}) copy-start(bf16[1024,128]{1,0:T(8,128)(2,1)} %param.15) | copy-start | bytes 786436
  132.7 36.0 %all-to-all-start.2 = ((bf16[128,16,512]{2,1,0:T(8,128)(2,1)}), bf16[128,16,512]{2,1,0:T(8,128)(2,1)S(1)}, u32[]{:S(2)}, u32[]{:S(2)}) async-start(bf16[128,16,512]{2,1,0:T(8,128)(2,1)} %bitcast.12), calls=%async_computation.2 | async-start | bytes 4194304 | tf_op jit(solution)/shard_map/all_to_all | solution.py:76
  171.5 16.6 %copy-start.1 = (bf16[1024,256]{1,0:T(8,128)(2,1)S(1)}, bf16[1024,256]{1,0:T(8,128)(2,1)}, u32[]{:S(2)}) copy-start(bf16[1024,256]{1,0:T(8,128)(2,1)} %param.13) | copy-start | bytes 1572868
Sparse Core Ops, SparseCore 0:
  21.1 111.5 all-gather.1

commit v4 on v3

--- a/solution.py
+++ b/solution.py
@@ -76,25 +76,47 @@
     return lax.all_to_all(product, ("branch", "rows"), split_axis=0, concat_axis=0, tiled=True)
 
 
+def front_kernel(pair_ref, wt_ref, left_ref, right_ref):
+    rows, columns, chans = pair_ref.shape
+    for r in range(rows):
+        pair_norm = standardize_features(pair_ref[r].astype(jnp.float32), -1).astype(jnp.bfloat16)
+        proj = lax.dot_general(
+            wt_ref[...], pair_norm, (((1,), (1,)), ((), ())), preferred_element_type=jnp.float32
+        )
+        cols = slice(r * columns, (r + 1) * columns)
+        left_ref[:, cols] = (
+            jax.nn.sigmoid(proj[chans : 2 * chans]) * proj[:chans]
+        ).astype(left_ref.dtype)
+        right_ref[:, cols] = (
+            jax.nn.sigmoid(proj[3 * chans :]) * proj[2 * chans : 3 * chans]
+        ).astype(right_ref.dtype)
+
+
 def pair_front(pairwise_input, triangle_projection_weight):
     tile_rows, columns, chans = pairwise_input.shape
-    pair_float = pairwise_input.astype(jnp.float32)
-    pair_norm = standardize_features(pair_float, -1).astype(jnp.bfloat16)
-    norm_flat = pair_norm.reshape(tile_rows * columns, chans)
-    proj_flat = lax.dot_general(
-        triangle_projection_weight[:, : 4 * chans],
-        norm_flat,
-        (((0,), (1,)), ((), ())),
-        preferred_element_type=jnp.float32,
-    )
-    proj_tile = proj_flat.reshape(4 * chans, tile_rows, columns)
-    tri_left = (jax.nn.sigmoid(proj_tile[chans : 2 * chans]) * proj_tile[:chans]).astype(
-        jnp.bfloat16
-    )
-    tri_right = (jax.nn.sigmoid(proj_tile[3 * chans :]) * proj_tile[2 * chans : 3 * chans]).astype(
-        jnp.bfloat16
-    )
-    return tri_left, tri_right
+    step_rows = 4
+    weight_t = triangle_projection_weight[:, : 4 * chans].T
+    side = jax.ShapeDtypeStruct((chans, tile_rows * columns), jnp.bfloat16)
+    out_block = pl.BlockSpec((chans, step_rows * columns), lambda g: (0, g))
+    tri_left, tri_right = pl.pallas_call(
+        front_kernel,
+        out_shape=(side, side),
+        grid=(tile_rows // step_rows,),
+        in_specs=[
+            pl.BlockSpec((step_rows, columns, chans), lambda g: (g, 0, 0)),
+            pl.BlockSpec((4 * chans, chans), lambda g: (0, 0)),
+        ],
+        out_specs=(out_block, out_block),
+        cost_estimate=pl.CostEstimate(
+            flops=2 * tile_rows * columns * chans * 4 * chans,
+            transcendentals=2 * tile_rows * columns * chans,
+            bytes_accessed=tile_rows * columns * chans * 6,
+        ),
+    )(pairwise_input, weight_t)
+    return (
+        tri_left.reshape(chans, tile_rows, columns),
+        tri_right.reshape(chans, tile_rows, columns),
+    )
 
 
 def triangle_product(left_chan, right_chan):

time: 196 us -> 189 us (0.964)
  other arithmetic: 15.4 us -> 5.03 us
  Pallas kernels: 36.5 us -> 43 us
  matrix products: 9.27 us -> 3.95 us
  waiting for transfers between devices: 65.1 us -> 67.9 us
    convert_element_type x2 -> x0, local copies, waits for them, and re-layouts: 7.5 us -> none  [the longest x1 4.61 us: pair_front(): (jax.nn.sigmoid(proj_tile[3 * chans:]) * proj_tile[2 * chans:3 * chans])....]
    pallas_call x0 -> x1, Pallas kernels: none -> 6.54 us  [pair_front(): pl.pallas_call(front_kernel, out_shape=(side, side), grid=(tile_rows // s...]
    unnamed x19 -> x20, local copies, waits for them, and re-layouts: 6.39 us -> 12.9 us
    convert_element_type x2 -> x0, other arithmetic: 5.67 us -> none  [the longest x1 3.19 us: pair_front(): (jax.nn.sigmoid(proj_tile[chans:2 * chans]) * proj_tile[:chans]).astype(j...]
    reduce_sum x3 -> x2, other arithmetic: 3.73 us -> 0.32 us  [standardize_features(): variance = jnp.mean(centered * centered, axis=dimension, keepdims=True)]
    dot_general x1 -> x0, matrix products: 2.32 us -> none  [pair_front(): lax.dot_general(triangle_projection_weight[:, :4 * chans], norm_flat, (((...]
    ppermute x1, starting transfers between devices: 0.12 us -> 2.2 us  [gather_sides(): right_pair = branch_pair(keep, lax.ppermute(send, 'branch', swap))]
  transfers between devices with their start and end apart: 6 -> 6, of which waited for: 4 -> 4; matrix products, arithmetic and copies ran while one was open for 23% -> 16% of each run, Pallas kernels for 10% -> 14%
where the time goes in v4:
time: 189 us
  waiting for transfers between devices  67.9 us (36%)
  Pallas kernels  43 us (23%)
  local copies, waits for them, and re-layouts  28.8 us (15%)
  starting transfers between devices  25.8 us (14%)
  between operations  14.2 us (8%)
  other arithmetic  5.03 us (3%)
  matrix products  3.95 us (2%)
    all_to_all x1, waiting for transfers between devices, send_whole(): lax.all_to_all(jnp.stack([tri_left, tri_right], axis=1), both, split_axis...  55.7 us
    pallas_call x1, Pallas kernels, outer_product(): pl.pallas_call(outer_kernel, out_shape=jax.ShapeDtypeStruct((tile_rows, c...  19.9 us
    pallas_call x1, Pallas kernels, pair_back(): pl.pallas_call(back_kernel, out_shape=jax.ShapeDtypeStruct((tile_rows, co...  16.6 us
    unnamed x20, local copies, waits for them, and re-layouts  12.9 us
    all_to_all x1, starting transfers between devices, gather_sides(): lax.all_to_all(left_pair, 'rows', split_axis=1, concat_axis=0, tiled=True)  12.8 us
    pallas_call x1, Pallas kernels, pair_front(): pl.pallas_call(front_kernel, out_shape=(side, side), grid=(tile_rows // s...  6.54 us
    optimization_barrier x1, local copies, waits for them, and re-layouts, on_device(): lax.optimization_barrier((product, left_gathered, right_gathered))  6.49 us
    all_to_all x1, waiting for transfers between devices, gather_sides(): lax.all_to_all(left_pair, 'rows', split_axis=1, concat_axis=0, tiled=True)  6.06 us
  transfers between devices with their start and end apart: 6, of which 4 were waited for; matrix products, arithmetic and copies ran while one was open for 16% of the time, Pallas kernels for 14%

profile of v4, /device:TPU:1, one launch (start us, length us, event | category | flops | bytes accessed | tf_op | source)
XLA Modules:
  0.0 188.8 jit_solution(7686474318473893991)
XLA Ops:
  7.2 0.0 copy-start
  7.2 0.0 copy-start.4
  7.2 0.0 all-gather.2.cloned.1.call-start
  7.2 1.3 copy.36
  8.6 0.1 convert_reduce_fusion
  8.7 0.2 fusion.9
  8.8 0.0 copy-done
  8.9 0.0 copy-done.4
  8.9 0.0 copy-start.5
  8.9 1.3 convert_reduce_fusion.1
  10.2 0.0 copy-start.2
  10.2 0.0 slice-start
  10.2 0.2 fusion.11
  10.4 0.0 copy-done.5
  10.4 0.3 fusion.8
  10.7 2.2 %collective-permute-start.1 = (bf16[1,32,512]{2,1,0:T(8,128)(2,1)S(1)}, bf16[1,32,512]{2,1,0:T(8,128)(2,1)S(1)}, u32[]{:S(2)}, u32[]{:S(2)}) collective-permute-start(bf16[1,32,512]{2,1,0:T(8,128)(2,1)S(1)} %get-tuple-element.29), channel_id=1, source_target_pairs={{0,64},{64,0},{1,65},{65,1},{2,66},{66,2},{3,67},{67,3},{4,68},{68... | collective-permute-start | bytes 98312 | tf_op jit(solution)/shard_map/ppermute | solution.py:62
  12.9 1.3 collective-permute-done.1
  14.2 0.6 fusion.24
  14.9 0.0 all-gather.2.cloned.1.call-update
  14.9 1.5 collective-permute-start
  16.4 0.0 slice-done
  16.4 0.8 copy.51
  17.2 6.5 %shard_map.113 = (bf16[128,8192]{1,0:T(8,128)(2,1)}, bf16[128,8192]{1,0:T(8,128)(2,1)}) custom-call(bf16[16,512,128]{2,1,0:T(8,128)(2,1)} %pair_ref.1, bf16[512,128]{1,0:T(8,128)(2,1)} %bitcast.87), custom_call_target="tpu_custom_call" | custom-call | flops 1073741824 | bytes 6291456 | tf_op jit(solution)/shard_map/pallas_call | solution.py:101
  23.8 0.0 copy-done.2
  23.8 0.0 copy-start.1
  23.8 2.6 %copy.54 = bf16[16,8,16,512]{3,2,1,0:T(8,128)(2,1)S(1)} copy(bf16[16,8,16,512]{3,1,2,0:T(8,128)(2,1)} %bitcast.78) | data formatting | bytes 4194304
  26.3 0.0 copy-done.1
  26.3 2.1 %copy.53 = bf16[16,8,16,512]{3,2,1,0:T(8,128)(2,1)} copy(bf16[16,8,16,512]{3,1,2,0:T(8,128)(2,1)S(1)} %bitcast.77) | data formatting | bytes 4194304
  28.5 0.0 collective-permute-done
  28.5 0.4 copy.42
  28.9 1.1 reshape.87
  30.0 12.8 %all-to-all-start.1 = ((bf16[64,2,512]{2,1,0:T(2,128)(2,1)}), bf16[64,2,512]{2,1,0:T(2,128)(2,1)S(1)}, u32[]{:S(2)}, u32[]{:S(2)}) async-start(bf16[64,2,512]{2,1,0:T(2,128)(2,1)} %reshape.87), calls=%async_computation.1 | async-start | bytes 262144 | tf_op jit(solution)/shard_map/all_to_all | solution.py:57
  42.8 3.9 %pad_maximum_fusion = bf16[128,2,16,512]{3,2,1,0:T(8,128)(2,1)} fusion(bf16[128,1,16,512]{3,2,1,0:T(8,128)(2,1)S(1)} %bitcast.72, bf16[128,1,16,512]{3,2,1,0:T(8,128)(2,1)} %bitcast.73), kind=kLoop, calls=%fused_computation | loop fusion | flops 2097152 | bytes 8388608 | tf_op jit(solution)/shard_map/stack | solution.py:70
  46.7 6.1 %all-to-all-done.1 = bf16[64,2,512]{2,1,0:T(2,128)(2,1)S(1)} async-done(((bf16[64,2,512]{2,1,0:T(2,128)(2,1)}), bf16[64,2,512]{2,1,0:T(2,128)(2,1)S(1)}, u32[]{:S(2)}, u32[]{:S(2)}) %all-to-all-start.1) | async-done | bytes 131104 | tf_op jit(solution)/shard_map/all_to_all | solution.py:57
  52.8 5.0 %all-to-all-start = ((bf16[128,2,16,512]{3,2,1,0:T(8,128)(2,1)}), bf16[128,2,16,512]{3,2,1,0:T(8,128)(2,1)}, u32[]{:S(2)}, u32[]{:S(2)}) async-start(bf16[128,2,16,512]{3,2,1,0:T(8,128)(2,1)} %pad_maximum_fusion), calls=%async_computation | async-start | bytes 8388608 | tf_op jit(solution)/shard_map/all_to_all | solution.py:69
  57.7 0.3 reshape.88
  58.0 0.1 copy.43
  58.1 55.7 %all-to-all-done = bf16[128,2,16,512]{3,2,1,0:T(8,128)(2,1)} async-done(((bf16[128,2,16,512]{3,2,1,0:T(8,128)(2,1)}), bf16[128,2,16,512]{3,2,1,0:T(8,128)(2,1)}, u32[]{:S(2)}, u32[]{:S(2)}) %all-to-all-start) | async-done | bytes 4194336 | tf_op jit(solution)/shard_map/all_to_all | solution.py:69
  113.9 2.7 %fusion.26 = (bf16[128,1,16,512]{3,2,1,0:T(8,128)(2,1)S(1)}, bf16[128,1,16,512]{3,2,1,0:T(8,128)(2,1)S(1)}) fusion(bf16[128,2,16,512]{3,2,1,0:T(8,128)(2,1)} %all-to-all-done), kind=kLoop, calls=%fused_computation.38 | loop fusion | bytes 8388608 | tf_op jit(solution)/shard_map/slice | solution.py:72
  116.6 2.4 %fusion = bf16[2,1024,512]{1,2,0:T(8,128)(2,1)S(1)} fusion(bf16[2,2,512,512]{3,2,1,0:T(8,128)(2,1)S(1)} %bitcast.82, bf16[2,1024,512,1]{2,1,3,0:T(8,128)(2,1)S(1)} %bitcast.81), kind=kOutput, calls=%fused_computation.3 | convolution fusion | flops 2148532224 | bytes 6291456 | tf_op jit(solution)/shard_map/bik,bhjk->hij/dot_general | solution.py:128
  118.9 2.6 %copy.41 = bf16[2,1024,512]{2,1,0:T(8,128)(2,1)} copy(bf16[2,1024,512]{1,2,0:T(8,128)(2,1)S(1)} %fusion) | data formatting | bytes 4194304 | tf_op jit(solution)/shard_map/convert_element_type | solution.py:130
  121.5 4.8 %all-gather.2.cloned.1.call-done = bf16[32,128,512]{2,0,1:T(8,128)(2,1)} async-done(((bf16[32,2,512]{2,0,1:T(8,128)(2,1)}), bf16[32,128,512]{2,0,1:T(8,128)(2,1)}) %all-gather.2.cloned.1.call-update) | async-done | bytes 4194320 | tf_op jit(solution)/shard_map/all_gather | solution.py:63
  126.3 0.0 copy-start.3
  126.3 4.3 %all-to-all-start.2 = ((bf16[128,16,512]{2,1,0:T(8,128)(2,1)}), bf16[128,16,512]{2,1,0:T(8,128)(2,1)S(1)}, u32[]{:S(2)}, u32[]{:S(2)}) async-start(bf16[128,16,512]{2,1,0:T(8,128)(2,1)} %bitcast.11), calls=%async_computation.2 | async-start | bytes 4194304 | tf_op jit(solution)/shard_map/all_to_all | solution.py:76
  130.6 2.0 %copy.49 = bf16[1,1024,256]{2,1,0:T(8,128)(2,1)} copy(bf16[1,1024,256]{1,2,0:T(8,128)(2,1)} %copy-done.2) | data formatting | bytes 1048576
  132.6 0.0 copy-done.3
  132.6 0.6 slice.25.wg_ref
  133.2 1.1 copy.46
  134.3 0.9 copy.47
  135.1 1.1 copy.45
  136.2 6.5 %copy.48.r_ref = bf16[32,128,512]{2,1,0:T(8,128)(2,1)} copy(bf16[32,128,512]{2,0,1:T(8,128)(2,1)} %all-gather.2.cloned.1.call-done) | data formatting | bytes 8388608 | tf_op jit(solution)/shard_map/optimization_barrier | solution.py:267
  142.7 19.9 %shard_map.114.outer_ref = f32[16,512,128]{2,1,0:T(8,128)} custom-call(bf16[512,128]{1,0:T(8,128)(2,1)} %bitcast.86, bf16[32,128,512]{2,1,0:T(8,128)(2,1)} %copy.48.r_ref, bf16[128,1024]{1,0:T(8,128)(2,1)} %bitcast.85), custom_call_target="tpu_custom_call" | custom-call | flops 4294967296 | bytes 8388608 | tf_op jit(solution)/shard_map/pallas_call | solution.py:232
  162.7 0.0 all-to-all-done.2
  162.7 2.7 %copy.55 = bf16[16,8,16,512]{3,1,2,0:T(8,128)(2,1)} copy(bf16[16,8,16,512]{3,2,1,0:T(8,128)(2,1)S(1)} %bitcast.71) | data formatting | bytes 4194304
  165.4 16.6 %shard_map.115 = bf16[16,512,128]{2,1,0:T(8,128)(2,1)} custom-call(bf16[128,8192]{1,0:T(8,128)(2,1)} %bitcast.79, bf16[16,512,128]{2,1,0:T(8,128)(2,1)} %pair_ref.1, f32[16,512,128]{2,1,0:T(8,128)} %shard_map.114.outer_ref, bf16[128,128]{1,0:T(8,128)(2,1)} %wo_ref.1, bf16[128,128]{1,0:T(8,128)(2,1)} %slice.25.wg_ref, bf16[128,512]{1,0:T(8,128)(2,1)} %wu_ref.1, ...), custom_call_target="tpu_custom_call" | custom-call | flops 2952790016 | bytes 10485760 | tf_op jit(solution)/shard_map/pallas_call | solution.py:170
  (8 shorter events, 0.1 us)
Async XLA Ops:
  7.2 1.7 copy-start
  7.2 1.7 copy-start.4
  7.2 119.1 %all-gather.2.cloned.1.call-start = ((), (), s32[]{:S(2)}) async-start(), calls=%async_computation.3 | async-start | bytes 4259840 | tf_op jit(solution)/shard_map/all_gather | solution.py:63
  8.9 1.5 copy-start.5
  10.2 13.6 %copy-start.2 = (bf16[1,1024,256]{1,2,0:T(8,128)(2,1)}, bf16[1,1024,256]{1,2,0:T(8,128)(2,1)S(1)}, u32[]{:S(2)}) copy-start(bf16[1,1024,256]{1,2,0:T(8,128)(2,1)S(1)} %get-tuple-element.31) | copy-start | bytes 1572868
  10.2 6.2 %slice-start = ((bf16[128,640]{1,0:T(8,128)(2,1)}), bf16[128,512]{1,0:T(8,128)(2,1)S(1)}, s32[]{:S(2)}) async-start(bf16[128,640]{1,0:T(8,128)(2,1)} %param.16), calls=%async_computation.4 | async-start | bytes 262144 | tf_op jit(solution)/shard_map/slice | solution.py:98
  10.7 3.5 %collective-permute-start.1 = (bf16[1,32,512]{2,1,0:T(8,128)(2,1)S(1)}, bf16[1,32,512]{2,1,0:T(8,128)(2,1)S(1)}, u32[]{:S(2)}, u32[]{:S(2)}) collective-permute-start(bf16[1,32,512]{2,1,0:T(8,128)(2,1)S(1)} %get-tuple-element.29), channel_id=1, source_target_pairs={{0,64},{64,0},{1,65},{65,1},{2,66},{66,2},{3,67},{67,3},{4,68},{68... | collective-permute-start | bytes 98312 | tf_op jit(solution)/shard_map/ppermute | solution.py:62
  14.9 13.6 %collective-permute-start = (bf16[1,1024,32]{1,2,0:T(8,128)(2,1)S(1)}, bf16[1,1024,32]{1,2,0:T(8,128)(2,1)S(1)}, u32[]{:S(2)}, u32[]{:S(2)}) collective-permute-start(bf16[1,1024,32]{1,2,0:T(8,128)(2,1)S(1)} %get-tuple-element.27), channel_id=1, source_target_pairs={{0,64},{64,0},{1,65},{65,1},{2,66},{66,2},{3,67},{67,3},{4,68},{68... | collective-permute-start | bytes 196616 | tf_op jit(solution)/shard_map/ppermute | solution.py:56
  23.8 2.6 %copy-start.1 = (bf16[128,8192]{1,0:T(8,128)(2,1)S(1)}, bf16[128,8192]{1,0:T(8,128)(2,1)}, u32[]{:S(2)}) copy-start(bf16[128,8192]{1,0:T(8,128)(2,1)} %get-tuple-element.9) | copy-start | bytes 6291460
  30.0 22.8 %all-to-all-start.1 = ((bf16[64,2,512]{2,1,0:T(2,128)(2,1)}), bf16[64,2,512]{2,1,0:T(2,128)(2,1)S(1)}, u32[]{:S(2)}, u32[]{:S(2)}) async-start(bf16[64,2,512]{2,1,0:T(2,128)(2,1)} %reshape.87), calls=%async_computation.1 | async-start | bytes 262144 | tf_op jit(solution)/shard_map/all_to_all | solution.py:57
  52.8 61.1 %all-to-all-start = ((bf16[128,2,16,512]{3,2,1,0:T(8,128)(2,1)}), bf16[128,2,16,512]{3,2,1,0:T(8,128)(2,1)}, u32[]{:S(2)}, u32[]{:S(2)}) async-start(bf16[128,2,16,512]{3,2,1,0:T(8,128)(2,1)} %pad_maximum_fusion), calls=%async_computation | async-start | bytes 8388608 | tf_op jit(solution)/shard_map/all_to_all | solution.py:69
  126.3 6.3 %copy-start.3 = (bf16[128,640]{1,0:T(8,128)(2,1)S(1)}, bf16[128,640]{1,0:T(8,128)(2,1)}, u32[]{:S(2)}) copy-start(bf16[128,640]{1,0:T(8,128)(2,1)} %param.16) | copy-start | bytes 491524
  126.3 36.4 %all-to-all-start.2 = ((bf16[128,16,512]{2,1,0:T(8,128)(2,1)}), bf16[128,16,512]{2,1,0:T(8,128)(2,1)S(1)}, u32[]{:S(2)}, u32[]{:S(2)}) async-start(bf16[128,16,512]{2,1,0:T(8,128)(2,1)} %bitcast.11), calls=%async_computation.2 | async-start | bytes 4194304 | tf_op jit(solution)/shard_map/all_to_all | solution.py:76
Sparse Core Ops, SparseCore 0:
  15.0 111.2 all-gather.1

commit v5 on v4

--- a/solution.py
+++ b/solution.py
@@ -69,7 +69,7 @@
     moved = lax.all_to_all(
         jnp.stack([tri_left, tri_right], axis=1), both, split_axis=0, concat_axis=0, tiled=True
     )
-    return moved[:, 0], moved[:, 1]
+    return moved
 
 
 def send_back(product):
@@ -119,15 +119,41 @@
     )
 
 
-def triangle_product(left_chan, right_chan):
+def product_kernel(moved_ref, out_ref):
+    halves, span, columns = out_ref.shape
+    n_src, _, tile_rows, _ = moved_ref.shape
+    per_half = n_src // halves
+    per_out = per_half // halves
+    for h in range(halves):
+        total = None
+        for b in range(halves):
+            left = moved_ref[b * per_half : (b + 1) * per_half, 0]
+            first = b * per_half + h * per_out
+            right = moved_ref[first : first + per_out, 1]
+            part = lax.dot_general(
+                left.reshape(per_half * tile_rows, columns),
+                right.reshape(per_out * tile_rows, columns),
+                (((1,), (1,)), ((), ())),
+                preferred_element_type=jnp.float32,
+            )
+            total = part if total is None else total + part
+        out_ref[h] = total.astype(out_ref.dtype)
+
+
+def triangle_product(moved):
+    n_src, _, tile_rows, columns = moved.shape
     halves = lax.axis_size("branch")
-    columns = left_chan.shape[-1]
-    tile_rows = left_chan.shape[1]
-    left_src = left_chan.reshape(halves, -1, columns)
-    right_src = right_chan.reshape(halves, halves, -1, columns)
-    product = jnp.einsum(
-        "bik,bhjk->hij", left_src, right_src, preferred_element_type=jnp.float32
-    ).astype(jnp.bfloat16)
+    product = pl.pallas_call(
+        product_kernel,
+        out_shape=jax.ShapeDtypeStruct((halves, n_src * tile_rows // halves, columns), jnp.bfloat16),
+        in_specs=[pl.BlockSpec(memory_space=pltpu.VMEM)],
+        out_specs=pl.BlockSpec(memory_space=pltpu.VMEM),
+        cost_estimate=pl.CostEstimate(
+            flops=2 * (n_src * tile_rows) ** 2 * columns // halves,
+            transcendentals=0,
+            bytes_accessed=moved.size * 2 + n_src * tile_rows * columns * 2,
+        ),
+    )(moved)
     return product.reshape(-1, tile_rows, columns)
 
 
@@ -262,8 +288,8 @@
     tri_left, tri_right = pair_front(
         pairwise_input, triangle_projection_weight
     )
-    left_chan, right_chan = send_whole(tri_left, tri_right)
-    product = triangle_product(left_chan, right_chan)
+    moved = send_whole(tri_left, tri_right)
+    product = triangle_product(moved)
     product, left_gathered, right_gathered = lax.optimization_barrier(
         (product, left_gathered, right_gathered)
     )

time: 189 us -> 189 us (level)
  Pallas kernels: 43 us -> 48.9 us
  local copies, waits for them, and re-layouts: 28.8 us -> 23.6 us
  matrix products: 3.95 us -> 1.59 us
    pallas_call x0 -> x1, Pallas kernels: none -> 5.87 us  [triangle_product(): pl.pallas_call(product_kernel, out_shape=jax.ShapeDtypeStruct((halves, n_...]
    slice x1 -> x0, local copies, waits for them, and re-layouts: 2.69 us -> none  [send_whole(): return (moved[:, 0], moved[:, 1])]
    convert_element_type x1 -> x0, local copies, waits for them, and re-layouts: 2.56 us -> none  [triangle_product(): product = jnp.einsum('bik,bhjk->hij', left_src, right_src, preferred_elem...]
    dot_general x1 -> x0, matrix products: 2.36 us -> none  [triangle_product(): jnp.einsum('bik,bhjk->hij', left_src, right_src, preferred_element_type=j...]
  transfers between devices with their start and end apart: 6 -> 6, of which waited for: 4 -> 4; matrix products, arithmetic and copies ran while one was open for 16% -> 12% of each run, Pallas kernels for 14% -> 17%
where the time goes in v5:
time: 189 us
  waiting for transfers between devices  69.5 us (37%)
  Pallas kernels  48.9 us (26%)
  starting transfers between devices  26 us (14%)
  local copies, waits for them, and re-layouts  23.6 us (12%)
  between operations  14.2 us (8%)
  other arithmetic  5.03 us (3%)
    all_to_all x1, waiting for transfers between devices, send_whole(): lax.all_to_all(jnp.stack([tri_left, tri_right], axis=1), both, split_axis...  55.7 us
    pallas_call x1, Pallas kernels, outer_product(): pl.pallas_call(outer_kernel, out_shape=jax.ShapeDtypeStruct((tile_rows, c...  19.9 us
    pallas_call x1, Pallas kernels, pair_back(): pl.pallas_call(back_kernel, out_shape=jax.ShapeDtypeStruct((tile_rows, co...  16.6 us
    unnamed x20, local copies, waits for them, and re-layouts  12.9 us
    all_to_all x1, starting transfers between devices, gather_sides(): lax.all_to_all(left_pair, 'rows', split_axis=1, concat_axis=0, tiled=True)  12.8 us
    pallas_call x1, Pallas kernels, pair_front(): pl.pallas_call(front_kernel, out_shape=(side, side), grid=(tile_rows // s...  6.53 us
    optimization_barrier x1, local copies, waits for them, and re-layouts, on_device(): lax.optimization_barrier((product, left_gathered, right_gathered))  6.49 us
    all_gather x1, waiting for transfers between devices, gather_sides(): lax.all_gather(jnp.swapaxes(right_pair, 0, 1), 'rows', axis=1, tiled=True)  6.46 us
  transfers between devices with their start and end apart: 6, of which 4 were waited for; matrix products, arithmetic and copies ran while one was open for 12% of the time, Pallas kernels for 17%

profile of v5, /device:TPU:1, one launch (start us, length us, event | category | flops | bytes accessed | tf_op | source)
XLA Modules:
  0.0 188.8 jit_solution(16971029739528204813)
XLA Ops:
  7.2 0.0 copy-start
  7.2 0.0 copy-start.4
  7.2 0.0 all-gather.2.cloned.1.call-start
  7.2 1.3 copy.33
  8.6 0.1 convert_reduce_fusion
  8.7 0.2 fusion.8
  8.8 0.0 copy-done
  8.9 0.0 copy-done.4
  8.9 0.0 copy-start.5
  8.9 1.3 convert_reduce_fusion.1
  10.2 0.0 copy-start.2
  10.2 0.0 slice-start
  10.2 0.2 fusion.10
  10.4 0.0 copy-done.5
  10.4 0.3 fusion.7
  10.7 2.2 %collective-permute-start.1 = (bf16[1,32,512]{2,1,0:T(8,128)(2,1)S(1)}, bf16[1,32,512]{2,1,0:T(8,128)(2,1)S(1)}, u32[]{:S(2)}, u32[]{:S(2)}) collective-permute-start(bf16[1,32,512]{2,1,0:T(8,128)(2,1)S(1)} %get-tuple-element.27), channel_id=1, source_target_pairs={{0,64},{64,0},{1,65},{65,1},{2,66},{66,2},{3,67},{67,3},{4,68},{68... | collective-permute-start | bytes 98312 | tf_op jit(solution)/shard_map/ppermute | solution.py:62
  12.9 1.3 collective-permute-done.1
  14.2 0.6 fusion.23
  14.9 0.0 all-gather.2.cloned.1.call-update
  14.9 1.5 collective-permute-start
  16.4 0.0 slice-done
  16.4 0.8 copy.43
  17.2 6.5 %shard_map.113 = (bf16[128,8192]{1,0:T(8,128)(2,1)}, bf16[128,8192]{1,0:T(8,128)(2,1)}) custom-call(bf16[16,512,128]{2,1,0:T(8,128)(2,1)} %pair_ref.1, bf16[512,128]{1,0:T(8,128)(2,1)} %bitcast.64), custom_call_target="tpu_custom_call" | custom-call | flops 1073741824 | bytes 6291456 | tf_op jit(solution)/shard_map/pallas_call | solution.py:101
  23.7 0.0 copy-done.2
  23.7 0.0 copy-start.1
  23.7 2.6 %copy.45 = bf16[16,8,16,512]{3,2,1,0:T(8,128)(2,1)S(1)} copy(bf16[16,8,16,512]{3,1,2,0:T(8,128)(2,1)} %bitcast.57) | data formatting | bytes 4194304
  26.3 0.0 copy-done.1
  26.3 2.1 %copy.44 = bf16[16,8,16,512]{3,2,1,0:T(8,128)(2,1)} copy(bf16[16,8,16,512]{3,1,2,0:T(8,128)(2,1)S(1)} %bitcast.56) | data formatting | bytes 4194304
  28.5 0.0 collective-permute-done
  28.5 0.4 copy.35
  28.9 1.1 reshape.85
  30.0 12.8 %all-to-all-start.1 = ((bf16[64,2,512]{2,1,0:T(2,128)(2,1)}), bf16[64,2,512]{2,1,0:T(2,128)(2,1)S(1)}, u32[]{:S(2)}, u32[]{:S(2)}) async-start(bf16[64,2,512]{2,1,0:T(2,128)(2,1)} %reshape.85), calls=%async_computation.1 | async-start | bytes 262144 | tf_op jit(solution)/shard_map/all_to_all | solution.py:57
  42.7 3.9 %pad_maximum_fusion = bf16[128,2,16,512]{3,2,1,0:T(8,128)(2,1)} fusion(bf16[128,1,16,512]{3,2,1,0:T(8,128)(2,1)S(1)} %bitcast.50, bf16[128,1,16,512]{3,2,1,0:T(8,128)(2,1)} %bitcast.51), kind=kLoop, calls=%fused_computation | loop fusion | flops 2097152 | bytes 8388608 | tf_op jit(solution)/shard_map/stack | solution.py:70
  46.7 6.1 %all-to-all-done.1 = bf16[64,2,512]{2,1,0:T(2,128)(2,1)S(1)} async-done(((bf16[64,2,512]{2,1,0:T(2,128)(2,1)}), bf16[64,2,512]{2,1,0:T(2,128)(2,1)S(1)}, u32[]{:S(2)}, u32[]{:S(2)}) %all-to-all-start.1) | async-done | bytes 131104 | tf_op jit(solution)/shard_map/all_to_all | solution.py:57
  52.7 4.9 %all-to-all-start = ((bf16[128,2,16,512]{3,2,1,0:T(8,128)(2,1)}), bf16[128,2,16,512]{3,2,1,0:T(8,128)(2,1)}, u32[]{:S(2)}, u32[]{:S(2)}) async-start(bf16[128,2,16,512]{3,2,1,0:T(8,128)(2,1)} %pad_maximum_fusion), calls=%async_computation | async-start | bytes 8388608 | tf_op jit(solution)/shard_map/all_to_all | solution.py:69
  57.7 0.3 reshape.86
  58.0 0.1 copy.36
  58.1 55.7 %all-to-all-done.moved_ref = bf16[128,2,16,512]{3,2,1,0:T(8,128)(2,1)} async-done(((bf16[128,2,16,512]{3,2,1,0:T(8,128)(2,1)}), bf16[128,2,16,512]{3,2,1,0:T(8,128)(2,1)}, u32[]{:S(2)}, u32[]{:S(2)}) %all-to-all-start) | async-done | bytes 4194336 | tf_op jit(solution)/shard_map/all_to_all | solution.py:69
  113.8 5.9 %shard_map.114 = bf16[2,1024,512]{2,1,0:T(8,128)(2,1)} custom-call(bf16[128,2,16,512]{3,2,1,0:T(8,128)(2,1)} %all-to-all-done.moved_ref), custom_call_target="tpu_custom_call" | custom-call | flops 2147483648 | bytes 6291456 | tf_op jit(solution)/shard_map/pallas_call | solution.py:146
  119.7 6.5 %all-gather.2.cloned.1.call-done = bf16[32,128,512]{2,0,1:T(8,128)(2,1)} async-done(((bf16[32,2,512]{2,0,1:T(8,128)(2,1)}), bf16[32,128,512]{2,0,1:T(8,128)(2,1)}) %all-gather.2.cloned.1.call-update) | async-done | bytes 4194320 | tf_op jit(solution)/shard_map/all_gather | solution.py:63
  126.1 0.0 copy-start.3
  126.1 4.5 %all-to-all-start.2 = ((bf16[128,16,512]{2,1,0:T(8,128)(2,1)}), bf16[128,16,512]{2,1,0:T(8,128)(2,1)S(1)}, u32[]{:S(2)}, u32[]{:S(2)}) async-start(bf16[128,16,512]{2,1,0:T(8,128)(2,1)} %bitcast.55), calls=%async_computation.2 | async-start | bytes 4194304 | tf_op jit(solution)/shard_map/all_to_all | solution.py:76
  130.6 2.0 %copy.42 = bf16[1,1024,256]{2,1,0:T(8,128)(2,1)} copy(bf16[1,1024,256]{1,2,0:T(8,128)(2,1)} %copy-done.2) | data formatting | bytes 1048576
  132.7 0.0 copy-done.3
  132.7 0.6 slice.17.wg_ref
  133.3 1.1 copy.39
  134.3 0.9 copy.40
  135.2 1.1 copy.38
  136.3 6.5 %copy.41.r_ref = bf16[32,128,512]{2,1,0:T(8,128)(2,1)} copy(bf16[32,128,512]{2,0,1:T(8,128)(2,1)} %all-gather.2.cloned.1.call-done) | data formatting | bytes 8388608 | tf_op jit(solution)/shard_map/optimization_barrier | solution.py:293
  142.8 19.9 %shard_map.115.outer_ref = f32[16,512,128]{2,1,0:T(8,128)} custom-call(bf16[512,128]{1,0:T(8,128)(2,1)} %bitcast.63, bf16[32,128,512]{2,1,0:T(8,128)(2,1)} %copy.41.r_ref, bf16[128,1024]{1,0:T(8,128)(2,1)} %bitcast.62), custom_call_target="tpu_custom_call" | custom-call | flops 4294967296 | bytes 8388608 | tf_op jit(solution)/shard_map/pallas_call | solution.py:258
  162.7 0.0 all-to-all-done.2
  162.7 2.7 %copy.46 = bf16[16,8,16,512]{3,1,2,0:T(8,128)(2,1)} copy(bf16[16,8,16,512]{3,2,1,0:T(8,128)(2,1)S(1)} %bitcast.49) | data formatting | bytes 4194304
  165.4 16.6 %shard_map.116 = bf16[16,512,128]{2,1,0:T(8,128)(2,1)} custom-call(bf16[128,8192]{1,0:T(8,128)(2,1)} %bitcast.58, bf16[16,512,128]{2,1,0:T(8,128)(2,1)} %pair_ref.1, f32[16,512,128]{2,1,0:T(8,128)} %shard_map.115.outer_ref, bf16[128,128]{1,0:T(8,128)(2,1)} %wo_ref.1, bf16[128,128]{1,0:T(8,128)(2,1)} %slice.17.wg_ref, bf16[128,512]{1,0:T(8,128)(2,1)} %wu_ref.1, ...), custom_call_target="tpu_custom_call" | custom-call | flops 2952790016 | bytes 10485760 | tf_op jit(solution)/shard_map/pallas_call | solution.py:196
  (8 shorter events, 0.1 us)
Async XLA Ops:
  7.2 1.7 copy-start
  7.2 1.7 copy-start.4
  7.2 118.9 %all-gather.2.cloned.1.call-start = ((), (), s32[]{:S(2)}) async-start(), calls=%async_computation.3 | async-start | bytes 4259840 | tf_op jit(solution)/shard_map/all_gather | solution.py:63
  8.9 1.5 copy-start.5
  10.2 13.5 %copy-start.2 = (bf16[1,1024,256]{1,2,0:T(8,128)(2,1)}, bf16[1,1024,256]{1,2,0:T(8,128)(2,1)S(1)}, u32[]{:S(2)}) copy-start(bf16[1,1024,256]{1,2,0:T(8,128)(2,1)S(1)} %get-tuple-element.29) | copy-start | bytes 1572868
  10.2 6.2 %slice-start = ((bf16[128,640]{1,0:T(8,128)(2,1)}), bf16[128,512]{1,0:T(8,128)(2,1)S(1)}, s32[]{:S(2)}) async-start(bf16[128,640]{1,0:T(8,128)(2,1)} %param.16), calls=%async_computation.4 | async-start | bytes 262144 | tf_op jit(solution)/shard_map/slice | solution.py:98
  10.7 3.5 %collective-permute-start.1 = (bf16[1,32,512]{2,1,0:T(8,128)(2,1)S(1)}, bf16[1,32,512]{2,1,0:T(8,128)(2,1)S(1)}, u32[]{:S(2)}, u32[]{:S(2)}) collective-permute-start(bf16[1,32,512]{2,1,0:T(8,128)(2,1)S(1)} %get-tuple-element.27), channel_id=1, source_target_pairs={{0,64},{64,0},{1,65},{65,1},{2,66},{66,2},{3,67},{67,3},{4,68},{68... | collective-permute-start | bytes 98312 | tf_op jit(solution)/shard_map/ppermute | solution.py:62
  14.9 13.6 %collective-permute-start = (bf16[1,1024,32]{1,2,0:T(8,128)(2,1)S(1)}, bf16[1,1024,32]{1,2,0:T(8,128)(2,1)S(1)}, u32[]{:S(2)}, u32[]{:S(2)}) collective-permute-start(bf16[1,1024,32]{1,2,0:T(8,128)(2,1)S(1)} %get-tuple-element.25), channel_id=1, source_target_pairs={{0,64},{64,0},{1,65},{65,1},{2,66},{66,2},{3,67},{67,3},{4,68},{68... | collective-permute-start | bytes 196616 | tf_op jit(solution)/shard_map/ppermute | solution.py:56
  23.7 2.6 %copy-start.1 = (bf16[128,8192]{1,0:T(8,128)(2,1)S(1)}, bf16[128,8192]{1,0:T(8,128)(2,1)}, u32[]{:S(2)}) copy-start(bf16[128,8192]{1,0:T(8,128)(2,1)} %get-tuple-element.9) | copy-start | bytes 6291460
  30.0 22.8 %all-to-all-start.1 = ((bf16[64,2,512]{2,1,0:T(2,128)(2,1)}), bf16[64,2,512]{2,1,0:T(2,128)(2,1)S(1)}, u32[]{:S(2)}, u32[]{:S(2)}) async-start(bf16[64,2,512]{2,1,0:T(2,128)(2,1)} %reshape.85), calls=%async_computation.1 | async-start | bytes 262144 | tf_op jit(solution)/shard_map/all_to_all | solution.py:57
  52.7 61.0 %all-to-all-start = ((bf16[128,2,16,512]{3,2,1,0:T(8,128)(2,1)}), bf16[128,2,16,512]{3,2,1,0:T(8,128)(2,1)}, u32[]{:S(2)}, u32[]{:S(2)}) async-start(bf16[128,2,16,512]{3,2,1,0:T(8,128)(2,1)} %pad_maximum_fusion), calls=%async_computation | async-start | bytes 8388608 | tf_op jit(solution)/shard_map/all_to_all | solution.py:69
  126.1 6.5 %copy-start.3 = (bf16[128,640]{1,0:T(8,128)(2,1)S(1)}, bf16[128,640]{1,0:T(8,128)(2,1)}, u32[]{:S(2)}) copy-start(bf16[128,640]{1,0:T(8,128)(2,1)} %param.16) | copy-start | bytes 491524
  126.1 36.6 %all-to-all-start.2 = ((bf16[128,16,512]{2,1,0:T(8,128)(2,1)}), bf16[128,16,512]{2,1,0:T(8,128)(2,1)S(1)}, u32[]{:S(2)}, u32[]{:S(2)}) async-start(bf16[128,16,512]{2,1,0:T(8,128)(2,1)} %bitcast.55), calls=%async_computation.2 | async-start | bytes 4194304 | tf_op jit(solution)/shard_map/all_to_all | solution.py:76
Sparse Core Ops, SparseCore 0:
  15.0 111.0 all-gather.1

commit v6 on v5

--- a/solution.py
+++ b/solution.py
@@ -290,9 +290,7 @@
     )
     moved = send_whole(tri_left, tri_right)
     product = triangle_product(moved)
-    product, left_gathered, right_gathered = lax.optimization_barrier(
-        (product, left_gathered, right_gathered)
-    )
+    product, left_gathered = lax.optimization_barrier((product, left_gathered))
     product_tile = send_back(product)
     outer_update = outer_product(left_gathered, right_gathered, outer_output_weight)
     product_tile, outer_update = lax.optimization_barrier((product_tile, outer_update))

time: 189 us -> 186 us (0.984)
  waiting for transfers between devices: 69.5 us -> 63.1 us
  starting transfers between devices: 26 us -> 28.6 us
    all_gather x0 -> x1, local copies, waits for them, and re-layouts: none -> 6.49 us  [gather_sides(): lax.all_gather(jnp.swapaxes(right_pair, 0, 1), 'rows', axis=1, tiled=True)]
    optimization_barrier x1 -> x0, local copies, waits for them, and re-layouts: 6.49 us -> none  [on_device(): lax.optimization_barrier((product, left_gathered, right_gathered))]
    all_gather x1, waiting for transfers between devices: 6.46 us -> 0.01 us  [gather_sides(): lax.all_gather(jnp.swapaxes(right_pair, 0, 1), 'rows', axis=1, tiled=True)]
    all_to_all x1, starting transfers between devices: 4.49 us -> 7.09 us  [send_back(): lax.all_to_all(product, ('branch', 'rows'), split_axis=0, concat_axis=0,...]
  transfers between devices with their start and end apart: 6 -> 6, of which waited for: 4 -> 3; matrix products, arithmetic and copies ran while one was open for 12% -> 13% of each run, Pallas kernels for 17% -> 17%
where the time goes in v6:
time: 186 us; the launch traced here: 185 us
  waiting for transfers between devices  63.1 us (34%)
  Pallas kernels  48.9 us (26%)
  starting transfers between devices  28.6 us (15%)
  local copies, waits for them, and re-layouts  23.6 us (13%)
  between operations  14.2 us (8%)
  other arithmetic  5.03 us (3%)
    all_to_all x1, waiting for transfers between devices, send_whole(): lax.all_to_all(jnp.stack([tri_left, tri_right], axis=1), both, split_axis...  55.7 us
    pallas_call x1, Pallas kernels, outer_product(): pl.pallas_call(outer_kernel, out_shape=jax.ShapeDtypeStruct((tile_rows, c...  19.9 us
    pallas_call x1, Pallas kernels, pair_back(): pl.pallas_call(back_kernel, out_shape=jax.ShapeDtypeStruct((tile_rows, co...  16.6 us
    unnamed x20, local copies, waits for them, and re-layouts  12.9 us
    all_to_all x1, starting transfers between devices, gather_sides(): lax.all_to_all(left_pair, 'rows', split_axis=1, concat_axis=0, tiled=True)  12.8 us
    all_to_all x1, starting transfers between devices, send_back(): lax.all_to_all(product, ('branch', 'rows'), split_axis=0, concat_axis=0,...  7.09 us
    pallas_call x1, Pallas kernels, pair_front(): pl.pallas_call(front_kernel, out_shape=(side, side), grid=(tile_rows // s...  6.53 us
    all_gather x1, local copies, waits for them, and re-layouts, gather_sides(): lax.all_gather(jnp.swapaxes(right_pair, 0, 1), 'rows', axis=1, tiled=True)  6.49 us
  transfers between devices with their start and end apart: 6, of which 3 were waited for; matrix products, arithmetic and copies ran while one was open for 13% of the time, Pallas kernels for 17%

profile of v6, /device:TPU:1, one launch (start us, length us, event | category | flops | bytes accessed | tf_op | source)
XLA Modules:
  0.0 185.0 jit_solution(11204048652027274505)
XLA Ops:
  7.2 0.0 copy-start
  7.2 0.0 copy-start.4
  7.2 0.0 all-gather.2.cloned.1.call-start
  7.2 1.3 copy.33
  8.6 0.1 convert_reduce_fusion
  8.7 0.2 fusion.8
  8.8 0.0 copy-done
  8.9 0.0 copy-done.4
  8.9 0.0 copy-start.5
  8.9 1.3 convert_reduce_fusion.1
  10.2 0.0 copy-start.2
  10.2 0.0 slice-start
  10.2 0.2 fusion.10
  10.4 0.0 copy-done.5
  10.4 0.3 fusion.7
  10.7 2.2 %collective-permute-start.1 = (bf16[1,32,512]{2,1,0:T(8,128)(2,1)S(1)}, bf16[1,32,512]{2,1,0:T(8,128)(2,1)S(1)}, u32[]{:S(2)}, u32[]{:S(2)}) collective-permute-start(bf16[1,32,512]{2,1,0:T(8,128)(2,1)S(1)} %get-tuple-element.25), channel_id=1, source_target_pairs={{0,64},{64,0},{1,65},{65,1},{2,66},{66,2},{3,67},{67,3},{4,68},{68... | collective-permute-start | bytes 98312 | tf_op jit(solution)/shard_map/ppermute | solution.py:62
  12.9 1.3 collective-permute-done.1
  14.2 0.6 fusion.23
  14.9 0.0 all-gather.2.cloned.1.call-update
  14.9 1.5 collective-permute-start
  16.4 0.0 slice-done
  16.4 0.8 copy.43
  17.2 6.5 %shard_map.113 = (bf16[128,8192]{1,0:T(8,128)(2,1)}, bf16[128,8192]{1,0:T(8,128)(2,1)}) custom-call(bf16[16,512,128]{2,1,0:T(8,128)(2,1)} %pair_ref.1, bf16[512,128]{1,0:T(8,128)(2,1)} %bitcast.64), custom_call_target="tpu_custom_call" | custom-call | flops 1073741824 | bytes 6291456 | tf_op jit(solution)/shard_map/pallas_call | solution.py:101
  23.7 0.0 copy-done.2
  23.7 0.0 copy-start.1
  23.7 2.6 %copy.45 = bf16[16,8,16,512]{3,2,1,0:T(8,128)(2,1)S(1)} copy(bf16[16,8,16,512]{3,1,2,0:T(8,128)(2,1)} %bitcast.57) | data formatting | bytes 4194304
  26.3 0.0 copy-done.1
  26.3 2.1 %copy.44 = bf16[16,8,16,512]{3,2,1,0:T(8,128)(2,1)} copy(bf16[16,8,16,512]{3,1,2,0:T(8,128)(2,1)S(1)} %bitcast.56) | data formatting | bytes 4194304
  28.5 0.0 collective-permute-done
  28.5 0.4 copy.35
  28.9 1.1 reshape.85
  30.0 12.8 %all-to-all-start.1 = ((bf16[64,2,512]{2,1,0:T(2,128)(2,1)}), bf16[64,2,512]{2,1,0:T(2,128)(2,1)S(1)}, u32[]{:S(2)}, u32[]{:S(2)}) async-start(bf16[64,2,512]{2,1,0:T(2,128)(2,1)} %reshape.85), calls=%async_computation.1 | async-start | bytes 262144 | tf_op jit(solution)/shard_map/all_to_all | solution.py:57
  42.7 3.9 %pad_maximum_fusion = bf16[128,2,16,512]{3,2,1,0:T(8,128)(2,1)} fusion(bf16[128,1,16,512]{3,2,1,0:T(8,128)(2,1)S(1)} %bitcast.50, bf16[128,1,16,512]{3,2,1,0:T(8,128)(2,1)} %bitcast.51), kind=kLoop, calls=%fused_computation | loop fusion | flops 2097152 | bytes 8388608 | tf_op jit(solution)/shard_map/stack | solution.py:70
  46.7 6.1 %all-to-all-done.1 = bf16[64,2,512]{2,1,0:T(2,128)(2,1)S(1)} async-done(((bf16[64,2,512]{2,1,0:T(2,128)(2,1)}), bf16[64,2,512]{2,1,0:T(2,128)(2,1)S(1)}, u32[]{:S(2)}, u32[]{:S(2)}) %all-to-all-start.1) | async-done | bytes 131104 | tf_op jit(solution)/shard_map/all_to_all | solution.py:57
  52.7 4.9 %all-to-all-start = ((bf16[128,2,16,512]{3,2,1,0:T(8,128)(2,1)}), bf16[128,2,16,512]{3,2,1,0:T(8,128)(2,1)}, u32[]{:S(2)}, u32[]{:S(2)}) async-start(bf16[128,2,16,512]{3,2,1,0:T(8,128)(2,1)} %pad_maximum_fusion), calls=%async_computation | async-start | bytes 8388608 | tf_op jit(solution)/shard_map/all_to_all | solution.py:69
  57.7 0.3 reshape.86
  58.0 0.1 copy.36
  58.1 55.7 %all-to-all-done.moved_ref = bf16[128,2,16,512]{3,2,1,0:T(8,128)(2,1)} async-done(((bf16[128,2,16,512]{3,2,1,0:T(8,128)(2,1)}), bf16[128,2,16,512]{3,2,1,0:T(8,128)(2,1)}, u32[]{:S(2)}, u32[]{:S(2)}) %all-to-all-start) | async-done | bytes 4194336 | tf_op jit(solution)/shard_map/all_to_all | solution.py:69
  113.8 5.9 %shard_map.114 = bf16[2,1024,512]{2,1,0:T(8,128)(2,1)} custom-call(bf16[128,2,16,512]{3,2,1,0:T(8,128)(2,1)} %all-to-all-done.moved_ref), custom_call_target="tpu_custom_call" | custom-call | flops 2147483648 | bytes 6291456 | tf_op jit(solution)/shard_map/pallas_call | solution.py:146
  119.7 0.0 copy-start.3
  119.7 7.1 %all-to-all-start.2 = ((bf16[128,16,512]{2,1,0:T(8,128)(2,1)}), bf16[128,16,512]{2,1,0:T(8,128)(2,1)S(1)}, u32[]{:S(2)}, u32[]{:S(2)}) async-start(bf16[128,16,512]{2,1,0:T(8,128)(2,1)} %bitcast.55), calls=%async_computation.2 | async-start | bytes 4194304 | tf_op jit(solution)/shard_map/all_to_all | solution.py:76
  126.8 2.0 %copy.42 = bf16[1,1024,256]{2,1,0:T(8,128)(2,1)} copy(bf16[1,1024,256]{1,2,0:T(8,128)(2,1)} %copy-done.2) | data formatting | bytes 1048576
  128.8 0.0 copy-done.3
  128.8 0.6 slice.17.wg_ref
  129.4 1.1 copy.39
  130.5 0.9 copy.40
  131.3 1.1 copy.38
  132.4 0.0 all-gather.2.cloned.1.call-done
  132.4 6.5 %copy.41.r_ref = bf16[32,128,512]{2,1,0:T(8,128)(2,1)} copy(bf16[32,128,512]{2,0,1:T(8,128)(2,1)} %all-gather.2.cloned.1.call-done) | data formatting | bytes 8388608 | tf_op jit(solution)/shard_map/all_gather | solution.py:63
  138.9 19.9 %shard_map.115.outer_ref = f32[16,512,128]{2,1,0:T(8,128)} custom-call(bf16[512,128]{1,0:T(8,128)(2,1)} %bitcast.63, bf16[32,128,512]{2,1,0:T(8,128)(2,1)} %copy.41.r_ref, bf16[128,1024]{1,0:T(8,128)(2,1)} %bitcast.62), custom_call_target="tpu_custom_call" | custom-call | flops 4294967296 | bytes 8388608 | tf_op jit(solution)/shard_map/pallas_call | solution.py:258
  158.9 0.0 all-to-all-done.2
  158.9 2.7 %copy.46 = bf16[16,8,16,512]{3,1,2,0:T(8,128)(2,1)} copy(bf16[16,8,16,512]{3,2,1,0:T(8,128)(2,1)S(1)} %bitcast.49) | data formatting | bytes 4194304
  161.6 16.6 %shard_map.116 = bf16[16,512,128]{2,1,0:T(8,128)(2,1)} custom-call(bf16[128,8192]{1,0:T(8,128)(2,1)} %bitcast.58, bf16[16,512,128]{2,1,0:T(8,128)(2,1)} %pair_ref.1, f32[16,512,128]{2,1,0:T(8,128)} %shard_map.115.outer_ref, bf16[128,128]{1,0:T(8,128)(2,1)} %wo_ref.1, bf16[128,128]{1,0:T(8,128)(2,1)} %slice.17.wg_ref, bf16[128,512]{1,0:T(8,128)(2,1)} %wu_ref.1, ...), custom_call_target="tpu_custom_call" | custom-call | flops 2952790016 | bytes 10485760 | tf_op jit(solution)/shard_map/pallas_call | solution.py:196
  (8 shorter events, 0.1 us)
Async XLA Ops:
  7.2 1.7 copy-start
  7.2 1.7 copy-start.4
  7.2 125.2 %all-gather.2.cloned.1.call-start = ((), (), s32[]{:S(2)}) async-start(), calls=%async_computation.3 | async-start | bytes 4259840 | tf_op jit(solution)/shard_map/all_gather | solution.py:63
  8.9 1.5 copy-start.5
  10.2 13.5 %copy-start.2 = (bf16[1,1024,256]{1,2,0:T(8,128)(2,1)}, bf16[1,1024,256]{1,2,0:T(8,128)(2,1)S(1)}, u32[]{:S(2)}) copy-start(bf16[1,1024,256]{1,2,0:T(8,128)(2,1)S(1)} %get-tuple-element.27) | copy-start | bytes 1572868
  10.2 6.2 %slice-start = ((bf16[128,640]{1,0:T(8,128)(2,1)}), bf16[128,512]{1,0:T(8,128)(2,1)S(1)}, s32[]{:S(2)}) async-start(bf16[128,640]{1,0:T(8,128)(2,1)} %param.16), calls=%async_computation.4 | async-start | bytes 262144 | tf_op jit(solution)/shard_map/slice | solution.py:98
  10.7 3.5 %collective-permute-start.1 = (bf16[1,32,512]{2,1,0:T(8,128)(2,1)S(1)}, bf16[1,32,512]{2,1,0:T(8,128)(2,1)S(1)}, u32[]{:S(2)}, u32[]{:S(2)}) collective-permute-start(bf16[1,32,512]{2,1,0:T(8,128)(2,1)S(1)} %get-tuple-element.25), channel_id=1, source_target_pairs={{0,64},{64,0},{1,65},{65,1},{2,66},{66,2},{3,67},{67,3},{4,68},{68... | collective-permute-start | bytes 98312 | tf_op jit(solution)/shard_map/ppermute | solution.py:62
  14.9 13.6 %collective-permute-start = (bf16[1,1024,32]{1,2,0:T(8,128)(2,1)S(1)}, bf16[1,1024,32]{1,2,0:T(8,128)(2,1)S(1)}, u32[]{:S(2)}, u32[]{:S(2)}) collective-permute-start(bf16[1,1024,32]{1,2,0:T(8,128)(2,1)S(1)} %get-tuple-element.23), channel_id=1, source_target_pairs={{0,64},{64,0},{1,65},{65,1},{2,66},{66,2},{3,67},{67,3},{4,68},{68... | collective-permute-start | bytes 196616 | tf_op jit(solution)/shard_map/ppermute | solution.py:56
  23.7 2.6 %copy-start.1 = (bf16[128,8192]{1,0:T(8,128)(2,1)S(1)}, bf16[128,8192]{1,0:T(8,128)(2,1)}, u32[]{:S(2)}) copy-start(bf16[128,8192]{1,0:T(8,128)(2,1)} %get-tuple-element.8) | copy-start | bytes 6291460
  30.0 22.8 %all-to-all-start.1 = ((bf16[64,2,512]{2,1,0:T(2,128)(2,1)}), bf16[64,2,512]{2,1,0:T(2,128)(2,1)S(1)}, u32[]{:S(2)}, u32[]{:S(2)}) async-start(bf16[64,2,512]{2,1,0:T(2,128)(2,1)} %reshape.85), calls=%async_computation.1 | async-start | bytes 262144 | tf_op jit(solution)/shard_map/all_to_all | solution.py:57
  52.7 61.0 %all-to-all-start = ((bf16[128,2,16,512]{3,2,1,0:T(8,128)(2,1)}), bf16[128,2,16,512]{3,2,1,0:T(8,128)(2,1)}, u32[]{:S(2)}, u32[]{:S(2)}) async-start(bf16[128,2,16,512]{3,2,1,0:T(8,128)(2,1)} %pad_maximum_fusion), calls=%async_computation | async-start | bytes 8388608 | tf_op jit(solution)/shard_map/all_to_all | solution.py:69
  119.7 9.1 %copy-start.3 = (bf16[128,640]{1,0:T(8,128)(2,1)S(1)}, bf16[128,640]{1,0:T(8,128)(2,1)}, u32[]{:S(2)}) copy-start(bf16[128,640]{1,0:T(8,128)(2,1)} %param.16) | copy-start | bytes 491524
  119.7 39.2 %all-to-all-start.2 = ((bf16[128,16,512]{2,1,0:T(8,128)(2,1)}), bf16[128,16,512]{2,1,0:T(8,128)(2,1)S(1)}, u32[]{:S(2)}, u32[]{:S(2)}) async-start(bf16[128,16,512]{2,1,0:T(8,128)(2,1)} %bitcast.55), calls=%async_computation.2 | async-start | bytes 4194304 | tf_op jit(solution)/shard_map/all_to_all | solution.py:76
Sparse Core Ops, SparseCore 0:
  15.0 111.0 all-gather.1

commit v7 on v6

--- a/solution.py
+++ b/solution.py
@@ -60,7 +60,8 @@
     keep = lax.dynamic_slice_in_dim(right_side, me * half, half, axis=2)
     send = lax.dynamic_slice_in_dim(right_side, (1 - me) * half, half, axis=2)
     right_pair = branch_pair(keep, lax.ppermute(send, "branch", swap))
-    right_gathered = lax.all_gather(jnp.swapaxes(right_pair, 0, 1), "rows", axis=1, tiled=True)
+    right_flat = right_pair.reshape(right_pair.shape[0], -1)
+    right_gathered = lax.all_gather(right_flat, "rows", axis=0, tiled=True)
     return left_gathered, right_gathered
 
 
@@ -224,12 +225,13 @@
 
 
 def outer_kernel(lt_ref, r_ref, wt_ref, out_ref, x_ref):
-    n_factor = r_ref.shape[0]
-    tile_rows = out_ref.shape[0]
-    scale = 1.0 / r_ref.shape[1]
+    tile_rows, columns, _ = out_ref.shape
+    n_factor = r_ref.shape[1] // columns
+    scale = 1.0 / r_ref.shape[0]
 
     def fill(d, carry):
-        vals = jnp.dot(lt_ref[...], r_ref[d], preferred_element_type=jnp.float32)
+        lanes = pl.ds(pl.multiple_of(d * columns, columns), columns)
+        vals = jnp.dot(lt_ref[...], r_ref[:, lanes], preferred_element_type=jnp.float32)
         vals = (vals * scale).astype(jnp.bfloat16)
         start = pl.multiple_of(d * n_factor, n_factor)
         for i in range(tile_rows):
@@ -248,7 +250,7 @@
 
 def outer_product(left_gathered, right_gathered, outer_output_weight):
     total_rows, tile_rows, channels = left_gathered.shape
-    columns = right_gathered.shape[2]
+    columns = right_gathered.shape[1] // channels
     pair = outer_output_weight.shape[1]
     left_t = jnp.transpose(left_gathered, (1, 2, 0)).reshape(tile_rows * channels, total_rows)
     weight_t = jnp.transpose(

time: 186 us -> 187 us (level)
    unnamed x20 -> x24, local copies, waits for them, and re-layouts: 12.9 us -> 20.3 us
    all_gather x1 -> x0, local copies, waits for them, and re-layouts: 6.49 us -> none  [gather_sides(): lax.all_gather(jnp.swapaxes(right_pair, 0, 1), 'rows', axis=1, tiled=True)]
where the time goes in v7:
time: 187 us; the launch traced here: 186 us
  waiting for transfers between devices  63 us (34%)
  Pallas kernels  49.1 us (26%)
  starting transfers between devices  28.6 us (15%)
  local copies, waits for them, and re-layouts  24.4 us (13%)
  between operations  14.2 us (8%)
  other arithmetic  5.3 us (3%)
    all_to_all x1, waiting for transfers between devices, send_whole(): lax.all_to_all(jnp.stack([tri_left, tri_right], axis=1), both, split_axis...  55.6 us
    unnamed x24, local copies, waits for them, and re-layouts  20.3 us
    pallas_call x1, Pallas kernels, outer_product(): pl.pallas_call(outer_kernel, out_shape=jax.ShapeDtypeStruct((tile_rows, c...  20.1 us
    pallas_call x1, Pallas kernels, pair_back(): pl.pallas_call(back_kernel, out_shape=jax.ShapeDtypeStruct((tile_rows, co...  16.6 us
    all_to_all x1, starting transfers between devices, gather_sides(): lax.all_to_all(left_pair, 'rows', split_axis=1, concat_axis=0, tiled=True)  12.8 us
    all_to_all x1, starting transfers between devices, send_back(): lax.all_to_all(product, ('branch', 'rows'), split_axis=0, concat_axis=0,...  7.14 us
    pallas_call x1, Pallas kernels, pair_front(): pl.pallas_call(front_kernel, out_shape=(side, side), grid=(tile_rows // s...  6.54 us
    all_to_all x1, waiting for transfers between devices, gather_sides(): lax.all_to_all(left_pair, 'rows', split_axis=1, concat_axis=0, tiled=True)  6.06 us
  transfers between devices with their start and end apart: 6, of which 3 were waited for; matrix products, arithmetic and copies ran while one was open for 13% of the time, Pallas kernels for 17%

profile of v7, /device:TPU:1, one launch (start us, length us, event | category | flops | bytes accessed | tf_op | source)
XLA Modules:
  0.0 186.3 jit_solution(1906729604676545181)
XLA Ops:
  7.2 0.0 copy-start
  7.2 0.0 copy-start.4
  7.2 0.0 all-gather.3.cloned.1.call-start
  7.2 1.3 copy.32
  8.6 0.1 convert_reduce_fusion
  8.7 0.2 fusion.8
  8.8 0.0 copy-done
  8.9 0.0 copy-done.4
  8.9 0.0 copy-start.5
  8.9 1.3 convert_reduce_fusion.1
  10.2 0.0 copy-start.2
  10.2 0.0 slice-start
  10.2 0.2 fusion.10
  10.4 0.0 copy-done.5
  10.4 0.3 fusion.7
  10.7 2.2 %collective-permute-start.1 = (bf16[1,32,512]{2,1,0:T(8,128)(2,1)S(1)}, bf16[1,32,512]{2,1,0:T(8,128)(2,1)S(1)}, u32[]{:S(2)}, u32[]{:S(2)}) collective-permute-start(bf16[1,32,512]{2,1,0:T(8,128)(2,1)S(1)} %get-tuple-element.25), channel_id=1, source_target_pairs={{0,64},{64,0},{1,65},{65,1},{2,66},{66,2},{3,67},{67,3},{4,68},{68... | collective-permute-start | bytes 98312 | tf_op jit(solution)/shard_map/ppermute | solution.py:62
  12.9 0.1 copy.44
  13.0 1.2 collective-permute-done.1
  14.2 0.1 copy.45
  14.3 0.9 fusion.23
  15.2 0.0 all-gather.3.cloned.1.call-update
  15.2 1.5 collective-permute-start
  16.8 0.0 slice-done
  16.8 0.8 copy.41
  17.5 6.5 %shard_map.113 = (bf16[128,8192]{1,0:T(8,128)(2,1)}, bf16[128,8192]{1,0:T(8,128)(2,1)}) custom-call(bf16[16,512,128]{2,1,0:T(8,128)(2,1)} %pair_ref.1, bf16[512,128]{1,0:T(8,128)(2,1)} %bitcast.70), custom_call_target="tpu_custom_call" | custom-call | flops 1073741824 | bytes 6291456 | tf_op jit(solution)/shard_map/pallas_call | solution.py:102
  24.1 0.0 copy-done.2
  24.1 0.0 copy-start.1
  24.1 2.6 %copy.43 = bf16[16,8,16,512]{3,2,1,0:T(8,128)(2,1)S(1)} copy(bf16[16,8,16,512]{3,1,2,0:T(8,128)(2,1)} %bitcast.61) | data formatting | bytes 4194304
  26.6 0.0 copy-done.1
  26.7 2.1 %copy.42 = bf16[16,8,16,512]{3,2,1,0:T(8,128)(2,1)} copy(bf16[16,8,16,512]{3,1,2,0:T(8,128)(2,1)S(1)} %bitcast.60) | data formatting | bytes 4194304
  28.8 0.0 collective-permute-done
  28.8 0.4 copy.34
  29.2 1.1 reshape.92
  30.3 12.8 %all-to-all-start.1 = ((bf16[64,2,512]{2,1,0:T(2,128)(2,1)}), bf16[64,2,512]{2,1,0:T(2,128)(2,1)S(1)}, u32[]{:S(2)}, u32[]{:S(2)}) async-start(bf16[64,2,512]{2,1,0:T(2,128)(2,1)} %reshape.92), calls=%async_computation.1 | async-start | bytes 262144 | tf_op jit(solution)/shard_map/all_to_all | solution.py:57
  43.1 3.9 %pad_maximum_fusion = bf16[128,2,16,512]{3,2,1,0:T(8,128)(2,1)} fusion(bf16[128,1,16,512]{3,2,1,0:T(8,128)(2,1)S(1)} %bitcast.54, bf16[128,1,16,512]{3,2,1,0:T(8,128)(2,1)} %bitcast.55), kind=kLoop, calls=%fused_computation | loop fusion | flops 2097152 | bytes 8388608 | tf_op jit(solution)/shard_map/stack | solution.py:71
  47.0 6.1 %all-to-all-done.1 = bf16[64,2,512]{2,1,0:T(2,128)(2,1)S(1)} async-done(((bf16[64,2,512]{2,1,0:T(2,128)(2,1)}), bf16[64,2,512]{2,1,0:T(2,128)(2,1)S(1)}, u32[]{:S(2)}, u32[]{:S(2)}) %all-to-all-start.1) | async-done | bytes 131104 | tf_op jit(solution)/shard_map/all_to_all | solution.py:57
  53.1 4.9 %all-to-all-start = ((bf16[128,2,16,512]{3,2,1,0:T(8,128)(2,1)}), bf16[128,2,16,512]{3,2,1,0:T(8,128)(2,1)}, u32[]{:S(2)}, u32[]{:S(2)}) async-start(bf16[128,2,16,512]{3,2,1,0:T(8,128)(2,1)} %pad_maximum_fusion), calls=%async_computation | async-start | bytes 8388608 | tf_op jit(solution)/shard_map/all_to_all | solution.py:70
  58.0 0.3 reshape.93
  58.3 0.1 copy.35
  58.4 55.6 %all-to-all-done.moved_ref = bf16[128,2,16,512]{3,2,1,0:T(8,128)(2,1)} async-done(((bf16[128,2,16,512]{3,2,1,0:T(8,128)(2,1)}), bf16[128,2,16,512]{3,2,1,0:T(8,128)(2,1)}, u32[]{:S(2)}, u32[]{:S(2)}) %all-to-all-start) | async-done | bytes 4194336 | tf_op jit(solution)/shard_map/all_to_all | solution.py:70
  114.1 5.9 %shard_map.114 = bf16[2,1024,512]{2,1,0:T(8,128)(2,1)} custom-call(bf16[128,2,16,512]{3,2,1,0:T(8,128)(2,1)} %all-to-all-done.moved_ref), custom_call_target="tpu_custom_call" | custom-call | flops 2147483648 | bytes 6291456 | tf_op jit(solution)/shard_map/pallas_call | solution.py:147
  119.9 0.0 copy-start.3
  119.9 7.1 %all-to-all-start.2 = ((bf16[128,16,512]{2,1,0:T(8,128)(2,1)}), bf16[128,16,512]{2,1,0:T(8,128)(2,1)S(1)}, u32[]{:S(2)}, u32[]{:S(2)}) async-start(bf16[128,16,512]{2,1,0:T(8,128)(2,1)} %bitcast.59), calls=%async_computation.2 | async-start | bytes 4194304 | tf_op jit(solution)/shard_map/all_to_all | solution.py:77
  127.1 2.0 %copy.40 = bf16[1,1024,256]{2,1,0:T(8,128)(2,1)} copy(bf16[1,1024,256]{1,2,0:T(8,128)(2,1)} %copy-done.2) | data formatting | bytes 1048576
  129.1 0.0 copy-done.3
  129.1 0.6 slice.17.wg_ref
  129.7 1.1 copy.38
  130.8 0.9 copy.39
  131.7 1.1 copy.37
  132.7 0.0 all-gather.3.cloned.1.call-done
  132.7 7.3 %reshape.91.r_ref = bf16[128,16384]{1,0:T(8,128)(2,1)} reshape(bf16[64,2,16384]{2,1,0:T(2,128)(2,1)} %all-gather.3.cloned.1.call-done) | data formatting | bytes 8388608
  140.0 20.1 %shard_map.115.outer_ref = f32[16,512,128]{2,1,0:T(8,128)} custom-call(bf16[512,128]{1,0:T(8,128)(2,1)} %bitcast.69, bf16[128,16384]{1,0:T(8,128)(2,1)} %reshape.91.r_ref, bf16[128,1024]{1,0:T(8,128)(2,1)} %bitcast.68), custom_call_target="tpu_custom_call" | custom-call | flops 4294967296 | bytes 8388608 | tf_op jit(solution)/shard_map/pallas_call | solution.py:260
  160.1 0.0 all-to-all-done.2
  160.1 2.7 %copy.46 = bf16[16,8,16,512]{3,1,2,0:T(8,128)(2,1)} copy(bf16[16,8,16,512]{3,2,1,0:T(8,128)(2,1)S(1)} %bitcast.53) | data formatting | bytes 4194304
  162.8 16.6 %shard_map.116 = bf16[16,512,128]{2,1,0:T(8,128)(2,1)} custom-call(bf16[128,8192]{1,0:T(8,128)(2,1)} %bitcast.62, bf16[16,512,128]{2,1,0:T(8,128)(2,1)} %pair_ref.1, f32[16,512,128]{2,1,0:T(8,128)} %shard_map.115.outer_ref, bf16[128,128]{1,0:T(8,128)(2,1)} %wo_ref.1, bf16[128,128]{1,0:T(8,128)(2,1)} %slice.17.wg_ref, bf16[128,512]{1,0:T(8,128)(2,1)} %wu_ref.1, ...), custom_call_target="tpu_custom_call" | custom-call | flops 2952790016 | bytes 10485760 | tf_op jit(solution)/shard_map/pallas_call | solution.py:197
  (8 shorter events, 0.1 us)
Async XLA Ops:
  7.2 1.7 copy-start
  7.2 1.7 copy-start.4
  7.2 125.6 %all-gather.3.cloned.1.call-start = ((), (), s32[]{:S(2)}) async-start(), calls=%async_computation.3 | async-start | bytes 4259840 | tf_op jit(solution)/shard_map/all_gather | solution.py:64
  8.9 1.5 copy-start.5
  10.2 13.9 %copy-start.2 = (bf16[1,1024,256]{1,2,0:T(8,128)(2,1)}, bf16[1,1024,256]{1,2,0:T(8,128)(2,1)S(1)}, u32[]{:S(2)}) copy-start(bf16[1,1024,256]{1,2,0:T(8,128)(2,1)S(1)} %get-tuple-element.27) | copy-start | bytes 1572868
  10.2 6.5 %slice-start = ((bf16[128,640]{1,0:T(8,128)(2,1)}), bf16[128,512]{1,0:T(8,128)(2,1)S(1)}, s32[]{:S(2)}) async-start(bf16[128,640]{1,0:T(8,128)(2,1)} %param.16), calls=%async_computation.4 | async-start | bytes 262144 | tf_op jit(solution)/shard_map/slice | solution.py:99
  10.7 3.5 %collective-permute-start.1 = (bf16[1,32,512]{2,1,0:T(8,128)(2,1)S(1)}, bf16[1,32,512]{2,1,0:T(8,128)(2,1)S(1)}, u32[]{:S(2)}, u32[]{:S(2)}) collective-permute-start(bf16[1,32,512]{2,1,0:T(8,128)(2,1)S(1)} %get-tuple-element.25), channel_id=1, source_target_pairs={{0,64},{64,0},{1,65},{65,1},{2,66},{66,2},{3,67},{67,3},{4,68},{68... | collective-permute-start | bytes 98312 | tf_op jit(solution)/shard_map/ppermute | solution.py:62
  15.2 13.6 %collective-permute-start = (bf16[1,1024,32]{1,2,0:T(8,128)(2,1)S(1)}, bf16[1,1024,32]{1,2,0:T(8,128)(2,1)S(1)}, u32[]{:S(2)}, u32[]{:S(2)}) collective-permute-start(bf16[1,1024,32]{1,2,0:T(8,128)(2,1)S(1)} %get-tuple-element.23), channel_id=1, source_target_pairs={{0,64},{64,0},{1,65},{65,1},{2,66},{66,2},{3,67},{67,3},{4,68},{68... | collective-permute-start | bytes 196616 | tf_op jit(solution)/shard_map/ppermute | solution.py:56
  24.1 2.6 %copy-start.1 = (bf16[128,8192]{1,0:T(8,128)(2,1)S(1)}, bf16[128,8192]{1,0:T(8,128)(2,1)}, u32[]{:S(2)}) copy-start(bf16[128,8192]{1,0:T(8,128)(2,1)} %get-tuple-element.8) | copy-start | bytes 6291460
  30.3 22.8 %all-to-all-start.1 = ((bf16[64,2,512]{2,1,0:T(2,128)(2,1)}), bf16[64,2,512]{2,1,0:T(2,128)(2,1)S(1)}, u32[]{:S(2)}, u32[]{:S(2)}) async-start(bf16[64,2,512]{2,1,0:T(2,128)(2,1)} %reshape.92), calls=%async_computation.1 | async-start | bytes 262144 | tf_op jit(solution)/shard_map/all_to_all | solution.py:57
  53.1 61.0 %all-to-all-start = ((bf16[128,2,16,512]{3,2,1,0:T(8,128)(2,1)}), bf16[128,2,16,512]{3,2,1,0:T(8,128)(2,1)}, u32[]{:S(2)}, u32[]{:S(2)}) async-start(bf16[128,2,16,512]{3,2,1,0:T(8,128)(2,1)} %pad_maximum_fusion), calls=%async_computation | async-start | bytes 8388608 | tf_op jit(solution)/shard_map/all_to_all | solution.py:70
  119.9 9.2 %copy-start.3 = (bf16[128,640]{1,0:T(8,128)(2,1)S(1)}, bf16[128,640]{1,0:T(8,128)(2,1)}, u32[]{:S(2)}) copy-start(bf16[128,640]{1,0:T(8,128)(2,1)} %param.16) | copy-start | bytes 491524
  119.9 40.2 %all-to-all-start.2 = ((bf16[128,16,512]{2,1,0:T(8,128)(2,1)}), bf16[128,16,512]{2,1,0:T(8,128)(2,1)S(1)}, u32[]{:S(2)}, u32[]{:S(2)}) async-start(bf16[128,16,512]{2,1,0:T(8,128)(2,1)} %bitcast.59), calls=%async_computation.2 | async-start | bytes 4194304 | tf_op jit(solution)/shard_map/all_to_all | solution.py:77
Sparse Core Ops, SparseCore 0:
  15.3 111.0 all-gather.2

commit v8 on v6

--- a/solution.py
+++ b/solution.py
@@ -64,11 +64,9 @@
     return left_gathered, right_gathered
 
 
-def send_whole(tri_left, tri_right):
+def send_whole(tri_stack):
     both = ("branch", "rows")
-    moved = lax.all_to_all(
-        jnp.stack([tri_left, tri_right], axis=1), both, split_axis=0, concat_axis=0, tiled=True
-    )
+    moved = lax.all_to_all(tri_stack, both, split_axis=0, concat_axis=0, tiled=True)
     return moved
 
 
@@ -76,47 +74,50 @@
     return lax.all_to_all(product, ("branch", "rows"), split_axis=0, concat_axis=0, tiled=True)
 
 
-def front_kernel(pair_ref, wt_ref, left_ref, right_ref):
-    rows, columns, chans = pair_ref.shape
-    for r in range(rows):
-        pair_norm = standardize_features(pair_ref[r].astype(jnp.float32), -1).astype(jnp.bfloat16)
+def front_kernel(pair_ref, w_ref, out_ref, norm_ref):
+    tile_rows, columns, chans = pair_ref.shape
+    block = out_ref.shape[0]
+
+    @pl.when(pl.program_id(0) == 0)
+    def _():
+        for r in range(tile_rows):
+            norm_ref[r] = standardize_features(pair_ref[r].astype(jnp.float32), -1).astype(
+                norm_ref.dtype
+            )
+
+    weight = w_ref[...].reshape(4 * block, chans)
+    for r in range(tile_rows):
         proj = lax.dot_general(
-            wt_ref[...], pair_norm, (((1,), (1,)), ((), ())), preferred_element_type=jnp.float32
+            weight, norm_ref[r], (((1,), (1,)), ((), ())), preferred_element_type=jnp.float32
         )
-        cols = slice(r * columns, (r + 1) * columns)
-        left_ref[:, cols] = (
-            jax.nn.sigmoid(proj[chans : 2 * chans]) * proj[:chans]
-        ).astype(left_ref.dtype)
-        right_ref[:, cols] = (
-            jax.nn.sigmoid(proj[3 * chans :]) * proj[2 * chans : 3 * chans]
-        ).astype(right_ref.dtype)
+        out_ref[:, 0, r, :] = (
+            jax.nn.sigmoid(proj[block : 2 * block]) * proj[:block]
+        ).astype(out_ref.dtype)
+        out_ref[:, 1, r, :] = (
+            jax.nn.sigmoid(proj[3 * block :]) * proj[2 * block : 3 * block]
+        ).astype(out_ref.dtype)
 
 
 def pair_front(pairwise_input, triangle_projection_weight):
     tile_rows, columns, chans = pairwise_input.shape
-    step_rows = 4
-    weight_t = triangle_projection_weight[:, : 4 * chans].T
-    side = jax.ShapeDtypeStruct((chans, tile_rows * columns), jnp.bfloat16)
-    out_block = pl.BlockSpec((chans, step_rows * columns), lambda g: (0, g))
-    tri_left, tri_right = pl.pallas_call(
+    block = 32
+    weight = triangle_projection_weight[:, : 4 * chans].T.reshape(4, chans, chans)
+    return pl.pallas_call(
         front_kernel,
-        out_shape=(side, side),
-        grid=(tile_rows // step_rows,),
+        out_shape=jax.ShapeDtypeStruct((chans, 2, tile_rows, columns), jnp.bfloat16),
+        grid=(chans // block,),
         in_specs=[
-            pl.BlockSpec((step_rows, columns, chans), lambda g: (g, 0, 0)),
-            pl.BlockSpec((4 * chans, chans), lambda g: (0, 0)),
+            pl.BlockSpec((tile_rows, columns, chans), lambda g: (0, 0, 0)),
+            pl.BlockSpec((4, block, chans), lambda g: (0, g, 0)),
         ],
-        out_specs=(out_block, out_block),
+        out_specs=pl.BlockSpec((block, 2, tile_rows, columns), lambda g: (g, 0, 0, 0)),
+        scratch_shapes=[pltpu.VMEM((tile_rows, columns, chans), jnp.bfloat16)],
         cost_estimate=pl.CostEstimate(
             flops=2 * tile_rows * columns * chans * 4 * chans,
             transcendentals=2 * tile_rows * columns * chans,
             bytes_accessed=tile_rows * columns * chans * 6,
         ),
-    )(pairwise_input, weight_t)
-    return (
-        tri_left.reshape(chans, tile_rows, columns),
-        tri_right.reshape(chans, tile_rows, columns),
-    )
+    )(pairwise_input, weight)
 
 
 def product_kernel(moved_ref, out_ref):
@@ -285,10 +286,8 @@
     )
     left_gathered, right_gathered = gather_sides(left_side, right_side)
     pairwise_input, right_side = lax.optimization_barrier((pairwise_input, right_side))
-    tri_left, tri_right = pair_front(
-        pairwise_input, triangle_projection_weight
-    )
-    moved = send_whole(tri_left, tri_right)
+    tri_stack = pair_front(pairwise_input, triangle_projection_weight)
+    moved = send_whole(tri_stack)
     product = triangle_product(moved)
     product, left_gathered = lax.optimization_barrier((product, left_gathered))
     product_tile = send_back(product)

time: 186 us -> 184 us (0.989)
  Pallas kernels: 48.9 us -> 54.4 us
  local copies, waits for them, and re-layouts: 23.6 us -> 18.8 us
  starting transfers between devices: 28.6 us -> 33.1 us
  waiting for transfers between devices: 63.1 us -> 59.1 us
  other arithmetic: 5.03 us -> 1.09 us
    all_to_all x1, waiting for transfers between devices: 6.06 us -> 0.01 us  [gather_sides(): lax.all_to_all(left_pair, 'rows', split_axis=1, concat_axis=0, tiled=True)]
    unnamed x20 -> x13, local copies, waits for them, and re-layouts: 12.9 us -> 7.41 us
    pallas_call x1, Pallas kernels: 6.53 us -> 12 us  [pair_front(): pl.pallas_call(front_kernel, out_shape=jax.ShapeDtypeStruct((chans, 2, ti...]
    all_to_all x1, starting transfers between devices: 4.94 us -> 9.84 us  [send_whole(): lax.all_to_all(tri_stack, both, split_axis=0, concat_axis=0, tiled=True)]
    another operation x1 -> x0, other arithmetic: 3.94 us -> none  [send_whole(): jnp.stack([tri_left, tri_right], axis=1)]
  transfers between devices with their start and end apart: 6 -> 6, of which waited for: 3 -> 3; matrix products, arithmetic and copies ran while one was open for 13% -> 8% of each run, Pallas kernels for 17% -> 21%
where the time goes in v8:
time: 184 us; the launch traced here: 183 us
  waiting for transfers between devices  59.1 us (32%)
  Pallas kernels  54.4 us (30%)
  starting transfers between devices  33.1 us (18%)
  local copies, waits for them, and re-layouts  18.8 us (10%)
  between operations  14.2 us (8%)
  matrix products  2.65 us (1%)
    all_to_all x1, waiting for transfers between devices, send_whole(): lax.all_to_all(tri_stack, both, split_axis=0, concat_axis=0, tiled=True)  56.1 us
    pallas_call x1, Pallas kernels, outer_product(): pl.pallas_call(outer_kernel, out_shape=jax.ShapeDtypeStruct((tile_rows, c...  19.9 us
    pallas_call x1, Pallas kernels, pair_back(): pl.pallas_call(back_kernel, out_shape=jax.ShapeDtypeStruct((tile_rows, co...  16.6 us
    all_to_all x1, starting transfers between devices, gather_sides(): lax.all_to_all(left_pair, 'rows', split_axis=1, concat_axis=0, tiled=True)  14.1 us
    pallas_call x1, Pallas kernels, pair_front(): pl.pallas_call(front_kernel, out_shape=jax.ShapeDtypeStruct((chans, 2, ti...  12 us
    all_to_all x1, starting transfers between devices, send_whole(): lax.all_to_all(tri_stack, both, split_axis=0, concat_axis=0, tiled=True)  9.84 us
    unnamed x13, local copies, waits for them, and re-layouts  7.41 us
    all_gather x1, local copies, waits for them, and re-layouts, gather_sides(): lax.all_gather(jnp.swapaxes(right_pair, 0, 1), 'rows', axis=1, tiled=True)  6.5 us
  transfers between devices with their start and end apart: 6, of which 3 were waited for; matrix products, arithmetic and copies ran while one was open for 8% of the time, Pallas kernels for 21%

profile of v8, /device:TPU:1, one launch (start us, length us, event | category | flops | bytes accessed | tf_op | source)
XLA Modules:
  0.0 183.5 jit_solution(12970962192663781916)
XLA Ops:
  7.2 0.0 copy-start
  7.2 0.0 all-gather.2.cloned.1.call-start
  7.2 1.3 copy.33
  8.5 0.0 copy-start.3
  8.5 0.1 convert_reduce_fusion
  8.6 0.2 fusion.8
  8.8 0.0 copy-done
  8.8 0.0 copy-start.2
  8.8 2.4 %convert_reduce_fusion.1 = (f32[1024]{0:T(1024)S(1)}, bf16[1,1024,256]{1,2,0:T(8,128)(2,1)S(1)}) fusion(bf16[1024,256]{1,0:T(8,128)(2,1)S(1)} %copy-done, bf16[256,1024]{1,0:T(8,128)(2,1)} %param.12, bf16[1,1024,256]{1,2,0:T(8,128)(2,1)S(1)} %copy.33, f32[1024]{0:T(1024)S(1)} %add_rsqrt_fusion.1, f32[1024]{0:T(1024)S(1)} %broadcast_multiply_fusion.1), kind=kOutput, calls=%fused_computation.7 | convolution fusion | flops 1078197248 | bytes 2109440 | tf_op jit(solution)/shard_map/dot_general | solution.py:31
  11.2 0.0 copy-start.1
  11.3 0.2 fusion.10
  11.4 0.0 copy-done.3
  11.4 0.3 fusion.7
  11.7 2.2 %collective-permute-start.1 = (bf16[1,32,512]{2,1,0:T(8,128)(2,1)S(1)}, bf16[1,32,512]{2,1,0:T(8,128)(2,1)S(1)}, u32[]{:S(2)}, u32[]{:S(2)}) collective-permute-start(bf16[1,32,512]{2,1,0:T(8,128)(2,1)S(1)} %get-tuple-element.21), channel_id=1, source_target_pairs={{0,64},{64,0},{1,65},{65,1},{2,66},{66,2},{3,67},{67,3},{4,68},{68... | collective-permute-start | bytes 98312 | tf_op jit(solution)/shard_map/ppermute | solution.py:62
  14.0 1.3 collective-permute-done.1
  15.3 0.6 fusion.23
  15.9 0.0 all-gather.2.cloned.1.call-update
  15.9 1.5 collective-permute-start
  17.5 1.7 collective-permute-done
  19.1 0.4 copy.35
  19.5 1.1 reshape.89
  20.6 14.1 %all-to-all-start.1 = ((bf16[64,2,512]{2,1,0:T(2,128)(2,1)}), bf16[64,2,512]{2,1,0:T(2,128)(2,1)S(1)}, u32[]{:S(2)}, u32[]{:S(2)}) async-start(bf16[64,2,512]{2,1,0:T(2,128)(2,1)} %reshape.89), calls=%async_computation.1 | async-start | bytes 262144 | tf_op jit(solution)/shard_map/all_to_all | solution.py:57
  34.7 0.0 copy-done.2
  34.7 0.8 copy.34
  35.5 12.0 %shard_map.113 = bf16[128,2,16,512]{3,2,1,0:T(8,128)(2,1)} custom-call(bf16[16,512,128]{2,1,0:T(8,128)(2,1)} %pair_ref.1, bf16[4,128,128]{2,1,0:T(8,128)(2,1)} %bitcast.53), custom_call_target="tpu_custom_call" | custom-call | flops 1073741824 | bytes 6291456 | tf_op jit(solution)/shard_map/pallas_call | solution.py:105
  47.5 0.0 copy-done.1
  47.5 0.0 all-to-all-done.1
  47.5 9.8 %all-to-all-start = ((bf16[128,2,16,512]{3,2,1,0:T(8,128)(2,1)}), bf16[128,2,16,512]{3,2,1,0:T(8,128)(2,1)}, u32[]{:S(2)}, u32[]{:S(2)}) async-start(bf16[128,2,16,512]{3,2,1,0:T(8,128)(2,1)} %shard_map.113), calls=%async_computation | async-start | bytes 8388608 | tf_op jit(solution)/shard_map/all_to_all | solution.py:69
  57.4 0.3 reshape.90
  57.7 0.1 copy.36
  57.8 56.1 %all-to-all-done.moved_ref = bf16[128,2,16,512]{3,2,1,0:T(8,128)(2,1)} async-done(((bf16[128,2,16,512]{3,2,1,0:T(8,128)(2,1)}), bf16[128,2,16,512]{3,2,1,0:T(8,128)(2,1)}, u32[]{:S(2)}, u32[]{:S(2)}) %all-to-all-start) | async-done | bytes 4194336 | tf_op jit(solution)/shard_map/all_to_all | solution.py:69
  113.9 5.9 %shard_map.114 = bf16[2,1024,512]{2,1,0:T(8,128)(2,1)} custom-call(bf16[128,2,16,512]{3,2,1,0:T(8,128)(2,1)} %all-to-all-done.moved_ref), custom_call_target="tpu_custom_call" | custom-call | flops 2147483648 | bytes 6291456 | tf_op jit(solution)/shard_map/pallas_call | solution.py:147
  119.8 5.4 %all-to-all-start.2 = ((bf16[128,16,512]{2,1,0:T(8,128)(2,1)}), bf16[128,16,512]{2,1,0:T(8,128)(2,1)S(1)}, u32[]{:S(2)}, u32[]{:S(2)}) async-start(bf16[128,16,512]{2,1,0:T(8,128)(2,1)} %bitcast.49), calls=%async_computation.2 | async-start | bytes 4194304 | tf_op jit(solution)/shard_map/all_to_all | solution.py:74
  125.3 2.0 %copy.42 = bf16[1,1024,256]{2,1,0:T(8,128)(2,1)} copy(bf16[1,1024,256]{1,2,0:T(8,128)(2,1)} %copy-done.1) | data formatting | bytes 1048576
  127.3 0.6 slice.17.wg_ref
  127.9 1.1 copy.39
  129.0 0.9 copy.40
  129.9 1.1 copy.38
  130.9 0.0 all-gather.2.cloned.1.call-done
  130.9 6.5 %copy.41.r_ref = bf16[32,128,512]{2,1,0:T(8,128)(2,1)} copy(bf16[32,128,512]{2,0,1:T(8,128)(2,1)} %all-gather.2.cloned.1.call-done) | data formatting | bytes 8388608 | tf_op jit(solution)/shard_map/all_gather | solution.py:63
  137.4 19.9 %shard_map.115.outer_ref = f32[16,512,128]{2,1,0:T(8,128)} custom-call(bf16[512,128]{1,0:T(8,128)(2,1)} %bitcast.56, bf16[32,128,512]{2,1,0:T(8,128)(2,1)} %copy.41.r_ref, bf16[128,1024]{1,0:T(8,128)(2,1)} %bitcast.55), custom_call_target="tpu_custom_call" | custom-call | flops 4294967296 | bytes 8388608 | tf_op jit(solution)/shard_map/pallas_call | solution.py:259
  157.4 0.0 all-to-all-done.2
  157.4 2.7 %copy.43 = bf16[16,8,16,512]{3,1,2,0:T(8,128)(2,1)} copy(bf16[16,8,16,512]{3,2,1,0:T(8,128)(2,1)S(1)} %bitcast.45) | data formatting | bytes 4194304
  160.0 16.6 %shard_map.116 = bf16[16,512,128]{2,1,0:T(8,128)(2,1)} custom-call(bf16[128,8192]{1,0:T(8,128)(2,1)} %bitcast.50, bf16[16,512,128]{2,1,0:T(8,128)(2,1)} %pair_ref.1, f32[16,512,128]{2,1,0:T(8,128)} %shard_map.115.outer_ref, bf16[128,128]{1,0:T(8,128)(2,1)} %wo_ref.1, bf16[128,128]{1,0:T(8,128)(2,1)} %slice.17.wg_ref, bf16[128,512]{1,0:T(8,128)(2,1)} %wu_ref.1, ...), custom_call_target="tpu_custom_call" | custom-call | flops 2952790016 | bytes 10485760 | tf_op jit(solution)/shard_map/pallas_call | solution.py:197
  (9 shorter events, 0.1 us)
Async XLA Ops:
  7.2 1.7 copy-start
  7.2 123.8 %all-gather.2.cloned.1.call-start = ((), (), s32[]{:S(2)}) async-start(), calls=%async_computation.3 | async-start | bytes 4259840 | tf_op jit(solution)/shard_map/all_gather | solution.py:63
  8.5 2.9 %copy-start.3 = (bf16[256,64]{0,1:T(8,128)(2,1)S(1)}, bf16[256,64]{0,1:T(8,128)(2,1)}, u32[]{:S(2)}) copy-start(bf16[256,64]{0,1:T(8,128)(2,1)} %param.14) | copy-start | bytes 98308
  8.8 25.9 %copy-start.2 = (bf16[128,640]{1,0:T(8,128)(2,1)S(1)}, bf16[128,640]{1,0:T(8,128)(2,1)}, u32[]{:S(2)}) copy-start(bf16[128,640]{1,0:T(8,128)(2,1)} %param.16) | copy-start | bytes 491524
  11.2 36.3 %copy-start.1 = (bf16[1,1024,256]{1,2,0:T(8,128)(2,1)}, bf16[1,1024,256]{1,2,0:T(8,128)(2,1)S(1)}, u32[]{:S(2)}) copy-start(bf16[1,1024,256]{1,2,0:T(8,128)(2,1)S(1)} %get-tuple-element.23) | copy-start | bytes 1572868
  11.7 3.5 %collective-permute-start.1 = (bf16[1,32,512]{2,1,0:T(8,128)(2,1)S(1)}, bf16[1,32,512]{2,1,0:T(8,128)(2,1)S(1)}, u32[]{:S(2)}, u32[]{:S(2)}) collective-permute-start(bf16[1,32,512]{2,1,0:T(8,128)(2,1)S(1)} %get-tuple-element.21), channel_id=1, source_target_pairs={{0,64},{64,0},{1,65},{65,1},{2,66},{66,2},{3,67},{67,3},{4,68},{68... | collective-permute-start | bytes 98312 | tf_op jit(solution)/shard_map/ppermute | solution.py:62
  15.9 3.2 %collective-permute-start = (bf16[1,1024,32]{1,2,0:T(8,128)(2,1)S(1)}, bf16[1,1024,32]{1,2,0:T(8,128)(2,1)S(1)}, u32[]{:S(2)}, u32[]{:S(2)}) collective-permute-start(bf16[1,1024,32]{1,2,0:T(8,128)(2,1)S(1)} %get-tuple-element.19), channel_id=1, source_target_pairs={{0,64},{64,0},{1,65},{65,1},{2,66},{66,2},{3,67},{67,3},{4,68},{68... | collective-permute-start | bytes 196616 | tf_op jit(solution)/shard_map/ppermute | solution.py:56
  20.6 26.9 %all-to-all-start.1 = ((bf16[64,2,512]{2,1,0:T(2,128)(2,1)}), bf16[64,2,512]{2,1,0:T(2,128)(2,1)S(1)}, u32[]{:S(2)}, u32[]{:S(2)}) async-start(bf16[64,2,512]{2,1,0:T(2,128)(2,1)} %reshape.89), calls=%async_computation.1 | async-start | bytes 262144 | tf_op jit(solution)/shard_map/all_to_all | solution.py:57
  47.5 66.4 %all-to-all-start = ((bf16[128,2,16,512]{3,2,1,0:T(8,128)(2,1)}), bf16[128,2,16,512]{3,2,1,0:T(8,128)(2,1)}, u32[]{:S(2)}, u32[]{:S(2)}) async-start(bf16[128,2,16,512]{3,2,1,0:T(8,128)(2,1)} %shard_map.113), calls=%async_computation | async-start | bytes 8388608 | tf_op jit(solution)/shard_map/all_to_all | solution.py:69
  119.8 37.5 %all-to-all-start.2 = ((bf16[128,16,512]{2,1,0:T(8,128)(2,1)}), bf16[128,16,512]{2,1,0:T(8,128)(2,1)S(1)}, u32[]{:S(2)}, u32[]{:S(2)}) async-start(bf16[128,16,512]{2,1,0:T(8,128)(2,1)} %bitcast.49), calls=%async_computation.2 | async-start | bytes 4194304 | tf_op jit(solution)/shard_map/all_to_all | solution.py:74
Sparse Core Ops, SparseCore 0:
  16.0 109.4 all-gather.1

commit v9 on v8

--- a/solution.py
+++ b/solution.py
@@ -74,6 +74,10 @@
     return lax.all_to_all(product, ("branch", "rows"), split_axis=0, concat_axis=0, tiled=True)
 
 
+def logistic(values):
+    return 0.5 * jnp.tanh(0.5 * values) + 0.5
+
+
 def front_kernel(pair_ref, w_ref, out_ref, norm_ref):
     tile_rows, columns, chans = pair_ref.shape
     block = out_ref.shape[0]
@@ -91,10 +95,10 @@
             weight, norm_ref[r], (((1,), (1,)), ((), ())), preferred_element_type=jnp.float32
         )
         out_ref[:, 0, r, :] = (
-            jax.nn.sigmoid(proj[block : 2 * block]) * proj[:block]
+            logistic(proj[block : 2 * block]) * proj[:block]
         ).astype(out_ref.dtype)
         out_ref[:, 1, r, :] = (
-            jax.nn.sigmoid(proj[3 * block :]) * proj[2 * block : 3 * block]
+            logistic(proj[3 * block :]) * proj[2 * block : 3 * block]
         ).astype(out_ref.dtype)
 
 
@@ -166,7 +170,7 @@
         tri_update = jnp.dot(prod_norm, wo_ref[...], preferred_element_type=jnp.float32)
         pair_float = pair_ref[r].astype(jnp.float32)
         pair_norm = standardize_features(pair_float, -1).astype(jnp.bfloat16)
-        gate = jax.nn.sigmoid(
+        gate = logistic(
             jnp.dot(pair_norm, wg_ref[...], preferred_element_type=jnp.float32)
         )
         pair_mid = pair_float + gate * tri_update

time: 184 us -> 184 us (level)
  waiting for transfers between devices: 59.1 us -> 56.3 us
    all_to_all x1, waiting for transfers between devices: 56.1 us -> 53.3 us  [send_whole(): lax.all_to_all(tri_stack, both, split_axis=0, concat_axis=0, tiled=True)]
where the time goes in v9:
time: 184 us; the launch traced here: 183 us
  waiting for transfers between devices  56.3 us (31%)
  Pallas kernels  55.4 us (30%)
  starting transfers between devices  34.5 us (19%)
  local copies, waits for them, and re-layouts  18.8 us (10%)
  between operations  14.2 us (8%)
  matrix products  2.65 us (1%)
    all_to_all x1, waiting for transfers between devices, send_whole(): lax.all_to_all(tri_stack, both, split_axis=0, concat_axis=0, tiled=True)  53.3 us
    pallas_call x1, Pallas kernels, outer_product(): pl.pallas_call(outer_kernel, out_shape=jax.ShapeDtypeStruct((tile_rows, c...  19.9 us
    pallas_call x1, Pallas kernels, pair_back(): pl.pallas_call(back_kernel, out_shape=jax.ShapeDtypeStruct((tile_rows, co...  17.1 us
    all_to_all x1, starting transfers between devices, gather_sides(): lax.all_to_all(left_pair, 'rows', split_axis=1, concat_axis=0, tiled=True)  14.1 us
    pallas_call x1, Pallas kernels, pair_front(): pl.pallas_call(front_kernel, out_shape=jax.ShapeDtypeStruct((chans, 2, ti...  12.4 us
    all_to_all x1, starting transfers between devices, send_whole(): lax.all_to_all(tri_stack, both, split_axis=0, concat_axis=0, tiled=True)  9.84 us
    unnamed x13, local copies, waits for them, and re-layouts  7.41 us
    all_to_all x1, starting transfers between devices, send_back(): lax.all_to_all(product, ('branch', 'rows'), split_axis=0, concat_axis=0,...  6.84 us
  transfers between devices with their start and end apart: 6, of which 3 were waited for; matrix products, arithmetic and copies ran while one was open for 8% of the time, Pallas kernels for 21%

profile of v9, /device:TPU:1, one launch (start us, length us, event | category | flops | bytes accessed | tf_op | source)
XLA Modules:
  0.0 183.1 jit_solution(8133343621091817595)
XLA Ops:
  7.2 0.0 copy-start
  7.2 0.0 all-gather.2.cloned.1.call-start
  7.2 1.3 copy.33
  8.5 0.0 copy-start.3
  8.5 0.1 convert_reduce_fusion
  8.6 0.2 fusion.8
  8.8 0.0 copy-done
  8.8 0.0 copy-start.2
  8.8 2.4 %convert_reduce_fusion.1 = (f32[1024]{0:T(1024)S(1)}, bf16[1,1024,256]{1,2,0:T(8,128)(2,1)S(1)}) fusion(bf16[1024,256]{1,0:T(8,128)(2,1)S(1)} %copy-done, bf16[256,1024]{1,0:T(8,128)(2,1)} %param.12, bf16[1,1024,256]{1,2,0:T(8,128)(2,1)S(1)} %copy.33, f32[1024]{0:T(1024)S(1)} %add_rsqrt_fusion.1, f32[1024]{0:T(1024)S(1)} %broadcast_multiply_fusion.1), kind=kOutput, calls=%fused_computation.7 | convolution fusion | flops 1078197248 | bytes 2109440 | tf_op jit(solution)/shard_map/dot_general | solution.py:31
  11.2 0.0 copy-start.1
  11.3 0.2 fusion.10
  11.4 0.0 copy-done.3
  11.4 0.3 fusion.7
  11.7 2.2 %collective-permute-start.1 = (bf16[1,32,512]{2,1,0:T(8,128)(2,1)S(1)}, bf16[1,32,512]{2,1,0:T(8,128)(2,1)S(1)}, u32[]{:S(2)}, u32[]{:S(2)}) collective-permute-start(bf16[1,32,512]{2,1,0:T(8,128)(2,1)S(1)} %get-tuple-element.21), channel_id=1, source_target_pairs={{0,64},{64,0},{1,65},{65,1},{2,66},{66,2},{3,67},{67,3},{4,68},{68... | collective-permute-start | bytes 98312 | tf_op jit(solution)/shard_map/ppermute | solution.py:62
  14.0 1.3 collective-permute-done.1
  15.3 0.6 fusion.23
  15.9 0.0 all-gather.2.cloned.1.call-update
  15.9 1.5 collective-permute-start
  17.5 1.7 collective-permute-done
  19.1 0.4 copy.35
  19.5 1.1 reshape.89
  20.6 14.1 %all-to-all-start.1 = ((bf16[64,2,512]{2,1,0:T(2,128)(2,1)}), bf16[64,2,512]{2,1,0:T(2,128)(2,1)S(1)}, u32[]{:S(2)}, u32[]{:S(2)}) async-start(bf16[64,2,512]{2,1,0:T(2,128)(2,1)} %reshape.89), calls=%async_computation.1 | async-start | bytes 262144 | tf_op jit(solution)/shard_map/all_to_all | solution.py:57
  34.7 0.0 copy-done.2
  34.7 0.8 copy.34
  35.5 12.4 %shard_map.113 = bf16[128,2,16,512]{3,2,1,0:T(8,128)(2,1)} custom-call(bf16[16,512,128]{2,1,0:T(8,128)(2,1)} %pair_ref.1, bf16[4,128,128]{2,1,0:T(8,128)(2,1)} %bitcast.53), custom_call_target="tpu_custom_call" | custom-call | flops 1073741824 | bytes 6291456 | tf_op jit(solution)/shard_map/pallas_call | solution.py:109
  47.9 0.0 copy-done.1
  48.0 0.0 all-to-all-done.1
  48.0 9.8 %all-to-all-start = ((bf16[128,2,16,512]{3,2,1,0:T(8,128)(2,1)}), bf16[128,2,16,512]{3,2,1,0:T(8,128)(2,1)}, u32[]{:S(2)}, u32[]{:S(2)}) async-start(bf16[128,2,16,512]{3,2,1,0:T(8,128)(2,1)} %shard_map.113), calls=%async_computation | async-start | bytes 8388608 | tf_op jit(solution)/shard_map/all_to_all | solution.py:69
  57.8 0.3 reshape.90
  58.1 0.1 copy.36
  58.2 53.3 %all-to-all-done.moved_ref = bf16[128,2,16,512]{3,2,1,0:T(8,128)(2,1)} async-done(((bf16[128,2,16,512]{3,2,1,0:T(8,128)(2,1)}), bf16[128,2,16,512]{3,2,1,0:T(8,128)(2,1)}, u32[]{:S(2)}, u32[]{:S(2)}) %all-to-all-start) | async-done | bytes 4194336 | tf_op jit(solution)/shard_map/all_to_all | solution.py:69
  111.5 5.9 %shard_map.114 = bf16[2,1024,512]{2,1,0:T(8,128)(2,1)} custom-call(bf16[128,2,16,512]{3,2,1,0:T(8,128)(2,1)} %all-to-all-done.moved_ref), custom_call_target="tpu_custom_call" | custom-call | flops 2147483648 | bytes 6291456 | tf_op jit(solution)/shard_map/pallas_call | solution.py:151
  117.5 6.8 %all-to-all-start.2 = ((bf16[128,16,512]{2,1,0:T(8,128)(2,1)}), bf16[128,16,512]{2,1,0:T(8,128)(2,1)S(1)}, u32[]{:S(2)}, u32[]{:S(2)}) async-start(bf16[128,16,512]{2,1,0:T(8,128)(2,1)} %bitcast.49), calls=%async_computation.2 | async-start | bytes 4194304 | tf_op jit(solution)/shard_map/all_to_all | solution.py:74
  124.3 2.0 %copy.42 = bf16[1,1024,256]{2,1,0:T(8,128)(2,1)} copy(bf16[1,1024,256]{1,2,0:T(8,128)(2,1)} %copy-done.1) | data formatting | bytes 1048576
  126.4 0.6 slice.17.wg_ref
  127.0 1.1 copy.39
  128.0 0.9 copy.40
  128.9 1.1 copy.38
  130.0 0.0 all-gather.2.cloned.1.call-done
  130.0 6.5 %copy.41.r_ref = bf16[32,128,512]{2,1,0:T(8,128)(2,1)} copy(bf16[32,128,512]{2,0,1:T(8,128)(2,1)} %all-gather.2.cloned.1.call-done) | data formatting | bytes 8388608 | tf_op jit(solution)/shard_map/all_gather | solution.py:63
  136.5 19.9 %shard_map.115.outer_ref = f32[16,512,128]{2,1,0:T(8,128)} custom-call(bf16[512,128]{1,0:T(8,128)(2,1)} %bitcast.56, bf16[32,128,512]{2,1,0:T(8,128)(2,1)} %copy.41.r_ref, bf16[128,1024]{1,0:T(8,128)(2,1)} %bitcast.55), custom_call_target="tpu_custom_call" | custom-call | flops 4294967296 | bytes 8388608 | tf_op jit(solution)/shard_map/pallas_call | solution.py:263
  156.4 0.0 all-to-all-done.2
  156.4 2.7 %copy.43 = bf16[16,8,16,512]{3,1,2,0:T(8,128)(2,1)} copy(bf16[16,8,16,512]{3,2,1,0:T(8,128)(2,1)S(1)} %bitcast.45) | data formatting | bytes 4194304
  159.1 17.1 %shard_map.116 = bf16[16,512,128]{2,1,0:T(8,128)(2,1)} custom-call(bf16[128,8192]{1,0:T(8,128)(2,1)} %bitcast.50, bf16[16,512,128]{2,1,0:T(8,128)(2,1)} %pair_ref.1, f32[16,512,128]{2,1,0:T(8,128)} %shard_map.115.outer_ref, bf16[128,128]{1,0:T(8,128)(2,1)} %wo_ref.1, bf16[128,128]{1,0:T(8,128)(2,1)} %slice.17.wg_ref, bf16[128,512]{1,0:T(8,128)(2,1)} %wu_ref.1, ...), custom_call_target="tpu_custom_call" | custom-call | flops 2952790016 | bytes 10485760 | tf_op jit(solution)/shard_map/pallas_call | solution.py:201
  (9 shorter events, 0.1 us)
Async XLA Ops:
  7.2 1.7 copy-start
  7.2 122.8 %all-gather.2.cloned.1.call-start = ((), (), s32[]{:S(2)}) async-start(), calls=%async_computation.3 | async-start | bytes 4259840 | tf_op jit(solution)/shard_map/all_gather | solution.py:63
  8.5 2.9 %copy-start.3 = (bf16[256,64]{0,1:T(8,128)(2,1)S(1)}, bf16[256,64]{0,1:T(8,128)(2,1)}, u32[]{:S(2)}) copy-start(bf16[256,64]{0,1:T(8,128)(2,1)} %param.14) | copy-start | bytes 98308
  8.8 25.9 %copy-start.2 = (bf16[128,640]{1,0:T(8,128)(2,1)S(1)}, bf16[128,640]{1,0:T(8,128)(2,1)}, u32[]{:S(2)}) copy-start(bf16[128,640]{1,0:T(8,128)(2,1)} %param.16) | copy-start | bytes 491524
  11.2 36.7 %copy-start.1 = (bf16[1,1024,256]{1,2,0:T(8,128)(2,1)}, bf16[1,1024,256]{1,2,0:T(8,128)(2,1)S(1)}, u32[]{:S(2)}) copy-start(bf16[1,1024,256]{1,2,0:T(8,128)(2,1)S(1)} %get-tuple-element.23) | copy-start | bytes 1572868
  11.7 3.5 %collective-permute-start.1 = (bf16[1,32,512]{2,1,0:T(8,128)(2,1)S(1)}, bf16[1,32,512]{2,1,0:T(8,128)(2,1)S(1)}, u32[]{:S(2)}, u32[]{:S(2)}) collective-permute-start(bf16[1,32,512]{2,1,0:T(8,128)(2,1)S(1)} %get-tuple-element.21), channel_id=1, source_target_pairs={{0,64},{64,0},{1,65},{65,1},{2,66},{66,2},{3,67},{67,3},{4,68},{68... | collective-permute-start | bytes 98312 | tf_op jit(solution)/shard_map/ppermute | solution.py:62
  15.9 3.2 %collective-permute-start = (bf16[1,1024,32]{1,2,0:T(8,128)(2,1)S(1)}, bf16[1,1024,32]{1,2,0:T(8,128)(2,1)S(1)}, u32[]{:S(2)}, u32[]{:S(2)}) collective-permute-start(bf16[1,1024,32]{1,2,0:T(8,128)(2,1)S(1)} %get-tuple-element.19), channel_id=1, source_target_pairs={{0,64},{64,0},{1,65},{65,1},{2,66},{66,2},{3,67},{67,3},{4,68},{68... | collective-permute-start | bytes 196616 | tf_op jit(solution)/shard_map/ppermute | solution.py:56
  20.6 27.3 %all-to-all-start.1 = ((bf16[64,2,512]{2,1,0:T(2,128)(2,1)}), bf16[64,2,512]{2,1,0:T(2,128)(2,1)S(1)}, u32[]{:S(2)}, u32[]{:S(2)}) async-start(bf16[64,2,512]{2,1,0:T(2,128)(2,1)} %reshape.89), calls=%async_computation.1 | async-start | bytes 262144 | tf_op jit(solution)/shard_map/all_to_all | solution.py:57
  48.0 63.6 %all-to-all-start = ((bf16[128,2,16,512]{3,2,1,0:T(8,128)(2,1)}), bf16[128,2,16,512]{3,2,1,0:T(8,128)(2,1)}, u32[]{:S(2)}, u32[]{:S(2)}) async-start(bf16[128,2,16,512]{3,2,1,0:T(8,128)(2,1)} %shard_map.113), calls=%async_computation | async-start | bytes 8388608 | tf_op jit(solution)/shard_map/all_to_all | solution.py:69
  117.5 38.9 %all-to-all-start.2 = ((bf16[128,16,512]{2,1,0:T(8,128)(2,1)}), bf16[128,16,512]{2,1,0:T(8,128)(2,1)S(1)}, u32[]{:S(2)}, u32[]{:S(2)}) async-start(bf16[128,16,512]{2,1,0:T(8,128)(2,1)} %bitcast.49), calls=%async_computation.2 | async-start | bytes 4194304 | tf_op jit(solution)/shard_map/all_to_all | solution.py:74
Sparse Core Ops, SparseCore 0:
  16.0 110.1 all-gather.1

commit v10 on v9

--- a/solution.py
+++ b/solution.py
@@ -78,7 +78,7 @@
     return 0.5 * jnp.tanh(0.5 * values) + 0.5
 
 
-def front_kernel(pair_ref, w_ref, out_ref, norm_ref):
+def front_kernel(pair_ref, w_ref, out_ref, norm_ref, left_ref, right_ref):
     tile_rows, columns, chans = pair_ref.shape
     block = out_ref.shape[0]
 
@@ -94,12 +94,10 @@
         proj = lax.dot_general(
             weight, norm_ref[r], (((1,), (1,)), ((), ())), preferred_element_type=jnp.float32
         )
-        out_ref[:, 0, r, :] = (
-            logistic(proj[block : 2 * block]) * proj[:block]
-        ).astype(out_ref.dtype)
-        out_ref[:, 1, r, :] = (
-            logistic(proj[3 * block :]) * proj[2 * block : 3 * block]
-        ).astype(out_ref.dtype)
+        left_ref[:, r, :] = logistic(proj[block : 2 * block]) * proj[:block]
+        right_ref[:, r, :] = logistic(proj[3 * block :]) * proj[2 * block : 3 * block]
+    out_ref[:, 0] = left_ref[...].astype(out_ref.dtype)
+    out_ref[:, 1] = right_ref[...].astype(out_ref.dtype)
 
 
 def pair_front(pairwise_input, triangle_projection_weight):
@@ -115,7 +113,11 @@
             pl.BlockSpec((4, block, chans), lambda g: (0, g, 0)),
         ],
         out_specs=pl.BlockSpec((block, 2, tile_rows, columns), lambda g: (g, 0, 0, 0)),
-        scratch_shapes=[pltpu.VMEM((tile_rows, columns, chans), jnp.bfloat16)],
+        scratch_shapes=[
+            pltpu.VMEM((tile_rows, columns, chans), jnp.bfloat16),
+            pltpu.VMEM((block, tile_rows, columns), jnp.float32),
+            pltpu.VMEM((block, tile_rows, columns), jnp.float32),
+        ],
         cost_estimate=pl.CostEstimate(
             flops=2 * tile_rows * columns * chans * 4 * chans,
             transcendentals=2 * tile_rows * columns * chans,

time: 184 us -> 206 us (1.12)
  the two profiles are of different devices: /device:TPU:1 before, /device:TPU:31 now
where the time goes in v10:
time: 206 us; the launch traced here: 205 us
  waiting for transfers between devices  82.1 us (40%)
  Pallas kernels  53.5 us (26%)
  starting transfers between devices  32.9 us (16%)
  local copies, waits for them, and re-layouts  18.8 us (9%)
  between operations  14.2 us (7%)
  matrix products  2.65 us (1%)
    all_to_all x1, waiting for transfers between devices, send_whole(): lax.all_to_all(tri_stack, both, split_axis=0, concat_axis=0, tiled=True)  51.1 us
    all_gather x1, waiting for transfers between devices, gather_sides(): lax.all_gather(jnp.swapaxes(right_pair, 0, 1), 'rows', axis=1, tiled=True)  26 us
    pallas_call x1, Pallas kernels, outer_product(): pl.pallas_call(outer_kernel, out_shape=jax.ShapeDtypeStruct((tile_rows, c...  19.9 us
    pallas_call x1, Pallas kernels, pair_back(): pl.pallas_call(back_kernel, out_shape=jax.ShapeDtypeStruct((tile_rows, co...  17.1 us
    all_to_all x1, starting transfers between devices, gather_sides(): lax.all_to_all(left_pair, 'rows', split_axis=1, concat_axis=0, tiled=True)  14.1 us
    pallas_call x1, Pallas kernels, pair_front(): pl.pallas_call(front_kernel, out_shape=jax.ShapeDtypeStruct((chans, 2, ti...  10.5 us
    all_to_all x1, starting transfers between devices, send_whole(): lax.all_to_all(tri_stack, both, split_axis=0, concat_axis=0, tiled=True)  9.56 us
    all_to_all x1, starting transfers between devices, send_back(): lax.all_to_all(product, ('branch', 'rows'), split_axis=0, concat_axis=0,...  8.15 us
  transfers between devices with their start and end apart: 6, of which 4 were waited for; matrix products, arithmetic and copies ran while one was open for 7% of the time, Pallas kernels for 18%

profile of v10, /device:TPU:31, one launch (start us, length us, event | category | flops | bytes accessed | tf_op | source)
XLA Modules:
  0.0 205.3 jit_solution(5875034491199636388)
XLA Ops:
  7.2 0.0 copy-start
  7.2 0.0 all-gather.2.cloned.1.call-start
  7.2 1.3 copy.33
  8.5 0.0 copy-start.3
  8.5 0.1 convert_reduce_fusion
  8.6 0.2 fusion.8
  8.8 0.0 copy-done
  8.8 0.0 copy-start.2
  8.8 2.4 %convert_reduce_fusion.1 = (f32[1024]{0:T(1024)S(1)}, bf16[1,1024,256]{1,2,0:T(8,128)(2,1)S(1)}) fusion(bf16[1024,256]{1,0:T(8,128)(2,1)S(1)} %copy-done, bf16[256,1024]{1,0:T(8,128)(2,1)} %param.12, bf16[1,1024,256]{1,2,0:T(8,128)(2,1)S(1)} %copy.33, f32[1024]{0:T(1024)S(1)} %add_rsqrt_fusion.1, f32[1024]{0:T(1024)S(1)} %broadcast_multiply_fusion.1), kind=kOutput, calls=%fused_computation.7 | convolution fusion | flops 1078197248 | bytes 2109440 | tf_op jit(solution)/shard_map/dot_general | solution.py:31
  11.2 0.0 copy-start.1
  11.3 0.2 fusion.10
  11.4 0.0 copy-done.3
  11.4 0.3 fusion.7
  11.7 0.5 collective-permute-start.1
  12.3 2.3 %collective-permute-done.1 = bf16[1,32,512]{2,1,0:T(8,128)(2,1)S(1)} collective-permute-done((bf16[1,32,512]{2,1,0:T(8,128)(2,1)S(1)}, bf16[1,32,512]{2,1,0:T(8,128)(2,1)S(1)}, u32[]{:S(2)}, u32[]{:S(2)}) %collective-permute-start.1) | collective-permute-done | bytes 32800 | tf_op jit(solution)/shard_map/ppermute | solution.py:62
  14.6 0.6 fusion.23
  15.2 0.0 all-gather.2.cloned.1.call-update
  15.3 0.5 collective-permute-start
  15.8 2.7 %collective-permute-done = bf16[1,1024,32]{1,2,0:T(8,128)(2,1)S(1)} collective-permute-done((bf16[1,1024,32]{1,2,0:T(8,128)(2,1)S(1)}, bf16[1,1024,32]{1,2,0:T(8,128)(2,1)S(1)}, u32[]{:S(2)}, u32[]{:S(2)}) %collective-permute-start) | collective-permute-done | bytes 65568 | tf_op jit(solution)/shard_map/ppermute | solution.py:56
  18.5 0.4 copy.35
  18.9 1.1 reshape.89
  19.9 14.1 %all-to-all-start.1 = ((bf16[64,2,512]{2,1,0:T(2,128)(2,1)}), bf16[64,2,512]{2,1,0:T(2,128)(2,1)S(1)}, u32[]{:S(2)}, u32[]{:S(2)}) async-start(bf16[64,2,512]{2,1,0:T(2,128)(2,1)} %reshape.89), calls=%async_computation.1 | async-start | bytes 262144 | tf_op jit(solution)/shard_map/all_to_all | solution.py:57
  34.0 0.0 copy-done.2
  34.1 0.8 copy.34
  34.8 10.5 %shard_map.113 = bf16[128,2,16,512]{3,2,1,0:T(8,128)(2,1)} custom-call(bf16[16,512,128]{2,1,0:T(8,128)(2,1)} %pair_ref.1, bf16[4,128,128]{2,1,0:T(8,128)(2,1)} %bitcast.53), custom_call_target="tpu_custom_call" | custom-call | flops 1073741824 | bytes 6291456 | tf_op jit(solution)/shard_map/pallas_call | solution.py:107
  45.4 0.0 copy-done.1
  45.4 0.0 all-to-all-done.1
  45.4 9.6 %all-to-all-start = ((bf16[128,2,16,512]{3,2,1,0:T(8,128)(2,1)}), bf16[128,2,16,512]{3,2,1,0:T(8,128)(2,1)}, u32[]{:S(2)}, u32[]{:S(2)}) async-start(bf16[128,2,16,512]{3,2,1,0:T(8,128)(2,1)} %shard_map.113), calls=%async_computation | async-start | bytes 8388608 | tf_op jit(solution)/shard_map/all_to_all | solution.py:69
  54.9 0.3 reshape.90
  55.2 0.1 copy.36
  55.4 51.1 %all-to-all-done.moved_ref = bf16[128,2,16,512]{3,2,1,0:T(8,128)(2,1)} async-done(((bf16[128,2,16,512]{3,2,1,0:T(8,128)(2,1)}), bf16[128,2,16,512]{3,2,1,0:T(8,128)(2,1)}, u32[]{:S(2)}, u32[]{:S(2)}) %all-to-all-start) | async-done | bytes 4194336 | tf_op jit(solution)/shard_map/all_to_all | solution.py:69
  106.5 5.9 %shard_map.114 = bf16[2,1024,512]{2,1,0:T(8,128)(2,1)} custom-call(bf16[128,2,16,512]{3,2,1,0:T(8,128)(2,1)} %all-to-all-done.moved_ref), custom_call_target="tpu_custom_call" | custom-call | flops 2147483648 | bytes 6291456 | tf_op jit(solution)/shard_map/pallas_call | solution.py:153
  112.4 8.1 %all-to-all-start.2 = ((bf16[128,16,512]{2,1,0:T(8,128)(2,1)}), bf16[128,16,512]{2,1,0:T(8,128)(2,1)S(1)}, u32[]{:S(2)}, u32[]{:S(2)}) async-start(bf16[128,16,512]{2,1,0:T(8,128)(2,1)} %bitcast.49), calls=%async_computation.2 | async-start | bytes 4194304 | tf_op jit(solution)/shard_map/all_to_all | solution.py:74
  120.5 2.0 copy.42
  122.6 0.6 slice.17.wg_ref
  123.2 1.1 copy.39
  124.2 0.9 copy.40
  125.1 1.1 copy.38
  126.2 26.0 %all-gather.2.cloned.1.call-done = bf16[32,128,512]{2,0,1:T(8,128)(2,1)} async-done(((bf16[32,2,512]{2,0,1:T(8,128)(2,1)}), bf16[32,128,512]{2,0,1:T(8,128)(2,1)}) %all-gather.2.cloned.1.call-update) | async-done | bytes 4194320 | tf_op jit(solution)/shard_map/all_gather | solution.py:63
  152.2 6.5 %copy.41.r_ref = bf16[32,128,512]{2,1,0:T(8,128)(2,1)} copy(bf16[32,128,512]{2,0,1:T(8,128)(2,1)} %all-gather.2.cloned.1.call-done) | data formatting | bytes 8388608 | tf_op jit(solution)/shard_map/all_gather | solution.py:63
  158.7 19.9 %shard_map.115.outer_ref = f32[16,512,128]{2,1,0:T(8,128)} custom-call(bf16[512,128]{1,0:T(8,128)(2,1)} %bitcast.56, bf16[32,128,512]{2,1,0:T(8,128)(2,1)} %copy.41.r_ref, bf16[128,1024]{1,0:T(8,128)(2,1)} %bitcast.55), custom_call_target="tpu_custom_call" | custom-call | flops 4294967296 | bytes 8388608 | tf_op jit(solution)/shard_map/pallas_call | solution.py:265
  178.6 0.0 all-to-all-done.2
  178.6 2.7 %copy.43 = bf16[16,8,16,512]{3,1,2,0:T(8,128)(2,1)} copy(bf16[16,8,16,512]{3,2,1,0:T(8,128)(2,1)S(1)} %bitcast.45) | data formatting | bytes 4194304
  181.3 17.1 %shard_map.116 = bf16[16,512,128]{2,1,0:T(8,128)(2,1)} custom-call(bf16[128,8192]{1,0:T(8,128)(2,1)} %bitcast.50, bf16[16,512,128]{2,1,0:T(8,128)(2,1)} %pair_ref.1, f32[16,512,128]{2,1,0:T(8,128)} %shard_map.115.outer_ref, bf16[128,128]{1,0:T(8,128)(2,1)} %wo_ref.1, bf16[128,128]{1,0:T(8,128)(2,1)} %slice.17.wg_ref, bf16[128,512]{1,0:T(8,128)(2,1)} %wu_ref.1, ...), custom_call_target="tpu_custom_call" | custom-call | flops 2952790016 | bytes 10485760 | tf_op jit(solution)/shard_map/pallas_call | solution.py:203
  (9 shorter events, 0.1 us)
Async XLA Ops:
  7.2 1.7 copy-start
  7.2 145.0 %all-gather.2.cloned.1.call-start = ((), (), s32[]{:S(2)}) async-start(), calls=%async_computation.3 | async-start | bytes 4259840 | tf_op jit(solution)/shard_map/all_gather | solution.py:63
  8.5 2.9 %copy-start.3 = (bf16[256,64]{0,1:T(8,128)(2,1)S(1)}, bf16[256,64]{0,1:T(8,128)(2,1)}, u32[]{:S(2)}) copy-start(bf16[256,64]{0,1:T(8,128)(2,1)} %param.14) | copy-start | bytes 98308
  8.8 25.2 %copy-start.2 = (bf16[128,640]{1,0:T(8,128)(2,1)S(1)}, bf16[128,640]{1,0:T(8,128)(2,1)}, u32[]{:S(2)}) copy-start(bf16[128,640]{1,0:T(8,128)(2,1)} %param.16) | copy-start | bytes 491524
  11.2 34.1 %copy-start.1 = (bf16[1,1024,256]{1,2,0:T(8,128)(2,1)}, bf16[1,1024,256]{1,2,0:T(8,128)(2,1)S(1)}, u32[]{:S(2)}) copy-start(bf16[1,1024,256]{1,2,0:T(8,128)(2,1)S(1)} %get-tuple-element.23) | copy-start | bytes 1572868
  11.7 2.8 %collective-permute-start.1 = (bf16[1,32,512]{2,1,0:T(8,128)(2,1)S(1)}, bf16[1,32,512]{2,1,0:T(8,128)(2,1)S(1)}, u32[]{:S(2)}, u32[]{:S(2)}) collective-permute-start(bf16[1,32,512]{2,1,0:T(8,128)(2,1)S(1)} %get-tuple-element.21), channel_id=1, source_target_pairs={{0,64},{64,0},{1,65},{65,1},{2,66},{66,2},{3,67},{67,3},{4,68},{68... | collective-permute-start | bytes 98312 | tf_op jit(solution)/shard_map/ppermute | solution.py:62
  15.3 3.2 %collective-permute-start = (bf16[1,1024,32]{1,2,0:T(8,128)(2,1)S(1)}, bf16[1,1024,32]{1,2,0:T(8,128)(2,1)S(1)}, u32[]{:S(2)}, u32[]{:S(2)}) collective-permute-start(bf16[1,1024,32]{1,2,0:T(8,128)(2,1)S(1)} %get-tuple-element.19), channel_id=1, source_target_pairs={{0,64},{64,0},{1,65},{65,1},{2,66},{66,2},{3,67},{67,3},{4,68},{68... | collective-permute-start | bytes 196616 | tf_op jit(solution)/shard_map/ppermute | solution.py:56
  19.9 25.4 %all-to-all-start.1 = ((bf16[64,2,512]{2,1,0:T(2,128)(2,1)}), bf16[64,2,512]{2,1,0:T(2,128)(2,1)S(1)}, u32[]{:S(2)}, u32[]{:S(2)}) async-start(bf16[64,2,512]{2,1,0:T(2,128)(2,1)} %reshape.89), calls=%async_computation.1 | async-start | bytes 262144 | tf_op jit(solution)/shard_map/all_to_all | solution.py:57
  45.4 61.1 %all-to-all-start = ((bf16[128,2,16,512]{3,2,1,0:T(8,128)(2,1)}), bf16[128,2,16,512]{3,2,1,0:T(8,128)(2,1)}, u32[]{:S(2)}, u32[]{:S(2)}) async-start(bf16[128,2,16,512]{3,2,1,0:T(8,128)(2,1)} %shard_map.113), calls=%async_computation | async-start | bytes 8388608 | tf_op jit(solution)/shard_map/all_to_all | solution.py:69
  112.4 66.3 %all-to-all-start.2 = ((bf16[128,16,512]{2,1,0:T(8,128)(2,1)}), bf16[128,16,512]{2,1,0:T(8,128)(2,1)S(1)}, u32[]{:S(2)}, u32[]{:S(2)}) async-start(bf16[128,16,512]{2,1,0:T(8,128)(2,1)} %bitcast.49), calls=%async_computation.2 | async-start | bytes 4194304 | tf_op jit(solution)/shard_map/all_to_all | solution.py:74
Sparse Core Ops, SparseCore 0:
  15.4 136.7 all-gather.1

commit v11 on v9

--- a/solution.py
+++ b/solution.py
@@ -165,7 +165,7 @@
 def back_kernel(prod_ref, pair_ref, outer_ref, wo_ref, wg_ref, wu_ref, wd_ref, out_ref):
     rows, columns, chans = pair_ref.shape
     for r in range(rows):
-        prod = prod_ref[:, r * columns : (r + 1) * columns].astype(jnp.float32)
+        prod = prod_ref[:, r, :].astype(jnp.float32)
         prod_norm = standardize_features(prod, 0).T.astype(jnp.bfloat16)
         tri_update = jnp.dot(prod_norm, wo_ref[...], preferred_element_type=jnp.float32)
         pair_float = pair_ref[r].astype(jnp.float32)
@@ -192,8 +192,7 @@
     pairwise_down_weight,
 ):
     tile_rows, columns, chans = pairwise_input.shape
-    step_rows = 4
-    prod_flat = product_tile.reshape(chans, tile_rows * columns)
+    step_rows = 8
     gate_weight = triangle_projection_weight[:, 4 * chans :]
     hidden = pairwise_up_weight.shape[1]
     row_block = lambda g: (g, 0, 0)
@@ -203,7 +202,7 @@
         out_shape=jax.ShapeDtypeStruct((tile_rows, columns, chans), jnp.bfloat16),
         grid=(tile_rows // step_rows,),
         in_specs=[
-            pl.BlockSpec((chans, step_rows * columns), lambda g: (0, g)),
+            pl.BlockSpec((chans, step_rows, columns), lambda g: (0, g, 0)),
             pl.BlockSpec((step_rows, columns, chans), row_block),
             pl.BlockSpec((step_rows, columns, chans), row_block),
             pl.BlockSpec((chans, chans), fixed),
@@ -218,7 +217,7 @@
             bytes_accessed=tile_rows * columns * chans * 10,
         ),
     )(
-        prod_flat,
+        product_tile,
         pairwise_input,
         outer_update,
         triangle_output_weight,

time: 184 us -> 185 us (level)
  Pallas kernels: 55.4 us -> 58.5 us
    pallas_call x1, Pallas kernels: 17.1 us -> 20.3 us  [pair_back(): pl.pallas_call(back_kernel, out_shape=jax.ShapeDtypeStruct((tile_rows, co...]
    unnamed x13 -> x14, local copies, waits for them, and re-layouts: 7.41 us -> 6.04 us
where the time goes in v11:
time: 185 us
  Pallas kernels  58.5 us (32%)
  waiting for transfers between devices  56.3 us (30%)
  starting transfers between devices  34.5 us (19%)
  local copies, waits for them, and re-layouts  17.4 us (9%)
  between operations  14.2 us (8%)
  matrix products  2.65 us (1%)
    all_to_all x1, waiting for transfers between devices, send_whole(): lax.all_to_all(tri_stack, both, split_axis=0, concat_axis=0, tiled=True)  53.3 us
    pallas_call x1, Pallas kernels, pair_back(): pl.pallas_call(back_kernel, out_shape=jax.ShapeDtypeStruct((tile_rows, co...  20.3 us
    pallas_call x1, Pallas kernels, outer_product(): pl.pallas_call(outer_kernel, out_shape=jax.ShapeDtypeStruct((tile_rows, c...  19.9 us
    all_to_all x1, starting transfers between devices, gather_sides(): lax.all_to_all(left_pair, 'rows', split_axis=1, concat_axis=0, tiled=True)  14.1 us
    pallas_call x1, Pallas kernels, pair_front(): pl.pallas_call(front_kernel, out_shape=jax.ShapeDtypeStruct((chans, 2, ti...  12.4 us
    all_to_all x1, starting transfers between devices, send_whole(): lax.all_to_all(tri_stack, both, split_axis=0, concat_axis=0, tiled=True)  9.84 us
    all_to_all x1, starting transfers between devices, send_back(): lax.all_to_all(product, ('branch', 'rows'), split_axis=0, concat_axis=0,...  6.82 us
    all_gather x1, local copies, waits for them, and re-layouts, gather_sides(): lax.all_gather(jnp.swapaxes(right_pair, 0, 1), 'rows', axis=1, tiled=True)  6.51 us
  transfers between devices with their start and end apart: 6, of which 3 were waited for; matrix products, arithmetic and copies ran while one was open for 8% of the time, Pallas kernels for 21%

profile of v11, /device:TPU:1, one launch (start us, length us, event | category | flops | bytes accessed | tf_op | source)
XLA Modules:
  0.0 184.8 jit_solution(5996433695911112971)
XLA Ops:
  7.2 0.0 copy-start
  7.2 0.0 all-gather.2.cloned.1.call-start
  7.2 1.3 copy.33
  8.5 0.0 copy-start.4
  8.5 0.1 convert_reduce_fusion
  8.6 0.2 fusion.8
  8.8 0.0 copy-done
  8.8 0.0 copy-start.3
  8.8 2.4 %convert_reduce_fusion.1 = (f32[1024]{0:T(1024)S(1)}, bf16[1,1024,256]{1,2,0:T(8,128)(2,1)S(1)}) fusion(bf16[1024,256]{1,0:T(8,128)(2,1)S(1)} %copy-done, bf16[256,1024]{1,0:T(8,128)(2,1)} %param.12, bf16[1,1024,256]{1,2,0:T(8,128)(2,1)S(1)} %copy.33, f32[1024]{0:T(1024)S(1)} %add_rsqrt_fusion.1, f32[1024]{0:T(1024)S(1)} %broadcast_multiply_fusion.1), kind=kOutput, calls=%fused_computation.7 | convolution fusion | flops 1078197248 | bytes 2109440 | tf_op jit(solution)/shard_map/dot_general | solution.py:31
  11.2 0.0 copy-start.2
  11.3 0.2 fusion.10
  11.4 0.0 copy-done.4
  11.4 0.3 fusion.7
  11.7 2.2 %collective-permute-start.1 = (bf16[1,32,512]{2,1,0:T(8,128)(2,1)S(1)}, bf16[1,32,512]{2,1,0:T(8,128)(2,1)S(1)}, u32[]{:S(2)}, u32[]{:S(2)}) collective-permute-start(bf16[1,32,512]{2,1,0:T(8,128)(2,1)S(1)} %get-tuple-element.21), channel_id=1, source_target_pairs={{0,64},{64,0},{1,65},{65,1},{2,66},{66,2},{3,67},{67,3},{4,68},{68... | collective-permute-start | bytes 98312 | tf_op jit(solution)/shard_map/ppermute | solution.py:62
  14.0 1.3 collective-permute-done.1
  15.3 0.6 fusion.23
  15.9 0.0 all-gather.2.cloned.1.call-update
  15.9 1.5 collective-permute-start
  17.5 1.7 collective-permute-done
  19.1 0.4 copy.35
  19.5 1.1 reshape.85
  20.6 14.1 %all-to-all-start.1 = ((bf16[64,2,512]{2,1,0:T(2,128)(2,1)}), bf16[64,2,512]{2,1,0:T(2,128)(2,1)S(1)}, u32[]{:S(2)}, u32[]{:S(2)}) async-start(bf16[64,2,512]{2,1,0:T(2,128)(2,1)} %reshape.85), calls=%async_computation.1 | async-start | bytes 262144 | tf_op jit(solution)/shard_map/all_to_all | solution.py:57
  34.7 0.0 copy-done.3
  34.7 0.8 copy.34
  35.5 12.4 %shard_map.113 = bf16[128,2,16,512]{3,2,1,0:T(8,128)(2,1)} custom-call(bf16[16,512,128]{2,1,0:T(8,128)(2,1)} %pair_ref.1, bf16[4,128,128]{2,1,0:T(8,128)(2,1)} %bitcast.49), custom_call_target="tpu_custom_call" | custom-call | flops 1073741824 | bytes 6291456 | tf_op jit(solution)/shard_map/pallas_call | solution.py:109
  47.9 0.0 copy-done.2
  47.9 0.0 all-to-all-done.1
  47.9 9.8 %all-to-all-start = ((bf16[128,2,16,512]{3,2,1,0:T(8,128)(2,1)}), bf16[128,2,16,512]{3,2,1,0:T(8,128)(2,1)}, u32[]{:S(2)}, u32[]{:S(2)}) async-start(bf16[128,2,16,512]{3,2,1,0:T(8,128)(2,1)} %shard_map.113), calls=%async_computation | async-start | bytes 8388608 | tf_op jit(solution)/shard_map/all_to_all | solution.py:69
  57.8 0.3 reshape.86
  58.1 0.1 copy.36
  58.2 53.3 %all-to-all-done.moved_ref = bf16[128,2,16,512]{3,2,1,0:T(8,128)(2,1)} async-done(((bf16[128,2,16,512]{3,2,1,0:T(8,128)(2,1)}), bf16[128,2,16,512]{3,2,1,0:T(8,128)(2,1)}, u32[]{:S(2)}, u32[]{:S(2)}) %all-to-all-start) | async-done | bytes 4194336 | tf_op jit(solution)/shard_map/all_to_all | solution.py:69
  111.5 5.9 %shard_map.114 = bf16[2,1024,512]{2,1,0:T(8,128)(2,1)} custom-call(bf16[128,2,16,512]{3,2,1,0:T(8,128)(2,1)} %all-to-all-done.moved_ref), custom_call_target="tpu_custom_call" | custom-call | flops 2147483648 | bytes 6291456 | tf_op jit(solution)/shard_map/pallas_call | solution.py:151
  117.4 6.8 %all-to-all-start.2 = ((bf16[128,16,512]{2,1,0:T(8,128)(2,1)}), bf16[128,16,512]{2,1,0:T(8,128)(2,1)S(1)}, u32[]{:S(2)}, u32[]{:S(2)}) async-start(bf16[128,16,512]{2,1,0:T(8,128)(2,1)} %bitcast.46), calls=%async_computation.2 | async-start | bytes 4194304 | tf_op jit(solution)/shard_map/all_to_all | solution.py:74
  124.3 2.0 %copy.42 = bf16[1,1024,256]{2,1,0:T(8,128)(2,1)} copy(bf16[1,1024,256]{1,2,0:T(8,128)(2,1)} %copy-done.2) | data formatting | bytes 1048576
  126.3 0.6 slice.17.wg_ref
  126.9 1.1 copy.39
  128.0 0.9 copy.40
  128.8 1.1 copy.38
  129.9 0.0 all-gather.2.cloned.1.call-done
  129.9 6.5 %copy.41.r_ref = bf16[32,128,512]{2,1,0:T(8,128)(2,1)} copy(bf16[32,128,512]{2,0,1:T(8,128)(2,1)} %all-gather.2.cloned.1.call-done) | data formatting | bytes 8388608 | tf_op jit(solution)/shard_map/all_gather | solution.py:63
  136.4 19.9 %shard_map.115.outer_ref = f32[16,512,128]{2,1,0:T(8,128)} custom-call(bf16[512,128]{1,0:T(8,128)(2,1)} %bitcast.52, bf16[32,128,512]{2,1,0:T(8,128)(2,1)} %copy.41.r_ref, bf16[128,1024]{1,0:T(8,128)(2,1)} %bitcast.51), custom_call_target="tpu_custom_call" | custom-call | flops 4294967296 | bytes 8388608 | tf_op jit(solution)/shard_map/pallas_call | solution.py:262
  156.3 0.0 all-to-all-done.2.prod_ref
  156.3 0.0 copy-start.1
  156.3 1.3 copy-done.1
  157.7 20.3 %shard_map.116 = bf16[16,512,128]{2,1,0:T(8,128)(2,1)} custom-call(bf16[128,16,512]{2,1,0:T(8,128)(2,1)} %copy-done.1, bf16[16,512,128]{2,1,0:T(8,128)(2,1)} %pair_ref.1, f32[16,512,128]{2,1,0:T(8,128)} %shard_map.115.outer_ref, bf16[128,128]{1,0:T(8,128)(2,1)} %wo_ref.1, bf16[128,128]{1,0:T(8,128)(2,1)} %slice.17.wg_ref, bf16[128,512]{1,0:T(8,128)(2,1)} %wu_ref.1, ...), custom_call_target="tpu_custom_call" | custom-call | flops 2952790016 | bytes 10485760 | tf_op jit(solution)/shard_map/pallas_call | solution.py:200
  (9 shorter events, 0.1 us)
Async XLA Ops:
  7.2 1.7 copy-start
  7.2 122.7 %all-gather.2.cloned.1.call-start = ((), (), s32[]{:S(2)}) async-start(), calls=%async_computation.3 | async-start | bytes 4259840 | tf_op jit(solution)/shard_map/all_gather | solution.py:63
  8.5 2.9 %copy-start.4 = (bf16[256,64]{0,1:T(8,128)(2,1)S(1)}, bf16[256,64]{0,1:T(8,128)(2,1)}, u32[]{:S(2)}) copy-start(bf16[256,64]{0,1:T(8,128)(2,1)} %param.14) | copy-start | bytes 98308
  8.8 25.9 %copy-start.3 = (bf16[128,640]{1,0:T(8,128)(2,1)S(1)}, bf16[128,640]{1,0:T(8,128)(2,1)}, u32[]{:S(2)}) copy-start(bf16[128,640]{1,0:T(8,128)(2,1)} %param.16) | copy-start | bytes 491524
  11.2 36.7 %copy-start.2 = (bf16[1,1024,256]{1,2,0:T(8,128)(2,1)}, bf16[1,1024,256]{1,2,0:T(8,128)(2,1)S(1)}, u32[]{:S(2)}) copy-start(bf16[1,1024,256]{1,2,0:T(8,128)(2,1)S(1)} %get-tuple-element.23) | copy-start | bytes 1572868
  11.7 3.5 %collective-permute-start.1 = (bf16[1,32,512]{2,1,0:T(8,128)(2,1)S(1)}, bf16[1,32,512]{2,1,0:T(8,128)(2,1)S(1)}, u32[]{:S(2)}, u32[]{:S(2)}) collective-permute-start(bf16[1,32,512]{2,1,0:T(8,128)(2,1)S(1)} %get-tuple-element.21), channel_id=1, source_target_pairs={{0,64},{64,0},{1,65},{65,1},{2,66},{66,2},{3,67},{67,3},{4,68},{68... | collective-permute-start | bytes 98312 | tf_op jit(solution)/shard_map/ppermute | solution.py:62
  15.9 3.2 %collective-permute-start = (bf16[1,1024,32]{1,2,0:T(8,128)(2,1)S(1)}, bf16[1,1024,32]{1,2,0:T(8,128)(2,1)S(1)}, u32[]{:S(2)}, u32[]{:S(2)}) collective-permute-start(bf16[1,1024,32]{1,2,0:T(8,128)(2,1)S(1)} %get-tuple-element.19), channel_id=1, source_target_pairs={{0,64},{64,0},{1,65},{65,1},{2,66},{66,2},{3,67},{67,3},{4,68},{68... | collective-permute-start | bytes 196616 | tf_op jit(solution)/shard_map/ppermute | solution.py:56
  20.6 27.3 %all-to-all-start.1 = ((bf16[64,2,512]{2,1,0:T(2,128)(2,1)}), bf16[64,2,512]{2,1,0:T(2,128)(2,1)S(1)}, u32[]{:S(2)}, u32[]{:S(2)}) async-start(bf16[64,2,512]{2,1,0:T(2,128)(2,1)} %reshape.85), calls=%async_computation.1 | async-start | bytes 262144 | tf_op jit(solution)/shard_map/all_to_all | solution.py:57
  47.9 63.6 %all-to-all-start = ((bf16[128,2,16,512]{3,2,1,0:T(8,128)(2,1)}), bf16[128,2,16,512]{3,2,1,0:T(8,128)(2,1)}, u32[]{:S(2)}, u32[]{:S(2)}) async-start(bf16[128,2,16,512]{3,2,1,0:T(8,128)(2,1)} %shard_map.113), calls=%async_computation | async-start | bytes 8388608 | tf_op jit(solution)/shard_map/all_to_all | solution.py:69
  117.4 38.9 %all-to-all-start.2 = ((bf16[128,16,512]{2,1,0:T(8,128)(2,1)}), bf16[128,16,512]{2,1,0:T(8,128)(2,1)S(1)}, u32[]{:S(2)}, u32[]{:S(2)}) async-start(bf16[128,16,512]{2,1,0:T(8,128)(2,1)} %bitcast.46), calls=%async_computation.2 | async-start | bytes 4194304 | tf_op jit(solution)/shard_map/all_to_all | solution.py:74
  156.3 1.3 copy-start.1
Sparse Core Ops, SparseCore 0:
  16.0 110.1 all-gather.1

commit v12 on v9

--- a/solution.py
+++ b/solution.py
@@ -285,13 +285,13 @@
     pairwise_up_weight,
     pairwise_down_weight,
 ):
+    tri_stack = pair_front(pairwise_input, triangle_projection_weight)
+    moved = send_whole(tri_stack)
+    homolog_features, tri_stack = lax.optimization_barrier((homolog_features, tri_stack))
     refreshed_homolog_features, left_side, right_side = alignment_branch(
         homolog_features, transition_expand_matrix, transition_contract_matrix, factor_pair_matrices
     )
     left_gathered, right_gathered = gather_sides(left_side, right_side)
-    pairwise_input, right_side = lax.optimization_barrier((pairwise_input, right_side))
-    tri_stack = pair_front(pairwise_input, triangle_projection_weight)
-    moved = send_whole(tri_stack)
     product = triangle_product(moved)
     product, left_gathered = lax.optimization_barrier((product, left_gathered))
     product_tile = send_back(product)

time: 184 us -> 220 us (1.20)
  waiting for transfers between devices: 56.3 us -> 90.1 us
  blocking collectives: 0 us -> 24 us
  starting transfers between devices: 34.5 us -> 13.7 us
    all_gather x1, waiting for transfers between devices: 0.01 us -> 32 us  [gather_sides(): lax.all_gather(jnp.swapaxes(right_pair, 0, 1), 'rows', axis=1, tiled=True)]
    all_to_all x0 -> x1, blocking collectives: none -> 24 us  [gather_sides(): lax.all_to_all(left_pair, 'rows', split_axis=1, concat_axis=0, tiled=True)]
    all_to_all x1 -> x0, starting transfers between devices: 14.1 us -> none  [gather_sides(): lax.all_to_all(left_pair, 'rows', split_axis=1, concat_axis=0, tiled=True)]
    all_to_all x1, starting transfers between devices: 9.84 us -> 4.94 us  [send_whole(): lax.all_to_all(tri_stack, both, split_axis=0, concat_axis=0, tiled=True)]
    unnamed x13 -> x14, local copies, waits for them, and re-layouts: 7.41 us -> 5.45 us
  transfers between devices with their start and end apart: 6 -> 5, of which waited for: 3 -> 4; matrix products, arithmetic and copies ran while one was open for 8% -> 6% of each run, Pallas kernels for 21% -> 12%
where the time goes in v12:
time: 220 us; the launch traced here: 219 us
  waiting for transfers between devices  90.1 us (41%)
  Pallas kernels  55.4 us (25%)
  blocking collectives  24 us (11%)
  local copies, waits for them, and re-layouts  18.8 us (9%)
  between operations  14.2 us (6%)
  starting transfers between devices  13.7 us (6%)
    all_to_all x1, waiting for transfers between devices, send_whole(): lax.all_to_all(tri_stack, both, split_axis=0, concat_axis=0, tiled=True)  55.1 us
    all_gather x1, waiting for transfers between devices, gather_sides(): lax.all_gather(jnp.swapaxes(right_pair, 0, 1), 'rows', axis=1, tiled=True)  32 us
    all_to_all x1, blocking collectives, gather_sides(): lax.all_to_all(left_pair, 'rows', split_axis=1, concat_axis=0, tiled=True)  24 us
    pallas_call x1, Pallas kernels, outer_product(): pl.pallas_call(outer_kernel, out_shape=jax.ShapeDtypeStruct((tile_rows, c...  19.9 us
    pallas_call x1, Pallas kernels, pair_back(): pl.pallas_call(back_kernel, out_shape=jax.ShapeDtypeStruct((tile_rows, co...  17.1 us
    pallas_call x1, Pallas kernels, pair_front(): pl.pallas_call(front_kernel, out_shape=jax.ShapeDtypeStruct((chans, 2, ti...  12.5 us
    all_gather x1, local copies, waits for them, and re-layouts, gather_sides(): lax.all_gather(jnp.swapaxes(right_pair, 0, 1), 'rows', axis=1, tiled=True)  6.51 us
    pallas_call x1, Pallas kernels, triangle_product(): pl.pallas_call(product_kernel, out_shape=jax.ShapeDtypeStruct((halves, n_...  5.87 us
  transfers between devices with their start and end apart: 5, of which 4 were waited for; matrix products, arithmetic and copies ran while one was open for 6% of the time, Pallas kernels for 12%

profile of v12, /device:TPU:1, one launch (start us, length us, event | category | flops | bytes accessed | tf_op | source)
XLA Modules:
  0.0 218.9 jit_solution(10475296749999024820)
XLA Ops:
  7.2 0.0 copy-start
  7.2 0.0 copy-start.2
  7.2 0.0 all-gather.2.cloned.1.call-start
  7.2 1.0 slice_bitcast_fusion
  8.3 0.8 copy.33
  9.0 0.0 copy-start.3
  9.0 12.5 %shard_map.113 = bf16[128,2,16,512]{3,2,1,0:T(8,128)(2,1)} custom-call(bf16[16,512,128]{2,1,0:T(8,128)(2,1)} %pair_ref.3, bf16[4,128,128]{2,1,0:T(8,128)(2,1)} %bitcast.53), custom_call_target="tpu_custom_call" | custom-call | flops 1073741824 | bytes 6291456 | tf_op jit(solution)/shard_map/pallas_call | solution.py:109
  21.5 0.0 copy-done.2
  21.5 0.2 copy.34
  21.7 0.0 copy-start.4
  21.8 0.1 convert_reduce_fusion
  21.9 0.2 fusion.8
  22.0 0.0 copy-done
  22.0 0.0 copy-done.3
  22.1 1.3 convert_reduce_fusion.1
  23.4 0.0 copy-start.1
  23.4 0.2 fusion.10
  23.6 0.0 copy-done.4
  23.6 0.3 fusion.7
  23.9 2.2 %collective-permute-start.1 = (bf16[1,32,512]{2,1,0:T(8,128)(2,1)S(1)}, bf16[1,32,512]{2,1,0:T(8,128)(2,1)S(1)}, u32[]{:S(2)}, u32[]{:S(2)}) collective-permute-start(bf16[1,32,512]{2,1,0:T(8,128)(2,1)S(1)} %get-tuple-element.23), channel_id=1, source_target_pairs={{0,64},{64,0},{1,65},{65,1},{2,66},{66,2},{3,67},{67,3},{4,68},{68... | collective-permute-start | bytes 98312 | tf_op jit(solution)/shard_map/ppermute | solution.py:62
  26.1 1.3 collective-permute-done.1
  27.4 0.6 fusion.23
  28.0 0.0 all-gather.2.cloned.1.call-update
  28.1 1.5 collective-permute-start
  29.6 1.7 collective-permute-done
  31.3 0.4 copy.35
  31.7 0.4 reshape.89
  32.1 24.0 %all_to_all.28 = bf16[64,2,512]{2,1,0:T(2,128)(2,1)S(1)} all-to-all(bf16[64,2,512]{2,1,0:T(2,128)(2,1)S(1)} %reshape.89), channel_id=1, replica_groups=mesh['branch'=2,'rows'=64] {'rows'}, dimensions={0} | all-to-all | bytes 262144 | tf_op jit(solution)/shard_map/all_to_all | solution.py:57
  56.1 0.0 copy-done.1
  56.1 4.9 %all-to-all-start = ((bf16[128,2,16,512]{3,2,1,0:T(8,128)(2,1)}), bf16[128,2,16,512]{3,2,1,0:T(8,128)(2,1)}, u32[]{:S(2)}, u32[]{:S(2)}) async-start(bf16[128,2,16,512]{3,2,1,0:T(8,128)(2,1)} %shard_map.113), calls=%async_computation | async-start | bytes 8388608 | tf_op jit(solution)/shard_map/all_to_all | solution.py:69
  61.0 0.3 reshape.90
  61.3 0.1 copy.36
  61.5 55.1 %all-to-all-done.moved_ref = bf16[128,2,16,512]{3,2,1,0:T(8,128)(2,1)} async-done(((bf16[128,2,16,512]{3,2,1,0:T(8,128)(2,1)}), bf16[128,2,16,512]{3,2,1,0:T(8,128)(2,1)}, u32[]{:S(2)}, u32[]{:S(2)}) %all-to-all-start) | async-done | bytes 4194336 | tf_op jit(solution)/shard_map/all_to_all | solution.py:69
  116.6 5.9 %shard_map.114 = bf16[2,1024,512]{2,1,0:T(8,128)(2,1)} custom-call(bf16[128,2,16,512]{3,2,1,0:T(8,128)(2,1)} %all-to-all-done.moved_ref), custom_call_target="tpu_custom_call" | custom-call | flops 2147483648 | bytes 6291456 | tf_op jit(solution)/shard_map/pallas_call | solution.py:151
  122.4 5.0 %all-to-all-start.2 = ((bf16[128,16,512]{2,1,0:T(8,128)(2,1)}), bf16[128,16,512]{2,1,0:T(8,128)(2,1)S(1)}, u32[]{:S(2)}, u32[]{:S(2)}) async-start(bf16[128,16,512]{2,1,0:T(8,128)(2,1)} %bitcast.49), calls=%async_computation.2 | async-start | bytes 4194304 | tf_op jit(solution)/shard_map/all_to_all | solution.py:74
  127.4 2.0 copy.42
  129.5 1.4 slice.17.wg_ref
  130.8 1.1 copy.39
  131.9 0.9 copy.40
  132.8 1.1 copy.38
  133.8 32.0 %all-gather.2.cloned.1.call-done = bf16[32,128,512]{2,0,1:T(8,128)(2,1)} async-done(((bf16[32,2,512]{2,0,1:T(8,128)(2,1)}), bf16[32,128,512]{2,0,1:T(8,128)(2,1)}) %all-gather.2.cloned.1.call-update) | async-done | bytes 4194320 | tf_op jit(solution)/shard_map/all_gather | solution.py:63
  165.8 6.5 %copy.41.r_ref = bf16[32,128,512]{2,1,0:T(8,128)(2,1)} copy(bf16[32,128,512]{2,0,1:T(8,128)(2,1)} %all-gather.2.cloned.1.call-done) | data formatting | bytes 8388608 | tf_op jit(solution)/shard_map/all_gather | solution.py:63
  172.3 19.9 %shard_map.115.outer_ref = f32[16,512,128]{2,1,0:T(8,128)} custom-call(bf16[512,128]{1,0:T(8,128)(2,1)} %bitcast.56, bf16[32,128,512]{2,1,0:T(8,128)(2,1)} %copy.41.r_ref, bf16[128,1024]{1,0:T(8,128)(2,1)} %bitcast.55), custom_call_target="tpu_custom_call" | custom-call | flops 4294967296 | bytes 8388608 | tf_op jit(solution)/shard_map/pallas_call | solution.py:263
  192.2 0.0 all-to-all-done.2
  192.2 2.7 %copy.43 = bf16[16,8,16,512]{3,1,2,0:T(8,128)(2,1)} copy(bf16[16,8,16,512]{3,2,1,0:T(8,128)(2,1)S(1)} %bitcast.45) | data formatting | bytes 4194304
  194.9 17.1 %shard_map.116 = bf16[16,512,128]{2,1,0:T(8,128)(2,1)} custom-call(bf16[128,8192]{1,0:T(8,128)(2,1)} %bitcast.50, bf16[16,512,128]{2,1,0:T(8,128)(2,1)} %pair_ref.3, f32[16,512,128]{2,1,0:T(8,128)} %shard_map.115.outer_ref, bf16[128,128]{1,0:T(8,128)(2,1)} %wo_ref.1, bf16[128,128]{1,0:T(8,128)(2,1)} %slice.17.wg_ref, bf16[128,512]{1,0:T(8,128)(2,1)} %wu_ref.1, ...), custom_call_target="tpu_custom_call" | custom-call | flops 2952790016 | bytes 10485760 | tf_op jit(solution)/shard_map/pallas_call | solution.py:201
  (8 shorter events, 0.1 us)
Async XLA Ops:
  7.2 14.9 %copy-start = (bf16[1024,256]{1,0:T(8,128)(2,1)S(1)}, bf16[1024,256]{1,0:T(8,128)(2,1)}, u32[]{:S(2)}) copy-start(bf16[1024,256]{1,0:T(8,128)(2,1)} %param.13) | copy-start | bytes 1572868
  7.2 14.4 %copy-start.2 = (bf16[1,1024,256]{2,1,0:T(8,128)(2,1)S(1)}, bf16[1,1024,256]{2,1,0:T(8,128)(2,1)}, u32[]{:S(2)}) copy-start(bf16[1,1024,256]{2,1,0:T(8,128)(2,1)} %param.10) | copy-start | bytes 1572868
  7.2 158.6 %all-gather.2.cloned.1.call-start = ((), (), s32[]{:S(2)}) async-start(), calls=%async_computation.3 | async-start | bytes 4259840 | tf_op jit(solution)/shard_map/all_gather | solution.py:63
  9.0 13.0 %copy-start.3 = (bf16[256,1024]{1,0:T(8,128)(2,1)S(1)}, bf16[256,1024]{1,0:T(8,128)(2,1)}, u32[]{:S(2)}) copy-start(bf16[256,1024]{1,0:T(8,128)(2,1)} %param.12) | copy-start | bytes 1572868
  21.7 1.8 copy-start.4
  23.4 32.7 %copy-start.1 = (bf16[1,1024,256]{1,2,0:T(8,128)(2,1)}, bf16[1,1024,256]{1,2,0:T(8,128)(2,1)S(1)}, u32[]{:S(2)}) copy-start(bf16[1,1024,256]{1,2,0:T(8,128)(2,1)S(1)} %get-tuple-element.25) | copy-start | bytes 1572868
  23.9 3.5 %collective-permute-start.1 = (bf16[1,32,512]{2,1,0:T(8,128)(2,1)S(1)}, bf16[1,32,512]{2,1,0:T(8,128)(2,1)S(1)}, u32[]{:S(2)}, u32[]{:S(2)}) collective-permute-start(bf16[1,32,512]{2,1,0:T(8,128)(2,1)S(1)} %get-tuple-element.23), channel_id=1, source_target_pairs={{0,64},{64,0},{1,65},{65,1},{2,66},{66,2},{3,67},{67,3},{4,68},{68... | collective-permute-start | bytes 98312 | tf_op jit(solution)/shard_map/ppermute | solution.py:62
  28.1 3.2 %collective-permute-start = (bf16[1,1024,32]{1,2,0:T(8,128)(2,1)S(1)}, bf16[1,1024,32]{1,2,0:T(8,128)(2,1)S(1)}, u32[]{:S(2)}, u32[]{:S(2)}) collective-permute-start(bf16[1,1024,32]{1,2,0:T(8,128)(2,1)S(1)} %get-tuple-element.21), channel_id=1, source_target_pairs={{0,64},{64,0},{1,65},{65,1},{2,66},{66,2},{3,67},{67,3},{4,68},{68... | collective-permute-start | bytes 196616 | tf_op jit(solution)/shard_map/ppermute | solution.py:56
  56.1 60.5 %all-to-all-start = ((bf16[128,2,16,512]{3,2,1,0:T(8,128)(2,1)}), bf16[128,2,16,512]{3,2,1,0:T(8,128)(2,1)}, u32[]{:S(2)}, u32[]{:S(2)}) async-start(bf16[128,2,16,512]{3,2,1,0:T(8,128)(2,1)} %shard_map.113), calls=%async_computation | async-start | bytes 8388608 | tf_op jit(solution)/shard_map/all_to_all | solution.py:69
  122.4 69.8 %all-to-all-start.2 = ((bf16[128,16,512]{2,1,0:T(8,128)(2,1)}), bf16[128,16,512]{2,1,0:T(8,128)(2,1)S(1)}, u32[]{:S(2)}, u32[]{:S(2)}) async-start(bf16[128,16,512]{2,1,0:T(8,128)(2,1)} %bitcast.49), calls=%async_computation.2 | async-start | bytes 4194304 | tf_op jit(solution)/shard_map/all_to_all | solution.py:74
Sparse Core Ops, SparseCore 0:
  28.2 137.6 all-gather.1

commit v13 on v9

--- a/solution.py
+++ b/solution.py
@@ -104,7 +104,7 @@
 
 def pair_front(pairwise_input, triangle_projection_weight):
     tile_rows, columns, chans = pairwise_input.shape
-    block = 32
+    block = 64
     weight = triangle_projection_weight[:, : 4 * chans].T.reshape(4, chans, chans)
     return pl.pallas_call(
         front_kernel,

time: 184 us -> 183 us (level)
  no operation moved by 1% of the time
where the time goes in v13:
time: 183 us
  waiting for transfers between devices  56 us (31%)
  Pallas kernels  55.2 us (30%)
  starting transfers between devices  34.8 us (19%)
  local copies, waits for them, and re-layouts  18.8 us (10%)
  between operations  14.2 us (8%)
  matrix products  2.65 us (1%)
    all_to_all x1, waiting for transfers between devices, send_whole(): lax.all_to_all(tri_stack, both, split_axis=0, concat_axis=0, tiled=True)  53.1 us
    pallas_call x1, Pallas kernels, outer_product(): pl.pallas_call(outer_kernel, out_shape=jax.ShapeDtypeStruct((tile_rows, c...  19.9 us
    pallas_call x1, Pallas kernels, pair_back(): pl.pallas_call(back_kernel, out_shape=jax.ShapeDtypeStruct((tile_rows, co...  17.1 us
    all_to_all x1, starting transfers between devices, gather_sides(): lax.all_to_all(left_pair, 'rows', split_axis=1, concat_axis=0, tiled=True)  14.1 us
    pallas_call x1, Pallas kernels, pair_front(): pl.pallas_call(front_kernel, out_shape=jax.ShapeDtypeStruct((chans, 2, ti...  12.2 us
    all_to_all x1, starting transfers between devices, send_whole(): lax.all_to_all(tri_stack, both, split_axis=0, concat_axis=0, tiled=True)  9.85 us
    unnamed x13, local copies, waits for them, and re-layouts  7.41 us
    all_to_all x1, starting transfers between devices, send_back(): lax.all_to_all(product, ('branch', 'rows'), split_axis=0, concat_axis=0,...  7.03 us
  transfers between devices with their start and end apart: 6, of which 3 were waited for; matrix products, arithmetic and copies ran while one was open for 8% of the time, Pallas kernels for 21%

profile of v13, /device:TPU:1, one launch (start us, length us, event | category | flops | bytes accessed | tf_op | source)
XLA Modules:
  0.0 182.8 jit_solution(15853200394639646592)
XLA Ops:
  7.2 0.0 copy-start
  7.2 0.0 all-gather.2.cloned.1.call-start
  7.2 1.3 copy.33
  8.5 0.0 copy-start.3
  8.5 0.1 convert_reduce_fusion
  8.6 0.2 fusion.8
  8.8 0.0 copy-done
  8.8 0.0 copy-start.2
  8.8 2.4 %convert_reduce_fusion.1 = (f32[1024]{0:T(1024)S(1)}, bf16[1,1024,256]{1,2,0:T(8,128)(2,1)S(1)}) fusion(bf16[1024,256]{1,0:T(8,128)(2,1)S(1)} %copy-done, bf16[256,1024]{1,0:T(8,128)(2,1)} %param.12, bf16[1,1024,256]{1,2,0:T(8,128)(2,1)S(1)} %copy.33, f32[1024]{0:T(1024)S(1)} %add_rsqrt_fusion.1, f32[1024]{0:T(1024)S(1)} %broadcast_multiply_fusion.1), kind=kOutput, calls=%fused_computation.7 | convolution fusion | flops 1078197248 | bytes 2109440 | tf_op jit(solution)/shard_map/dot_general | solution.py:31
  11.2 0.0 copy-start.1
  11.3 0.2 fusion.10
  11.4 0.0 copy-done.3
  11.4 0.3 fusion.7
  11.7 2.2 %collective-permute-start.1 = (bf16[1,32,512]{2,1,0:T(8,128)(2,1)S(1)}, bf16[1,32,512]{2,1,0:T(8,128)(2,1)S(1)}, u32[]{:S(2)}, u32[]{:S(2)}) collective-permute-start(bf16[1,32,512]{2,1,0:T(8,128)(2,1)S(1)} %get-tuple-element.21), channel_id=1, source_target_pairs={{0,64},{64,0},{1,65},{65,1},{2,66},{66,2},{3,67},{67,3},{4,68},{68... | collective-permute-start | bytes 98312 | tf_op jit(solution)/shard_map/ppermute | solution.py:62
  14.0 1.3 collective-permute-done.1
  15.3 0.6 fusion.23
  15.9 0.0 all-gather.2.cloned.1.call-update
  15.9 1.5 collective-permute-start
  17.5 1.7 collective-permute-done
  19.1 0.4 copy.35
  19.5 1.1 reshape.89
  20.6 14.1 %all-to-all-start.1 = ((bf16[64,2,512]{2,1,0:T(2,128)(2,1)}), bf16[64,2,512]{2,1,0:T(2,128)(2,1)S(1)}, u32[]{:S(2)}, u32[]{:S(2)}) async-start(bf16[64,2,512]{2,1,0:T(2,128)(2,1)} %reshape.89), calls=%async_computation.1 | async-start | bytes 262144 | tf_op jit(solution)/shard_map/all_to_all | solution.py:57
  34.7 0.0 copy-done.2
  34.7 0.8 copy.34
  35.5 12.2 %shard_map.113 = bf16[128,2,16,512]{3,2,1,0:T(8,128)(2,1)} custom-call(bf16[16,512,128]{2,1,0:T(8,128)(2,1)} %pair_ref.1, bf16[4,128,128]{2,1,0:T(8,128)(2,1)} %bitcast.53), custom_call_target="tpu_custom_call" | custom-call | flops 1073741824 | bytes 6291456 | tf_op jit(solution)/shard_map/pallas_call | solution.py:109
  47.7 0.0 copy-done.1
  47.7 0.0 all-to-all-done.1
  47.7 9.8 %all-to-all-start = ((bf16[128,2,16,512]{3,2,1,0:T(8,128)(2,1)}), bf16[128,2,16,512]{3,2,1,0:T(8,128)(2,1)}, u32[]{:S(2)}, u32[]{:S(2)}) async-start(bf16[128,2,16,512]{3,2,1,0:T(8,128)(2,1)} %shard_map.113), calls=%async_computation | async-start | bytes 8388608 | tf_op jit(solution)/shard_map/all_to_all | solution.py:69
  57.6 0.3 reshape.90
  57.9 0.1 copy.36
  58.0 53.1 %all-to-all-done.moved_ref = bf16[128,2,16,512]{3,2,1,0:T(8,128)(2,1)} async-done(((bf16[128,2,16,512]{3,2,1,0:T(8,128)(2,1)}), bf16[128,2,16,512]{3,2,1,0:T(8,128)(2,1)}, u32[]{:S(2)}, u32[]{:S(2)}) %all-to-all-start) | async-done | bytes 4194336 | tf_op jit(solution)/shard_map/all_to_all | solution.py:69
  111.1 5.9 %shard_map.114 = bf16[2,1024,512]{2,1,0:T(8,128)(2,1)} custom-call(bf16[128,2,16,512]{3,2,1,0:T(8,128)(2,1)} %all-to-all-done.moved_ref), custom_call_target="tpu_custom_call" | custom-call | flops 2147483648 | bytes 6291456 | tf_op jit(solution)/shard_map/pallas_call | solution.py:151
  117.0 7.0 %all-to-all-start.2 = ((bf16[128,16,512]{2,1,0:T(8,128)(2,1)}), bf16[128,16,512]{2,1,0:T(8,128)(2,1)S(1)}, u32[]{:S(2)}, u32[]{:S(2)}) async-start(bf16[128,16,512]{2,1,0:T(8,128)(2,1)} %bitcast.49), calls=%async_computation.2 | async-start | bytes 4194304 | tf_op jit(solution)/shard_map/all_to_all | solution.py:74
  124.0 2.0 %copy.42 = bf16[1,1024,256]{2,1,0:T(8,128)(2,1)} copy(bf16[1,1024,256]{1,2,0:T(8,128)(2,1)} %copy-done.1) | data formatting | bytes 1048576
  126.1 0.6 slice.17.wg_ref
  126.7 1.1 copy.39
  127.7 0.9 copy.40
  128.6 1.1 copy.38
  129.7 0.0 all-gather.2.cloned.1.call-done
  129.7 6.5 %copy.41.r_ref = bf16[32,128,512]{2,1,0:T(8,128)(2,1)} copy(bf16[32,128,512]{2,0,1:T(8,128)(2,1)} %all-gather.2.cloned.1.call-done) | data formatting | bytes 8388608 | tf_op jit(solution)/shard_map/all_gather | solution.py:63
  136.2 19.9 %shard_map.115.outer_ref = f32[16,512,128]{2,1,0:T(8,128)} custom-call(bf16[512,128]{1,0:T(8,128)(2,1)} %bitcast.56, bf16[32,128,512]{2,1,0:T(8,128)(2,1)} %copy.41.r_ref, bf16[128,1024]{1,0:T(8,128)(2,1)} %bitcast.55), custom_call_target="tpu_custom_call" | custom-call | flops 4294967296 | bytes 8388608 | tf_op jit(solution)/shard_map/pallas_call | solution.py:263
  156.1 0.0 all-to-all-done.2
  156.1 2.7 %copy.43 = bf16[16,8,16,512]{3,1,2,0:T(8,128)(2,1)} copy(bf16[16,8,16,512]{3,2,1,0:T(8,128)(2,1)S(1)} %bitcast.45) | data formatting | bytes 4194304
  158.8 17.1 %shard_map.116 = bf16[16,512,128]{2,1,0:T(8,128)(2,1)} custom-call(bf16[128,8192]{1,0:T(8,128)(2,1)} %bitcast.50, bf16[16,512,128]{2,1,0:T(8,128)(2,1)} %pair_ref.1, f32[16,512,128]{2,1,0:T(8,128)} %shard_map.115.outer_ref, bf16[128,128]{1,0:T(8,128)(2,1)} %wo_ref.1, bf16[128,128]{1,0:T(8,128)(2,1)} %slice.17.wg_ref, bf16[128,512]{1,0:T(8,128)(2,1)} %wu_ref.1, ...), custom_call_target="tpu_custom_call" | custom-call | flops 2952790016 | bytes 10485760 | tf_op jit(solution)/shard_map/pallas_call | solution.py:201
  (9 shorter events, 0.1 us)
Async XLA Ops:
  7.2 1.7 copy-start
  7.2 122.5 %all-gather.2.cloned.1.call-start = ((), (), s32[]{:S(2)}) async-start(), calls=%async_computation.3 | async-start | bytes 4259840 | tf_op jit(solution)/shard_map/all_gather | solution.py:63
  8.5 2.9 %copy-start.3 = (bf16[256,64]{0,1:T(8,128)(2,1)S(1)}, bf16[256,64]{0,1:T(8,128)(2,1)}, u32[]{:S(2)}) copy-start(bf16[256,64]{0,1:T(8,128)(2,1)} %param.14) | copy-start | bytes 98308
  8.8 25.9 %copy-start.2 = (bf16[128,640]{1,0:T(8,128)(2,1)S(1)}, bf16[128,640]{1,0:T(8,128)(2,1)}, u32[]{:S(2)}) copy-start(bf16[128,640]{1,0:T(8,128)(2,1)} %param.16) | copy-start | bytes 491524
  11.2 36.5 %copy-start.1 = (bf16[1,1024,256]{1,2,0:T(8,128)(2,1)}, bf16[1,1024,256]{1,2,0:T(8,128)(2,1)S(1)}, u32[]{:S(2)}) copy-start(bf16[1,1024,256]{1,2,0:T(8,128)(2,1)S(1)} %get-tuple-element.23) | copy-start | bytes 1572868
  11.7 3.5 %collective-permute-start.1 = (bf16[1,32,512]{2,1,0:T(8,128)(2,1)S(1)}, bf16[1,32,512]{2,1,0:T(8,128)(2,1)S(1)}, u32[]{:S(2)}, u32[]{:S(2)}) collective-permute-start(bf16[1,32,512]{2,1,0:T(8,128)(2,1)S(1)} %get-tuple-element.21), channel_id=1, source_target_pairs={{0,64},{64,0},{1,65},{65,1},{2,66},{66,2},{3,67},{67,3},{4,68},{68... | collective-permute-start | bytes 98312 | tf_op jit(solution)/shard_map/ppermute | solution.py:62
  15.9 3.2 %collective-permute-start = (bf16[1,1024,32]{1,2,0:T(8,128)(2,1)S(1)}, bf16[1,1024,32]{1,2,0:T(8,128)(2,1)S(1)}, u32[]{:S(2)}, u32[]{:S(2)}) collective-permute-start(bf16[1,1024,32]{1,2,0:T(8,128)(2,1)S(1)} %get-tuple-element.19), channel_id=1, source_target_pairs={{0,64},{64,0},{1,65},{65,1},{2,66},{66,2},{3,67},{67,3},{4,68},{68... | collective-permute-start | bytes 196616 | tf_op jit(solution)/shard_map/ppermute | solution.py:56
  20.6 27.1 %all-to-all-start.1 = ((bf16[64,2,512]{2,1,0:T(2,128)(2,1)}), bf16[64,2,512]{2,1,0:T(2,128)(2,1)S(1)}, u32[]{:S(2)}, u32[]{:S(2)}) async-start(bf16[64,2,512]{2,1,0:T(2,128)(2,1)} %reshape.89), calls=%async_computation.1 | async-start | bytes 262144 | tf_op jit(solution)/shard_map/all_to_all | solution.py:57
  47.7 63.3 %all-to-all-start = ((bf16[128,2,16,512]{3,2,1,0:T(8,128)(2,1)}), bf16[128,2,16,512]{3,2,1,0:T(8,128)(2,1)}, u32[]{:S(2)}, u32[]{:S(2)}) async-start(bf16[128,2,16,512]{3,2,1,0:T(8,128)(2,1)} %shard_map.113), calls=%async_computation | async-start | bytes 8388608 | tf_op jit(solution)/shard_map/all_to_all | solution.py:69
  117.0 39.1 %all-to-all-start.2 = ((bf16[128,16,512]{2,1,0:T(8,128)(2,1)}), bf16[128,16,512]{2,1,0:T(8,128)(2,1)S(1)}, u32[]{:S(2)}, u32[]{:S(2)}) async-start(bf16[128,16,512]{2,1,0:T(8,128)(2,1)} %bitcast.49), calls=%async_computation.2 | async-start | bytes 4194304 | tf_op jit(solution)/shard_map/all_to_all | solution.py:74
Sparse Core Ops, SparseCore 0:
  16.0 109.8 all-gather.1

commit v14 on v9

--- a/solution.py
+++ b/solution.py
@@ -194,7 +194,7 @@
     tile_rows, columns, chans = pairwise_input.shape
     step_rows = 4
     prod_flat = product_tile.reshape(chans, tile_rows * columns)
-    gate_weight = triangle_projection_weight[:, 4 * chans :]
+    gate_weight = triangle_projection_weight
     hidden = pairwise_up_weight.shape[1]
     row_block = lambda g: (g, 0, 0)
     fixed = lambda g: (0, 0)
@@ -251,14 +251,21 @@
     lax.fori_loop(0, tile_rows, emit, 0)
 
 
-def outer_product(left_gathered, right_gathered, outer_output_weight):
+def outer_operands(left_gathered, outer_output_weight):
     total_rows, tile_rows, channels = left_gathered.shape
-    columns = right_gathered.shape[2]
     pair = outer_output_weight.shape[1]
     left_t = jnp.transpose(left_gathered, (1, 2, 0)).reshape(tile_rows * channels, total_rows)
     weight_t = jnp.transpose(
         outer_output_weight.reshape(channels, channels, pair), (1, 0, 2)
     ).reshape(channels * channels, pair).T
+    return left_t, weight_t
+
+
+def outer_product(left_t, right_gathered, weight_t, tile_rows):
+    channels = left_t.shape[0] // tile_rows
+    total_rows = left_t.shape[1]
+    columns = right_gathered.shape[2]
+    pair = weight_t.shape[0]
     flops = 4 * tile_rows * channels * channels * columns * (total_rows + pair) // 2
     return pl.pallas_call(
         outer_kernel,
@@ -293,15 +300,19 @@
     tri_stack = pair_front(pairwise_input, triangle_projection_weight)
     moved = send_whole(tri_stack)
     product = triangle_product(moved)
-    product, left_gathered = lax.optimization_barrier((product, left_gathered))
+    left_t, weight_t = outer_operands(left_gathered, outer_output_weight)
+    gate_weight = triangle_projection_weight[:, 4 * pairwise_input.shape[2] :]
+    product, left_t, weight_t, gate_weight = lax.optimization_barrier(
+        (product, left_t, weight_t, gate_weight)
+    )
     product_tile = send_back(product)
-    outer_update = outer_product(left_gathered, right_gathered, outer_output_weight)
+    outer_update = outer_product(left_t, right_gathered, weight_t, pairwise_input.shape[0])
     product_tile, outer_update = lax.optimization_barrier((product_tile, outer_update))
     pairwise_output = pair_back(
         pairwise_input,
         product_tile,
         outer_update,
-        triangle_projection_weight,
+        gate_weight,
         triangle_output_weight,
         pairwise_up_weight,
         pairwise_down_weight,

time: 184 us -> 182 us (0.989)
  local copies, waits for them, and re-layouts: 18.8 us -> 16.8 us
    all_to_all x1, waiting for transfers between devices: 53.3 us -> 50.7 us  [send_whole(): lax.all_to_all(tri_stack, both, split_axis=0, concat_axis=0, tiled=True)]
  transfers between devices with their start and end apart: 6 -> 6, of which waited for: 3 -> 5; matrix products, arithmetic and copies ran while one was open for 8% -> 7% of each run, Pallas kernels for 21% -> 21%
where the time goes in v14:
time: 182 us; the launch traced here: 181 us
  waiting for transfers between devices  56.4 us (31%)
  Pallas kernels  55.4 us (30%)
  starting transfers between devices  34.5 us (19%)
  local copies, waits for them, and re-layouts  16.8 us (9%)
  between operations  14.2 us (8%)
  matrix products  2.65 us (1%)
    all_to_all x1, waiting for transfers between devices, send_whole(): lax.all_to_all(tri_stack, both, split_axis=0, concat_axis=0, tiled=True)  50.7 us
    pallas_call x1, Pallas kernels, outer_product(): pl.pallas_call(outer_kernel, out_shape=jax.ShapeDtypeStruct((tile_rows, c...  19.9 us
    pallas_call x1, Pallas kernels, pair_back(): pl.pallas_call(back_kernel, out_shape=jax.ShapeDtypeStruct((tile_rows, co...  17.1 us
    all_to_all x1, starting transfers between devices, gather_sides(): lax.all_to_all(left_pair, 'rows', split_axis=1, concat_axis=0, tiled=True)  14.1 us
    pallas_call x1, Pallas kernels, pair_front(): pl.pallas_call(front_kernel, out_shape=jax.ShapeDtypeStruct((chans, 2, ti...  12.4 us
    all_to_all x1, starting transfers between devices, send_whole(): lax.all_to_all(tri_stack, both, split_axis=0, concat_axis=0, tiled=True)  9.84 us
    all_to_all x1, starting transfers between devices, send_back(): lax.all_to_all(product, ('branch', 'rows'), split_axis=0, concat_axis=0,...  6.81 us
    all_gather x1, local copies, waits for them, and re-layouts, gather_sides(): lax.all_gather(jnp.swapaxes(right_pair, 0, 1), 'rows', axis=1, tiled=True)  6.5 us
  transfers between devices with their start and end apart: 6, of which 5 were waited for; matrix products, arithmetic and copies ran while one was open for 7% of the time, Pallas kernels for 21%

profile of v14, /device:TPU:1, one launch (start us, length us, event | category | flops | bytes accessed | tf_op | source)
XLA Modules:
  0.0 181.1 jit_solution(4568061304877984375)
XLA Ops:
  7.2 0.0 copy-start
  7.2 0.0 all-gather.2.cloned.1.call-start
  7.2 1.3 copy.33
  8.5 0.0 copy-start.3
  8.5 0.1 convert_reduce_fusion
  8.6 0.2 fusion.8
  8.8 0.0 copy-done
  8.8 0.0 copy-start.2
  8.8 2.4 %convert_reduce_fusion.1 = (f32[1024]{0:T(1024)S(1)}, bf16[1,1024,256]{1,2,0:T(8,128)(2,1)S(1)}) fusion(bf16[1024,256]{1,0:T(8,128)(2,1)S(1)} %copy-done, bf16[256,1024]{1,0:T(8,128)(2,1)} %param.12, bf16[1,1024,256]{1,2,0:T(8,128)(2,1)S(1)} %copy.33, f32[1024]{0:T(1024)S(1)} %add_rsqrt_fusion.1, f32[1024]{0:T(1024)S(1)} %broadcast_multiply_fusion.1), kind=kOutput, calls=%fused_computation.7 | convolution fusion | flops 1078197248 | bytes 2109440 | tf_op jit(solution)/shard_map/dot_general | solution.py:31
  11.2 0.2 fusion.10
  11.4 0.0 copy-done.3
  11.4 0.3 fusion.7
  11.7 2.2 %collective-permute-start.1 = (bf16[1,32,512]{2,1,0:T(8,128)(2,1)S(1)}, bf16[1,32,512]{2,1,0:T(8,128)(2,1)S(1)}, u32[]{:S(2)}, u32[]{:S(2)}) collective-permute-start(bf16[1,32,512]{2,1,0:T(8,128)(2,1)S(1)} %get-tuple-element.25), channel_id=1, source_target_pairs={{0,64},{64,0},{1,65},{65,1},{2,66},{66,2},{3,67},{67,3},{4,68},{68... | collective-permute-start | bytes 98312 | tf_op jit(solution)/shard_map/ppermute | solution.py:62
  13.9 1.3 collective-permute-done.1
  15.2 0.6 fusion.23
  15.9 0.0 all-gather.2.cloned.1.call-update
  15.9 1.5 collective-permute-start
  17.5 1.7 collective-permute-done
  19.1 0.4 copy.35
  19.5 1.1 reshape.89
  20.6 14.1 %all-to-all-start.1 = ((bf16[64,2,512]{2,1,0:T(2,128)(2,1)}), bf16[64,2,512]{2,1,0:T(2,128)(2,1)S(1)}, u32[]{:S(2)}, u32[]{:S(2)}) async-start(bf16[64,2,512]{2,1,0:T(2,128)(2,1)} %reshape.89), calls=%async_computation.1 | async-start | bytes 262144 | tf_op jit(solution)/shard_map/all_to_all | solution.py:57
  34.7 0.0 copy-done.2
  34.7 0.8 copy.34
  35.5 12.4 %shard_map.113 = bf16[128,2,16,512]{3,2,1,0:T(8,128)(2,1)} custom-call(bf16[16,512,128]{2,1,0:T(8,128)(2,1)} %pair_ref.1, bf16[4,128,128]{2,1,0:T(8,128)(2,1)} %bitcast.54), custom_call_target="tpu_custom_call" | custom-call | flops 1073741824 | bytes 6291456 | tf_op jit(solution)/shard_map/pallas_call | solution.py:109
  47.9 0.0 copy-start.1
  47.9 0.0 all-to-all-done.1
  47.9 9.8 %all-to-all-start = ((bf16[128,2,16,512]{3,2,1,0:T(8,128)(2,1)}), bf16[128,2,16,512]{3,2,1,0:T(8,128)(2,1)}, u32[]{:S(2)}, u32[]{:S(2)}) async-start(bf16[128,2,16,512]{3,2,1,0:T(8,128)(2,1)} %shard_map.113), calls=%async_computation | async-start | bytes 8388608 | tf_op jit(solution)/shard_map/all_to_all | solution.py:69
  57.8 0.6 slice.16.wg_ref
  58.4 0.0 copy-done.1
  58.4 0.1 copy.39
  58.5 0.9 copy.40
  59.4 0.3 reshape.90
  59.7 0.1 copy.36
  59.8 1.1 copy.38
  60.9 50.7 %all-to-all-done.moved_ref = bf16[128,2,16,512]{3,2,1,0:T(8,128)(2,1)} async-done(((bf16[128,2,16,512]{3,2,1,0:T(8,128)(2,1)}), bf16[128,2,16,512]{3,2,1,0:T(8,128)(2,1)}, u32[]{:S(2)}, u32[]{:S(2)}) %all-to-all-start) | async-done | bytes 4194336 | tf_op jit(solution)/shard_map/all_to_all | solution.py:69
  111.5 5.9 %shard_map.114 = bf16[2,1024,512]{2,1,0:T(8,128)(2,1)} custom-call(bf16[128,2,16,512]{3,2,1,0:T(8,128)(2,1)} %all-to-all-done.moved_ref), custom_call_target="tpu_custom_call" | custom-call | flops 2147483648 | bytes 6291456 | tf_op jit(solution)/shard_map/pallas_call | solution.py:151
  117.5 6.8 %all-to-all-start.2 = ((bf16[128,16,512]{2,1,0:T(8,128)(2,1)}), bf16[128,16,512]{2,1,0:T(8,128)(2,1)S(1)}, u32[]{:S(2)}, u32[]{:S(2)}) async-start(bf16[128,16,512]{2,1,0:T(8,128)(2,1)} %bitcast.50), calls=%async_computation.2 | async-start | bytes 4194304 | tf_op jit(solution)/shard_map/all_to_all | solution.py:74
  124.3 1.0 copy.42
  125.3 0.9 all-gather.2.cloned.1.call-done
  126.2 6.5 %copy.41.r_ref = bf16[32,128,512]{2,1,0:T(8,128)(2,1)} copy(bf16[32,128,512]{2,0,1:T(8,128)(2,1)} %all-gather.2.cloned.1.call-done) | data formatting | bytes 8388608 | tf_op jit(solution)/shard_map/all_gather | solution.py:63
  132.7 19.9 %shard_map.115.outer_ref = f32[16,512,128]{2,1,0:T(8,128)} custom-call(bf16[512,128]{1,0:T(8,128)(2,1)} %bitcast.57, bf16[32,128,512]{2,1,0:T(8,128)(2,1)} %copy.41.r_ref, bf16[128,1024]{1,0:T(8,128)(2,1)} %bitcast.56), custom_call_target="tpu_custom_call" | custom-call | flops 4294967296 | bytes 8388608 | tf_op jit(solution)/shard_map/pallas_call | solution.py:270
  152.6 1.8 all-to-all-done.2
  154.4 2.7 %copy.43 = bf16[16,8,16,512]{3,1,2,0:T(8,128)(2,1)} copy(bf16[16,8,16,512]{3,2,1,0:T(8,128)(2,1)S(1)} %bitcast.46) | data formatting | bytes 4194304
  157.1 17.1 %shard_map.116 = bf16[16,512,128]{2,1,0:T(8,128)(2,1)} custom-call(bf16[128,8192]{1,0:T(8,128)(2,1)} %bitcast.51, bf16[16,512,128]{2,1,0:T(8,128)(2,1)} %pair_ref.1, f32[16,512,128]{2,1,0:T(8,128)} %shard_map.115.outer_ref, bf16[128,128]{1,0:T(8,128)(2,1)} %wo_ref.1, bf16[128,128]{1,0:T(8,128)(2,1)} %slice.16.wg_ref, bf16[128,512]{1,0:T(8,128)(2,1)} %wu_ref.1, ...), custom_call_target="tpu_custom_call" | custom-call | flops 2952790016 | bytes 10485760 | tf_op jit(solution)/shard_map/pallas_call | solution.py:201
  (9 shorter events, 0.1 us)
Async XLA Ops:
  7.2 1.7 copy-start
  7.2 119.0 %all-gather.2.cloned.1.call-start = ((), (), s32[]{:S(2)}) async-start(), calls=%async_computation.3 | async-start | bytes 4259840 | tf_op jit(solution)/shard_map/all_gather | solution.py:63
  8.5 2.9 %copy-start.3 = (bf16[256,64]{0,1:T(8,128)(2,1)S(1)}, bf16[256,64]{0,1:T(8,128)(2,1)}, u32[]{:S(2)}) copy-start(bf16[256,64]{0,1:T(8,128)(2,1)} %param.14) | copy-start | bytes 98308
  8.8 25.9 %copy-start.2 = (bf16[128,640]{1,0:T(8,128)(2,1)S(1)}, bf16[128,640]{1,0:T(8,128)(2,1)}, u32[]{:S(2)}) copy-start(bf16[128,640]{1,0:T(8,128)(2,1)} %param.16) | copy-start | bytes 491524
  11.7 3.5 %collective-permute-start.1 = (bf16[1,32,512]{2,1,0:T(8,128)(2,1)S(1)}, bf16[1,32,512]{2,1,0:T(8,128)(2,1)S(1)}, u32[]{:S(2)}, u32[]{:S(2)}) collective-permute-start(bf16[1,32,512]{2,1,0:T(8,128)(2,1)S(1)} %get-tuple-element.25), channel_id=1, source_target_pairs={{0,64},{64,0},{1,65},{65,1},{2,66},{66,2},{3,67},{67,3},{4,68},{68... | collective-permute-start | bytes 98312 | tf_op jit(solution)/shard_map/ppermute | solution.py:62
  15.9 3.2 %collective-permute-start = (bf16[1,1024,32]{1,2,0:T(8,128)(2,1)S(1)}, bf16[1,1024,32]{1,2,0:T(8,128)(2,1)S(1)}, u32[]{:S(2)}, u32[]{:S(2)}) collective-permute-start(bf16[1,1024,32]{1,2,0:T(8,128)(2,1)S(1)} %get-tuple-element.23), channel_id=1, source_target_pairs={{0,64},{64,0},{1,65},{65,1},{2,66},{66,2},{3,67},{67,3},{4,68},{68... | collective-permute-start | bytes 196616 | tf_op jit(solution)/shard_map/ppermute | solution.py:56
  20.6 27.3 %all-to-all-start.1 = ((bf16[64,2,512]{2,1,0:T(2,128)(2,1)}), bf16[64,2,512]{2,1,0:T(2,128)(2,1)S(1)}, u32[]{:S(2)}, u32[]{:S(2)}) async-start(bf16[64,2,512]{2,1,0:T(2,128)(2,1)} %reshape.89), calls=%async_computation.1 | async-start | bytes 262144 | tf_op jit(solution)/shard_map/all_to_all | solution.py:57
  47.9 10.5 %copy-start.1 = (bf16[1024,128]{1,0:T(8,128)(2,1)S(1)}, bf16[1024,128]{1,0:T(8,128)(2,1)}, u32[]{:S(2)}) copy-start(bf16[1024,128]{1,0:T(8,128)(2,1)} %param.15) | copy-start | bytes 786436
  47.9 63.6 %all-to-all-start = ((bf16[128,2,16,512]{3,2,1,0:T(8,128)(2,1)}), bf16[128,2,16,512]{3,2,1,0:T(8,128)(2,1)}, u32[]{:S(2)}, u32[]{:S(2)}) async-start(bf16[128,2,16,512]{3,2,1,0:T(8,128)(2,1)} %shard_map.113), calls=%async_computation | async-start | bytes 8388608 | tf_op jit(solution)/shard_map/all_to_all | solution.py:69
  117.5 37.0 %all-to-all-start.2 = ((bf16[128,16,512]{2,1,0:T(8,128)(2,1)}), bf16[128,16,512]{2,1,0:T(8,128)(2,1)S(1)}, u32[]{:S(2)}, u32[]{:S(2)}) async-start(bf16[128,16,512]{2,1,0:T(8,128)(2,1)} %bitcast.50), calls=%async_computation.2 | async-start | bytes 4194304 | tf_op jit(solution)/shard_map/all_to_all | solution.py:74
Sparse Core Ops, SparseCore 0:
  16.0 110.1 all-gather.1

commit v15 on v14

--- a/solution.py
+++ b/solution.py
@@ -53,8 +53,13 @@
 
 def gather_sides(left_side, right_side):
     swap = [(0, 1), (1, 0)]
-    left_pair = branch_pair(left_side, lax.ppermute(left_side, "branch", swap))
-    left_gathered = lax.all_to_all(left_pair, "rows", split_axis=1, concat_axis=0, tiled=True)
+    halves = lax.axis_size("branch")
+    n_rows = lax.axis_size("rows")
+    left_dest = jnp.tile(left_side.reshape(n_rows, -1, left_side.shape[-1]), (halves, 1, 1))
+    left_src = lax.all_to_all(left_dest, ("branch", "rows"), split_axis=0, concat_axis=0, tiled=True)
+    left_gathered = jnp.swapaxes(
+        left_src.reshape(halves, n_rows, -1, left_side.shape[-1]), 0, 1
+    ).reshape(halves * n_rows, -1, left_side.shape[-1])
     half = right_side.shape[2] // 2
     me = lax.axis_index("branch")
     keep = lax.dynamic_slice_in_dim(right_side, me * half, half, axis=2)

time: 182 us -> 204 us (1.12)
  the two profiles are of different devices: /device:TPU:1 before, /device:TPU:31 now
where the time goes in v15:
time: 204 us
  waiting for transfers between devices  82 us (40%)
  Pallas kernels  55.4 us (27%)
  starting transfers between devices  30.6 us (15%)
  local copies, waits for them, and re-layouts  17.8 us (9%)
  between operations  14.2 us (7%)
  matrix products  2.65 us (1%)
    all_to_all x1, waiting for transfers between devices, send_whole(): lax.all_to_all(tri_stack, both, split_axis=0, concat_axis=0, tiled=True)  48.5 us
    all_gather x1, waiting for transfers between devices, gather_sides(): lax.all_gather(jnp.swapaxes(right_pair, 0, 1), 'rows', axis=1, tiled=True)  31.2 us
    pallas_call x1, Pallas kernels, outer_product(): pl.pallas_call(outer_kernel, out_shape=jax.ShapeDtypeStruct((tile_rows, c...  19.9 us
    pallas_call x1, Pallas kernels, pair_back(): pl.pallas_call(back_kernel, out_shape=jax.ShapeDtypeStruct((tile_rows, co...  17.1 us
    pallas_call x1, Pallas kernels, pair_front(): pl.pallas_call(front_kernel, out_shape=jax.ShapeDtypeStruct((chans, 2, ti...  12.4 us
    all_to_all x1, starting transfers between devices, gather_sides(): lax.all_to_all(left_dest, ('branch', 'rows'), split_axis=0, concat_axis=0...  11.7 us
    all_to_all x1, starting transfers between devices, send_whole(): lax.all_to_all(tri_stack, both, split_axis=0, concat_axis=0, tiled=True)  10.3 us
    all_to_all x1, starting transfers between devices, send_back(): lax.all_to_all(product, ('branch', 'rows'), split_axis=0, concat_axis=0,...  8.03 us
  transfers between devices with their start and end apart: 5, of which 3 were waited for; matrix products, arithmetic and copies ran while one was open for 7% of the time, Pallas kernels for 19%

profile of v15, /device:TPU:31, one launch (start us, length us, event | category | flops | bytes accessed | tf_op | source)
XLA Modules:
  0.0 203.7 jit_solution(689144654171920688)
XLA Ops:
  7.2 0.0 copy-start
  7.2 0.0 all-gather.2.cloned.1.call-start
  7.2 1.3 copy.36
  8.5 0.0 copy-start.3
  8.5 0.1 convert_reduce_fusion
  8.6 0.2 fusion.8
  8.8 0.0 copy-done
  8.8 0.0 copy-start.2
  8.8 2.4 %convert_reduce_fusion.1 = (f32[1024]{0:T(1024)S(1)}, bf16[1,1024,256]{1,2,0:T(8,128)(2,1)S(1)}) fusion(bf16[1024,256]{1,0:T(8,128)(2,1)S(1)} %copy-done, bf16[256,1024]{1,0:T(8,128)(2,1)} %param.12, bf16[1,1024,256]{1,2,0:T(8,128)(2,1)S(1)} %copy.36, f32[1024]{0:T(1024)S(1)} %add_rsqrt_fusion.1, f32[1024]{0:T(1024)S(1)} %broadcast_multiply_fusion.1), kind=kOutput, calls=%fused_computation.7 | convolution fusion | flops 1078197248 | bytes 2109440 | tf_op jit(solution)/shard_map/dot_general | solution.py:31
  11.2 0.2 fusion.10
  11.4 0.0 copy-done.3
  11.4 0.3 fusion.7
  11.7 0.5 collective-permute-start
  12.3 2.3 %collective-permute-done = bf16[1,32,512]{2,1,0:T(8,128)(2,1)S(1)} collective-permute-done((bf16[1,32,512]{2,1,0:T(8,128)(2,1)S(1)}, bf16[1,32,512]{2,1,0:T(8,128)(2,1)S(1)}, u32[]{:S(2)}, u32[]{:S(2)}) %collective-permute-start) | collective-permute-done | bytes 32800 | tf_op jit(solution)/shard_map/ppermute | solution.py:67
  14.6 0.6 fusion.23
  15.2 0.0 all-gather.2.cloned.1.call-update
  15.2 0.2 copy.38
  15.4 0.1 tile.11
  15.5 1.0 reshape.101
  16.5 11.7 %all-to-all-start.1 = ((bf16[128,2,256]{2,1,0:T(2,128)(2,1)}), bf16[128,2,256]{2,1,0:T(2,128)(2,1)S(1)}, u32[]{:S(2)}, u32[]{:S(2)}) async-start(bf16[128,2,256]{2,1,0:T(2,128)(2,1)} %reshape.101), calls=%async_computation.1 | async-start | bytes 262144 | tf_op jit(solution)/shard_map/all_to_all | solution.py:59
  28.2 0.0 copy-done.2
  28.2 0.8 copy.37
  29.0 12.4 %shard_map.113 = bf16[128,2,16,512]{3,2,1,0:T(8,128)(2,1)} custom-call(bf16[16,512,128]{2,1,0:T(8,128)(2,1)} %pair_ref.1, bf16[4,128,128]{2,1,0:T(8,128)(2,1)} %bitcast.54), custom_call_target="tpu_custom_call" | custom-call | flops 1073741824 | bytes 6291456 | tf_op jit(solution)/shard_map/pallas_call | solution.py:114
  41.4 0.0 copy-start.1
  41.4 0.0 all-to-all-done.1
  41.4 10.3 %all-to-all-start = ((bf16[128,2,16,512]{3,2,1,0:T(8,128)(2,1)}), bf16[128,2,16,512]{3,2,1,0:T(8,128)(2,1)}, u32[]{:S(2)}, u32[]{:S(2)}) async-start(bf16[128,2,16,512]{3,2,1,0:T(8,128)(2,1)} %shard_map.113), calls=%async_computation | async-start | bytes 8388608 | tf_op jit(solution)/shard_map/all_to_all | solution.py:74
  51.7 0.6 slice.16.wg_ref
  52.3 0.0 copy-done.1
  52.3 0.1 copy.42
  52.4 0.9 copy.43
  53.3 0.3 reshape.102
  53.6 0.5 copy.46
  54.1 0.8 copy.40
  54.9 1.1 copy.41
  56.0 48.5 %all-to-all-done.moved_ref = bf16[128,2,16,512]{3,2,1,0:T(8,128)(2,1)} async-done(((bf16[128,2,16,512]{3,2,1,0:T(8,128)(2,1)}), bf16[128,2,16,512]{3,2,1,0:T(8,128)(2,1)}, u32[]{:S(2)}, u32[]{:S(2)}) %all-to-all-start) | async-done | bytes 4194336 | tf_op jit(solution)/shard_map/all_to_all | solution.py:74
  104.5 5.9 %shard_map.114 = bf16[2,1024,512]{2,1,0:T(8,128)(2,1)} custom-call(bf16[128,2,16,512]{3,2,1,0:T(8,128)(2,1)} %all-to-all-done.moved_ref), custom_call_target="tpu_custom_call" | custom-call | flops 2147483648 | bytes 6291456 | tf_op jit(solution)/shard_map/pallas_call | solution.py:156
  110.4 8.0 %all-to-all-start.2 = ((bf16[128,16,512]{2,1,0:T(8,128)(2,1)}), bf16[128,16,512]{2,1,0:T(8,128)(2,1)S(1)}, u32[]{:S(2)}, u32[]{:S(2)}) async-start(bf16[128,16,512]{2,1,0:T(8,128)(2,1)} %bitcast.49), calls=%async_computation.2 | async-start | bytes 4194304 | tf_op jit(solution)/shard_map/all_to_all | solution.py:79
  118.4 1.0 copy.45
  119.4 31.2 %all-gather.2.cloned.1.call-done = bf16[32,128,512]{2,0,1:T(8,128)(2,1)} async-done(((bf16[32,2,512]{2,0,1:T(8,128)(2,1)}), bf16[32,128,512]{2,0,1:T(8,128)(2,1)}) %all-gather.2.cloned.1.call-update) | async-done | bytes 4194320 | tf_op jit(solution)/shard_map/all_gather | solution.py:68
  150.6 6.5 %copy.44.r_ref = bf16[32,128,512]{2,1,0:T(8,128)(2,1)} copy(bf16[32,128,512]{2,0,1:T(8,128)(2,1)} %all-gather.2.cloned.1.call-done) | data formatting | bytes 8388608 | tf_op jit(solution)/shard_map/all_gather | solution.py:68
  157.1 19.9 %shard_map.115.outer_ref = f32[16,512,128]{2,1,0:T(8,128)} custom-call(bf16[512,128]{1,0:T(8,128)(2,1)} %bitcast.57, bf16[32,128,512]{2,1,0:T(8,128)(2,1)} %copy.44.r_ref, bf16[128,1024]{1,0:T(8,128)(2,1)} %bitcast.56), custom_call_target="tpu_custom_call" | custom-call | flops 4294967296 | bytes 8388608 | tf_op jit(solution)/shard_map/pallas_call | solution.py:275
  177.0 0.0 all-to-all-done.2
  177.0 2.7 %copy.47 = bf16[16,8,16,512]{3,1,2,0:T(8,128)(2,1)} copy(bf16[16,8,16,512]{3,2,1,0:T(8,128)(2,1)S(1)} %bitcast.45) | data formatting | bytes 4194304
  179.7 17.1 %shard_map.116 = bf16[16,512,128]{2,1,0:T(8,128)(2,1)} custom-call(bf16[128,8192]{1,0:T(8,128)(2,1)} %bitcast.50, bf16[16,512,128]{2,1,0:T(8,128)(2,1)} %pair_ref.1, f32[16,512,128]{2,1,0:T(8,128)} %shard_map.115.outer_ref, bf16[128,128]{1,0:T(8,128)(2,1)} %wo_ref.1, bf16[128,128]{1,0:T(8,128)(2,1)} %slice.16.wg_ref, bf16[128,512]{1,0:T(8,128)(2,1)} %wu_ref.1, ...), custom_call_target="tpu_custom_call" | custom-call | flops 2952790016 | bytes 10485760 | tf_op jit(solution)/shard_map/pallas_call | solution.py:206
  (7 shorter events, 0.1 us)
Async XLA Ops:
  7.2 1.7 copy-start
  7.2 143.4 %all-gather.2.cloned.1.call-start = ((), (), s32[]{:S(2)}) async-start(), calls=%async_computation.3 | async-start | bytes 4259840 | tf_op jit(solution)/shard_map/all_gather | solution.py:68
  8.5 2.9 %copy-start.3 = (bf16[256,64]{0,1:T(8,128)(2,1)S(1)}, bf16[256,64]{0,1:T(8,128)(2,1)}, u32[]{:S(2)}) copy-start(bf16[256,64]{0,1:T(8,128)(2,1)} %param.14) | copy-start | bytes 98308
  8.8 19.4 %copy-start.2 = (bf16[128,640]{1,0:T(8,128)(2,1)S(1)}, bf16[128,640]{1,0:T(8,128)(2,1)}, u32[]{:S(2)}) copy-start(bf16[128,640]{1,0:T(8,128)(2,1)} %param.16) | copy-start | bytes 491524
  11.7 2.8 %collective-permute-start = (bf16[1,32,512]{2,1,0:T(8,128)(2,1)S(1)}, bf16[1,32,512]{2,1,0:T(8,128)(2,1)S(1)}, u32[]{:S(2)}, u32[]{:S(2)}) collective-permute-start(bf16[1,32,512]{2,1,0:T(8,128)(2,1)S(1)} %get-tuple-element.25), channel_id=1, source_target_pairs={{0,64},{64,0},{1,65},{65,1},{2,66},{66,2},{3,67},{67,3},{4,68},{68... | collective-permute-start | bytes 98312 | tf_op jit(solution)/shard_map/ppermute | solution.py:67
  16.5 24.9 %all-to-all-start.1 = ((bf16[128,2,256]{2,1,0:T(2,128)(2,1)}), bf16[128,2,256]{2,1,0:T(2,128)(2,1)S(1)}, u32[]{:S(2)}, u32[]{:S(2)}) async-start(bf16[128,2,256]{2,1,0:T(2,128)(2,1)} %reshape.101), calls=%async_computation.1 | async-start | bytes 262144 | tf_op jit(solution)/shard_map/all_to_all | solution.py:59
  41.4 10.9 %copy-start.1 = (bf16[1024,128]{1,0:T(8,128)(2,1)S(1)}, bf16[1024,128]{1,0:T(8,128)(2,1)}, u32[]{:S(2)}) copy-start(bf16[1024,128]{1,0:T(8,128)(2,1)} %param.15) | copy-start | bytes 786436
  41.4 63.0 %all-to-all-start = ((bf16[128,2,16,512]{3,2,1,0:T(8,128)(2,1)}), bf16[128,2,16,512]{3,2,1,0:T(8,128)(2,1)}, u32[]{:S(2)}, u32[]{:S(2)}) async-start(bf16[128,2,16,512]{3,2,1,0:T(8,128)(2,1)} %shard_map.113), calls=%async_computation | async-start | bytes 8388608 | tf_op jit(solution)/shard_map/all_to_all | solution.py:74
  110.4 66.6 %all-to-all-start.2 = ((bf16[128,16,512]{2,1,0:T(8,128)(2,1)}), bf16[128,16,512]{2,1,0:T(8,128)(2,1)S(1)}, u32[]{:S(2)}, u32[]{:S(2)}) async-start(bf16[128,16,512]{2,1,0:T(8,128)(2,1)} %bitcast.49), calls=%async_computation.2 | async-start | bytes 4194304 | tf_op jit(solution)/shard_map/all_to_all | solution.py:79
Sparse Core Ops, SparseCore 0:
  15.4 135.1 all-gather.1

commit v16 on v14

--- a/solution.py
+++ b/solution.py
@@ -192,7 +192,7 @@
     pairwise_down_weight,
 ):
     tile_rows, columns, chans = pairwise_input.shape
-    step_rows = 4
+    step_rows = 8
     prod_flat = product_tile.reshape(chans, tile_rows * columns)
     gate_weight = triangle_projection_weight
     hidden = pairwise_up_weight.shape[1]

time: 182 us -> 182 us (level)
  no operation moved by 1% of the time
where the time goes in v16:
time: 182 us; the launch traced here: 181 us
  waiting for transfers between devices  56.4 us (31%)
  Pallas kernels  55.6 us (31%)
  starting transfers between devices  34.5 us (19%)
  local copies, waits for them, and re-layouts  16.8 us (9%)
  between operations  14.2 us (8%)
  matrix products  2.65 us (1%)
    all_to_all x1, waiting for transfers between devices, send_whole(): lax.all_to_all(tri_stack, both, split_axis=0, concat_axis=0, tiled=True)  50.7 us
    pallas_call x1, Pallas kernels, outer_product(): pl.pallas_call(outer_kernel, out_shape=jax.ShapeDtypeStruct((tile_rows, c...  19.9 us
    pallas_call x1, Pallas kernels, pair_back(): pl.pallas_call(back_kernel, out_shape=jax.ShapeDtypeStruct((tile_rows, co...  17.4 us
    all_to_all x1, starting transfers between devices, gather_sides(): lax.all_to_all(left_pair, 'rows', split_axis=1, concat_axis=0, tiled=True)  14.1 us
    pallas_call x1, Pallas kernels, pair_front(): pl.pallas_call(front_kernel, out_shape=jax.ShapeDtypeStruct((chans, 2, ti...  12.4 us
    all_to_all x1, starting transfers between devices, send_whole(): lax.all_to_all(tri_stack, both, split_axis=0, concat_axis=0, tiled=True)  9.84 us
    all_to_all x1, starting transfers between devices, send_back(): lax.all_to_all(product, ('branch', 'rows'), split_axis=0, concat_axis=0,...  6.81 us
    all_gather x1, local copies, waits for them, and re-layouts, gather_sides(): lax.all_gather(jnp.swapaxes(right_pair, 0, 1), 'rows', axis=1, tiled=True)  6.5 us
  transfers between devices with their start and end apart: 6, of which 5 were waited for; matrix products, arithmetic and copies ran while one was open for 7% of the time, Pallas kernels for 21%

profile of v16, /device:TPU:1, one launch (start us, length us, event | category | flops | bytes accessed | tf_op | source)
XLA Modules:
  0.0 181.3 jit_solution(1849436679864089732)
XLA Ops:
  7.2 0.0 copy-start
  7.2 0.0 all-gather.2.cloned.1.call-start
  7.2 1.3 copy.33
  8.5 0.0 copy-start.3
  8.5 0.1 convert_reduce_fusion
  8.6 0.2 fusion.8
  8.8 0.0 copy-done
  8.8 0.0 copy-start.2
  8.8 2.4 %convert_reduce_fusion.1 = (f32[1024]{0:T(1024)S(1)}, bf16[1,1024,256]{1,2,0:T(8,128)(2,1)S(1)}) fusion(bf16[1024,256]{1,0:T(8,128)(2,1)S(1)} %copy-done, bf16[256,1024]{1,0:T(8,128)(2,1)} %param.12, bf16[1,1024,256]{1,2,0:T(8,128)(2,1)S(1)} %copy.33, f32[1024]{0:T(1024)S(1)} %add_rsqrt_fusion.1, f32[1024]{0:T(1024)S(1)} %broadcast_multiply_fusion.1), kind=kOutput, calls=%fused_computation.7 | convolution fusion | flops 1078197248 | bytes 2109440 | tf_op jit(solution)/shard_map/dot_general | solution.py:31
  11.2 0.2 fusion.10
  11.4 0.0 copy-done.3
  11.4 0.3 fusion.7
  11.7 2.2 %collective-permute-start.1 = (bf16[1,32,512]{2,1,0:T(8,128)(2,1)S(1)}, bf16[1,32,512]{2,1,0:T(8,128)(2,1)S(1)}, u32[]{:S(2)}, u32[]{:S(2)}) collective-permute-start(bf16[1,32,512]{2,1,0:T(8,128)(2,1)S(1)} %get-tuple-element.25), channel_id=1, source_target_pairs={{0,64},{64,0},{1,65},{65,1},{2,66},{66,2},{3,67},{67,3},{4,68},{68... | collective-permute-start | bytes 98312 | tf_op jit(solution)/shard_map/ppermute | solution.py:62
  13.9 1.3 collective-permute-done.1
  15.2 0.6 fusion.23
  15.9 0.0 all-gather.2.cloned.1.call-update
  15.9 1.5 collective-permute-start
  17.5 1.7 collective-permute-done
  19.1 0.4 copy.35
  19.5 1.1 reshape.89
  20.6 14.1 %all-to-all-start.1 = ((bf16[64,2,512]{2,1,0:T(2,128)(2,1)}), bf16[64,2,512]{2,1,0:T(2,128)(2,1)S(1)}, u32[]{:S(2)}, u32[]{:S(2)}) async-start(bf16[64,2,512]{2,1,0:T(2,128)(2,1)} %reshape.89), calls=%async_computation.1 | async-start | bytes 262144 | tf_op jit(solution)/shard_map/all_to_all | solution.py:57
  34.7 0.0 copy-done.2
  34.7 0.8 copy.34
  35.5 12.4 %shard_map.113 = bf16[128,2,16,512]{3,2,1,0:T(8,128)(2,1)} custom-call(bf16[16,512,128]{2,1,0:T(8,128)(2,1)} %pair_ref.1, bf16[4,128,128]{2,1,0:T(8,128)(2,1)} %bitcast.54), custom_call_target="tpu_custom_call" | custom-call | flops 1073741824 | bytes 6291456 | tf_op jit(solution)/shard_map/pallas_call | solution.py:109
  47.9 0.0 copy-start.1
  47.9 0.0 all-to-all-done.1
  47.9 9.8 %all-to-all-start = ((bf16[128,2,16,512]{3,2,1,0:T(8,128)(2,1)}), bf16[128,2,16,512]{3,2,1,0:T(8,128)(2,1)}, u32[]{:S(2)}, u32[]{:S(2)}) async-start(bf16[128,2,16,512]{3,2,1,0:T(8,128)(2,1)} %shard_map.113), calls=%async_computation | async-start | bytes 8388608 | tf_op jit(solution)/shard_map/all_to_all | solution.py:69
  57.8 0.6 slice.16.wg_ref
  58.4 0.0 copy-done.1
  58.4 0.1 copy.39
  58.5 0.9 copy.40
  59.4 0.3 reshape.90
  59.7 0.1 copy.36
  59.8 1.1 copy.38
  60.9 50.7 %all-to-all-done.moved_ref = bf16[128,2,16,512]{3,2,1,0:T(8,128)(2,1)} async-done(((bf16[128,2,16,512]{3,2,1,0:T(8,128)(2,1)}), bf16[128,2,16,512]{3,2,1,0:T(8,128)(2,1)}, u32[]{:S(2)}, u32[]{:S(2)}) %all-to-all-start) | async-done | bytes 4194336 | tf_op jit(solution)/shard_map/all_to_all | solution.py:69
  111.5 5.9 %shard_map.114 = bf16[2,1024,512]{2,1,0:T(8,128)(2,1)} custom-call(bf16[128,2,16,512]{3,2,1,0:T(8,128)(2,1)} %all-to-all-done.moved_ref), custom_call_target="tpu_custom_call" | custom-call | flops 2147483648 | bytes 6291456 | tf_op jit(solution)/shard_map/pallas_call | solution.py:151
  117.5 6.8 %all-to-all-start.2 = ((bf16[128,16,512]{2,1,0:T(8,128)(2,1)}), bf16[128,16,512]{2,1,0:T(8,128)(2,1)S(1)}, u32[]{:S(2)}, u32[]{:S(2)}) async-start(bf16[128,16,512]{2,1,0:T(8,128)(2,1)} %bitcast.50), calls=%async_computation.2 | async-start | bytes 4194304 | tf_op jit(solution)/shard_map/all_to_all | solution.py:74
  124.3 1.0 copy.42
  125.3 0.9 all-gather.2.cloned.1.call-done
  126.2 6.5 %copy.41.r_ref = bf16[32,128,512]{2,1,0:T(8,128)(2,1)} copy(bf16[32,128,512]{2,0,1:T(8,128)(2,1)} %all-gather.2.cloned.1.call-done) | data formatting | bytes 8388608 | tf_op jit(solution)/shard_map/all_gather | solution.py:63
  132.7 19.9 %shard_map.115.outer_ref = f32[16,512,128]{2,1,0:T(8,128)} custom-call(bf16[512,128]{1,0:T(8,128)(2,1)} %bitcast.57, bf16[32,128,512]{2,1,0:T(8,128)(2,1)} %copy.41.r_ref, bf16[128,1024]{1,0:T(8,128)(2,1)} %bitcast.56), custom_call_target="tpu_custom_call" | custom-call | flops 4294967296 | bytes 8388608 | tf_op jit(solution)/shard_map/pallas_call | solution.py:270
  152.6 1.8 all-to-all-done.2
  154.4 2.7 %copy.43 = bf16[16,8,16,512]{3,1,2,0:T(8,128)(2,1)} copy(bf16[16,8,16,512]{3,2,1,0:T(8,128)(2,1)S(1)} %bitcast.46) | data formatting | bytes 4194304
  157.1 17.4 %shard_map.116 = bf16[16,512,128]{2,1,0:T(8,128)(2,1)} custom-call(bf16[128,8192]{1,0:T(8,128)(2,1)} %bitcast.51, bf16[16,512,128]{2,1,0:T(8,128)(2,1)} %pair_ref.1, f32[16,512,128]{2,1,0:T(8,128)} %shard_map.115.outer_ref, bf16[128,128]{1,0:T(8,128)(2,1)} %wo_ref.1, bf16[128,128]{1,0:T(8,128)(2,1)} %slice.16.wg_ref, bf16[128,512]{1,0:T(8,128)(2,1)} %wu_ref.1, ...), custom_call_target="tpu_custom_call" | custom-call | flops 2952790016 | bytes 10485760 | tf_op jit(solution)/shard_map/pallas_call | solution.py:201
  (9 shorter events, 0.1 us)
Async XLA Ops:
  7.2 1.7 copy-start
  7.2 119.0 %all-gather.2.cloned.1.call-start = ((), (), s32[]{:S(2)}) async-start(), calls=%async_computation.3 | async-start | bytes 4259840 | tf_op jit(solution)/shard_map/all_gather | solution.py:63
  8.5 2.9 %copy-start.3 = (bf16[256,64]{0,1:T(8,128)(2,1)S(1)}, bf16[256,64]{0,1:T(8,128)(2,1)}, u32[]{:S(2)}) copy-start(bf16[256,64]{0,1:T(8,128)(2,1)} %param.14) | copy-start | bytes 98308
  8.8 25.9 %copy-start.2 = (bf16[128,640]{1,0:T(8,128)(2,1)S(1)}, bf16[128,640]{1,0:T(8,128)(2,1)}, u32[]{:S(2)}) copy-start(bf16[128,640]{1,0:T(8,128)(2,1)} %param.16) | copy-start | bytes 491524
  11.7 3.5 %collective-permute-start.1 = (bf16[1,32,512]{2,1,0:T(8,128)(2,1)S(1)}, bf16[1,32,512]{2,1,0:T(8,128)(2,1)S(1)}, u32[]{:S(2)}, u32[]{:S(2)}) collective-permute-start(bf16[1,32,512]{2,1,0:T(8,128)(2,1)S(1)} %get-tuple-element.25), channel_id=1, source_target_pairs={{0,64},{64,0},{1,65},{65,1},{2,66},{66,2},{3,67},{67,3},{4,68},{68... | collective-permute-start | bytes 98312 | tf_op jit(solution)/shard_map/ppermute | solution.py:62
  15.9 3.2 %collective-permute-start = (bf16[1,1024,32]{1,2,0:T(8,128)(2,1)S(1)}, bf16[1,1024,32]{1,2,0:T(8,128)(2,1)S(1)}, u32[]{:S(2)}, u32[]{:S(2)}) collective-permute-start(bf16[1,1024,32]{1,2,0:T(8,128)(2,1)S(1)} %get-tuple-element.23), channel_id=1, source_target_pairs={{0,64},{64,0},{1,65},{65,1},{2,66},{66,2},{3,67},{67,3},{4,68},{68... | collective-permute-start | bytes 196616 | tf_op jit(solution)/shard_map/ppermute | solution.py:56
  20.6 27.3 %all-to-all-start.1 = ((bf16[64,2,512]{2,1,0:T(2,128)(2,1)}), bf16[64,2,512]{2,1,0:T(2,128)(2,1)S(1)}, u32[]{:S(2)}, u32[]{:S(2)}) async-start(bf16[64,2,512]{2,1,0:T(2,128)(2,1)} %reshape.89), calls=%async_computation.1 | async-start | bytes 262144 | tf_op jit(solution)/shard_map/all_to_all | solution.py:57
  47.9 10.5 %copy-start.1 = (bf16[1024,128]{1,0:T(8,128)(2,1)S(1)}, bf16[1024,128]{1,0:T(8,128)(2,1)}, u32[]{:S(2)}) copy-start(bf16[1024,128]{1,0:T(8,128)(2,1)} %param.15) | copy-start | bytes 786436
  47.9 63.6 %all-to-all-start = ((bf16[128,2,16,512]{3,2,1,0:T(8,128)(2,1)}), bf16[128,2,16,512]{3,2,1,0:T(8,128)(2,1)}, u32[]{:S(2)}, u32[]{:S(2)}) async-start(bf16[128,2,16,512]{3,2,1,0:T(8,128)(2,1)} %shard_map.113), calls=%async_computation | async-start | bytes 8388608 | tf_op jit(solution)/shard_map/all_to_all | solution.py:69
  117.5 37.0 %all-to-all-start.2 = ((bf16[128,16,512]{2,1,0:T(8,128)(2,1)}), bf16[128,16,512]{2,1,0:T(8,128)(2,1)S(1)}, u32[]{:S(2)}, u32[]{:S(2)}) async-start(bf16[128,16,512]{2,1,0:T(8,128)(2,1)} %bitcast.50), calls=%async_computation.2 | async-start | bytes 4194304 | tf_op jit(solution)/shard_map/all_to_all | solution.py:74
Sparse Core Ops, SparseCore 0:
  16.0 110.1 all-gather.1

commit v17 on v14

--- a/solution.py
+++ b/solution.py
@@ -125,16 +125,18 @@
 
 
 def product_kernel(moved_ref, out_ref):
-    halves, span, columns = out_ref.shape
+    _, span, columns = out_ref.shape
     n_src, _, tile_rows, _ = moved_ref.shape
-    per_half = n_src // halves
-    per_out = per_half // halves
-    for h in range(halves):
+    halves = pl.num_programs(0)
+    h = pl.program_id(0)
+    per_half = n_src // 2
+    per_out = per_half // 2
+    if True:
         total = None
-        for b in range(halves):
+        for b in range(2):
             left = moved_ref[b * per_half : (b + 1) * per_half, 0]
-            first = b * per_half + h * per_out
-            right = moved_ref[first : first + per_out, 1]
+            first = pl.multiple_of(b * per_half + h * per_out, per_out)
+            right = moved_ref[pl.ds(first, per_out), 1]
             part = lax.dot_general(
                 left.reshape(per_half * tile_rows, columns),
                 right.reshape(per_out * tile_rows, columns),
@@ -142,7 +144,7 @@
                 preferred_element_type=jnp.float32,
             )
             total = part if total is None else total + part
-        out_ref[h] = total.astype(out_ref.dtype)
+        out_ref[0] = total.astype(out_ref.dtype)
 
 
 def triangle_product(moved):
@@ -151,8 +153,11 @@
     product = pl.pallas_call(
         product_kernel,
         out_shape=jax.ShapeDtypeStruct((halves, n_src * tile_rows // halves, columns), jnp.bfloat16),
+        grid=(halves,),
         in_specs=[pl.BlockSpec(memory_space=pltpu.VMEM)],
-        out_specs=pl.BlockSpec(memory_space=pltpu.VMEM),
+        out_specs=pl.BlockSpec(
+            (1, n_src * tile_rows // halves, columns), lambda h: (h, 0, 0)
+        ),
         cost_estimate=pl.CostEstimate(
             flops=2 * (n_src * tile_rows) ** 2 * columns // halves,
             transcendentals=0,

time: 182 us -> 181 us (level)
  no operation moved by 1% of the time
where the time goes in v17:
time: 181 us
  waiting for transfers between devices  56.4 us (31%)
  Pallas kernels  55.3 us (31%)
  starting transfers between devices  34.5 us (19%)
  local copies, waits for them, and re-layouts  16.8 us (9%)
  between operations  14.2 us (8%)
  matrix products  2.65 us (1%)
    all_to_all x1, waiting for transfers between devices, send_whole(): lax.all_to_all(tri_stack, both, split_axis=0, concat_axis=0, tiled=True)  50.7 us
    pallas_call x1, Pallas kernels, outer_product(): pl.pallas_call(outer_kernel, out_shape=jax.ShapeDtypeStruct((tile_rows, c...  19.9 us
    pallas_call x1, Pallas kernels, pair_back(): pl.pallas_call(back_kernel, out_shape=jax.ShapeDtypeStruct((tile_rows, co...  17.1 us
    all_to_all x1, starting transfers between devices, gather_sides(): lax.all_to_all(left_pair, 'rows', split_axis=1, concat_axis=0, tiled=True)  14.1 us
    pallas_call x1, Pallas kernels, pair_front(): pl.pallas_call(front_kernel, out_shape=jax.ShapeDtypeStruct((chans, 2, ti...  12.4 us
    all_to_all x1, starting transfers between devices, send_whole(): lax.all_to_all(tri_stack, both, split_axis=0, concat_axis=0, tiled=True)  9.84 us
    all_to_all x1, starting transfers between devices, send_back(): lax.all_to_all(product, ('branch', 'rows'), split_axis=0, concat_axis=0,...  6.82 us
    all_gather x1, local copies, waits for them, and re-layouts, gather_sides(): lax.all_gather(jnp.swapaxes(right_pair, 0, 1), 'rows', axis=1, tiled=True)  6.5 us
  transfers between devices with their start and end apart: 6, of which 5 were waited for; matrix products, arithmetic and copies ran while one was open for 7% of the time, Pallas kernels for 21%

profile of v17, /device:TPU:1, one launch (start us, length us, event | category | flops | bytes accessed | tf_op | source)
XLA Modules:
  0.0 181.0 jit_solution(9189717592000296558)
XLA Ops:
  7.2 0.0 copy-start
  7.2 0.0 all-gather.2.cloned.1.call-start
  7.2 1.3 copy.33
  8.5 0.0 copy-start.3
  8.5 0.1 convert_reduce_fusion
  8.6 0.2 fusion.8
  8.8 0.0 copy-done
  8.8 0.0 copy-start.2
  8.8 2.4 %convert_reduce_fusion.1 = (f32[1024]{0:T(1024)S(1)}, bf16[1,1024,256]{1,2,0:T(8,128)(2,1)S(1)}) fusion(bf16[1024,256]{1,0:T(8,128)(2,1)S(1)} %copy-done, bf16[256,1024]{1,0:T(8,128)(2,1)} %param.12, bf16[1,1024,256]{1,2,0:T(8,128)(2,1)S(1)} %copy.33, f32[1024]{0:T(1024)S(1)} %add_rsqrt_fusion.1, f32[1024]{0:T(1024)S(1)} %broadcast_multiply_fusion.1), kind=kOutput, calls=%fused_computation.7 | convolution fusion | flops 1078197248 | bytes 2109440 | tf_op jit(solution)/shard_map/dot_general | solution.py:31
  11.2 0.2 fusion.10
  11.4 0.0 copy-done.3
  11.4 0.3 fusion.7
  11.7 2.2 %collective-permute-start.1 = (bf16[1,32,512]{2,1,0:T(8,128)(2,1)S(1)}, bf16[1,32,512]{2,1,0:T(8,128)(2,1)S(1)}, u32[]{:S(2)}, u32[]{:S(2)}) collective-permute-start(bf16[1,32,512]{2,1,0:T(8,128)(2,1)S(1)} %get-tuple-element.25), channel_id=1, source_target_pairs={{0,64},{64,0},{1,65},{65,1},{2,66},{66,2},{3,67},{67,3},{4,68},{68... | collective-permute-start | bytes 98312 | tf_op jit(solution)/shard_map/ppermute | solution.py:62
  13.9 1.3 collective-permute-done.1
  15.2 0.6 fusion.23
  15.9 0.0 all-gather.2.cloned.1.call-update
  15.9 1.5 collective-permute-start
  17.5 1.7 collective-permute-done
  19.1 0.4 copy.35
  19.5 1.1 reshape.89
  20.6 14.1 %all-to-all-start.1 = ((bf16[64,2,512]{2,1,0:T(2,128)(2,1)}), bf16[64,2,512]{2,1,0:T(2,128)(2,1)S(1)}, u32[]{:S(2)}, u32[]{:S(2)}) async-start(bf16[64,2,512]{2,1,0:T(2,128)(2,1)} %reshape.89), calls=%async_computation.1 | async-start | bytes 262144 | tf_op jit(solution)/shard_map/all_to_all | solution.py:57
  34.7 0.0 copy-done.2
  34.7 0.8 copy.34
  35.5 12.4 %shard_map.113 = bf16[128,2,16,512]{3,2,1,0:T(8,128)(2,1)} custom-call(bf16[16,512,128]{2,1,0:T(8,128)(2,1)} %pair_ref.1, bf16[4,128,128]{2,1,0:T(8,128)(2,1)} %bitcast.54), custom_call_target="tpu_custom_call" | custom-call | flops 1073741824 | bytes 6291456 | tf_op jit(solution)/shard_map/pallas_call | solution.py:109
  47.9 0.0 copy-start.1
  47.9 0.0 all-to-all-done.1
  47.9 9.8 %all-to-all-start = ((bf16[128,2,16,512]{3,2,1,0:T(8,128)(2,1)}), bf16[128,2,16,512]{3,2,1,0:T(8,128)(2,1)}, u32[]{:S(2)}, u32[]{:S(2)}) async-start(bf16[128,2,16,512]{3,2,1,0:T(8,128)(2,1)} %shard_map.113), calls=%async_computation | async-start | bytes 8388608 | tf_op jit(solution)/shard_map/all_to_all | solution.py:69
  57.8 0.6 slice.16.wg_ref
  58.4 0.0 copy-done.1
  58.4 0.1 copy.39
  58.5 0.9 copy.40
  59.4 0.3 reshape.90
  59.7 0.1 copy.36
  59.8 1.1 copy.38
  60.9 50.7 %all-to-all-done.moved_ref = bf16[128,2,16,512]{3,2,1,0:T(8,128)(2,1)} async-done(((bf16[128,2,16,512]{3,2,1,0:T(8,128)(2,1)}), bf16[128,2,16,512]{3,2,1,0:T(8,128)(2,1)}, u32[]{:S(2)}, u32[]{:S(2)}) %all-to-all-start) | async-done | bytes 4194336 | tf_op jit(solution)/shard_map/all_to_all | solution.py:69
  111.5 5.8 %shard_map.114 = bf16[2,1024,512]{2,1,0:T(8,128)(2,1)} custom-call(bf16[128,2,16,512]{3,2,1,0:T(8,128)(2,1)} %all-to-all-done.moved_ref), custom_call_target="tpu_custom_call" | custom-call | flops 2147483648 | bytes 6291456 | tf_op jit(solution)/shard_map/pallas_call | solution.py:153
  117.3 6.8 %all-to-all-start.2 = ((bf16[128,16,512]{2,1,0:T(8,128)(2,1)}), bf16[128,16,512]{2,1,0:T(8,128)(2,1)S(1)}, u32[]{:S(2)}, u32[]{:S(2)}) async-start(bf16[128,16,512]{2,1,0:T(8,128)(2,1)} %bitcast.50), calls=%async_computation.2 | async-start | bytes 4194304 | tf_op jit(solution)/shard_map/all_to_all | solution.py:74
  124.2 1.0 copy.42
  125.2 1.1 all-gather.2.cloned.1.call-done
  126.2 6.5 %copy.41.r_ref = bf16[32,128,512]{2,1,0:T(8,128)(2,1)} copy(bf16[32,128,512]{2,0,1:T(8,128)(2,1)} %all-gather.2.cloned.1.call-done) | data formatting | bytes 8388608 | tf_op jit(solution)/shard_map/all_gather | solution.py:63
  132.7 19.9 %shard_map.115.outer_ref = f32[16,512,128]{2,1,0:T(8,128)} custom-call(bf16[512,128]{1,0:T(8,128)(2,1)} %bitcast.57, bf16[32,128,512]{2,1,0:T(8,128)(2,1)} %copy.41.r_ref, bf16[128,1024]{1,0:T(8,128)(2,1)} %bitcast.56), custom_call_target="tpu_custom_call" | custom-call | flops 4294967296 | bytes 8388608 | tf_op jit(solution)/shard_map/pallas_call | solution.py:275
  152.6 1.7 all-to-all-done.2
  154.3 2.7 %copy.43 = bf16[16,8,16,512]{3,1,2,0:T(8,128)(2,1)} copy(bf16[16,8,16,512]{3,2,1,0:T(8,128)(2,1)S(1)} %bitcast.46) | data formatting | bytes 4194304
  157.0 17.1 %shard_map.116 = bf16[16,512,128]{2,1,0:T(8,128)(2,1)} custom-call(bf16[128,8192]{1,0:T(8,128)(2,1)} %bitcast.51, bf16[16,512,128]{2,1,0:T(8,128)(2,1)} %pair_ref.1, f32[16,512,128]{2,1,0:T(8,128)} %shard_map.115.outer_ref, bf16[128,128]{1,0:T(8,128)(2,1)} %wo_ref.1, bf16[128,128]{1,0:T(8,128)(2,1)} %slice.16.wg_ref, bf16[128,512]{1,0:T(8,128)(2,1)} %wu_ref.1, ...), custom_call_target="tpu_custom_call" | custom-call | flops 2952790016 | bytes 10485760 | tf_op jit(solution)/shard_map/pallas_call | solution.py:206
  (9 shorter events, 0.1 us)
Async XLA Ops:
  7.2 1.7 copy-start
  7.2 119.0 %all-gather.2.cloned.1.call-start = ((), (), s32[]{:S(2)}) async-start(), calls=%async_computation.3 | async-start | bytes 4259840 | tf_op jit(solution)/shard_map/all_gather | solution.py:63
  8.5 2.9 %copy-start.3 = (bf16[256,64]{0,1:T(8,128)(2,1)S(1)}, bf16[256,64]{0,1:T(8,128)(2,1)}, u32[]{:S(2)}) copy-start(bf16[256,64]{0,1:T(8,128)(2,1)} %param.14) | copy-start | bytes 98308
  8.8 25.9 %copy-start.2 = (bf16[128,640]{1,0:T(8,128)(2,1)S(1)}, bf16[128,640]{1,0:T(8,128)(2,1)}, u32[]{:S(2)}) copy-start(bf16[128,640]{1,0:T(8,128)(2,1)} %param.16) | copy-start | bytes 491524
  11.7 3.5 %collective-permute-start.1 = (bf16[1,32,512]{2,1,0:T(8,128)(2,1)S(1)}, bf16[1,32,512]{2,1,0:T(8,128)(2,1)S(1)}, u32[]{:S(2)}, u32[]{:S(2)}) collective-permute-start(bf16[1,32,512]{2,1,0:T(8,128)(2,1)S(1)} %get-tuple-element.25), channel_id=1, source_target_pairs={{0,64},{64,0},{1,65},{65,1},{2,66},{66,2},{3,67},{67,3},{4,68},{68... | collective-permute-start | bytes 98312 | tf_op jit(solution)/shard_map/ppermute | solution.py:62
  15.9 3.2 %collective-permute-start = (bf16[1,1024,32]{1,2,0:T(8,128)(2,1)S(1)}, bf16[1,1024,32]{1,2,0:T(8,128)(2,1)S(1)}, u32[]{:S(2)}, u32[]{:S(2)}) collective-permute-start(bf16[1,1024,32]{1,2,0:T(8,128)(2,1)S(1)} %get-tuple-element.23), channel_id=1, source_target_pairs={{0,64},{64,0},{1,65},{65,1},{2,66},{66,2},{3,67},{67,3},{4,68},{68... | collective-permute-start | bytes 196616 | tf_op jit(solution)/shard_map/ppermute | solution.py:56
  20.6 27.3 %all-to-all-start.1 = ((bf16[64,2,512]{2,1,0:T(2,128)(2,1)}), bf16[64,2,512]{2,1,0:T(2,128)(2,1)S(1)}, u32[]{:S(2)}, u32[]{:S(2)}) async-start(bf16[64,2,512]{2,1,0:T(2,128)(2,1)} %reshape.89), calls=%async_computation.1 | async-start | bytes 262144 | tf_op jit(solution)/shard_map/all_to_all | solution.py:57
  47.9 10.5 %copy-start.1 = (bf16[1024,128]{1,0:T(8,128)(2,1)S(1)}, bf16[1024,128]{1,0:T(8,128)(2,1)}, u32[]{:S(2)}) copy-start(bf16[1024,128]{1,0:T(8,128)(2,1)} %param.15) | copy-start | bytes 786436
  47.9 63.6 %all-to-all-start = ((bf16[128,2,16,512]{3,2,1,0:T(8,128)(2,1)}), bf16[128,2,16,512]{3,2,1,0:T(8,128)(2,1)}, u32[]{:S(2)}, u32[]{:S(2)}) async-start(bf16[128,2,16,512]{3,2,1,0:T(8,128)(2,1)} %shard_map.113), calls=%async_computation | async-start | bytes 8388608 | tf_op jit(solution)/shard_map/all_to_all | solution.py:69
  117.3 37.0 %all-to-all-start.2 = ((bf16[128,16,512]{2,1,0:T(8,128)(2,1)}), bf16[128,16,512]{2,1,0:T(8,128)(2,1)S(1)}, u32[]{:S(2)}, u32[]{:S(2)}) async-start(bf16[128,16,512]{2,1,0:T(8,128)(2,1)} %bitcast.50), calls=%async_computation.2 | async-start | bytes 4194304 | tf_op jit(solution)/shard_map/all_to_all | solution.py:74
Sparse Core Ops, SparseCore 0:
  16.0 110.1 all-gather.1
